TPU v7x, 128 devices: a whole 4x4x4 slice. The times are simulated.
128 devices in a mesh: gx: 4 (over x), gy: 32 (over z, y, core).
Axes of the slice: x: 4, y: 4, z: 4, core: 2. Of those that a mesh axis runs over, the one named last changes fastest.
Arguments:
- densities: bfloat16 [16, 524288], P(None, ('gx', 'gy')), may hold values from -6 to 6
- points: float32 [3, 524288], P(None, ('gx', 'gy')), may hold values from 0 to 1
- weights: float32 [524288], P(('gx', 'gy')), may hold values from 0.03 to 0.6
- near_offsets: int32 [4096, 13], P(('gx', 'gy')), may hold values from -8 to 8, as said below
- leaf_basis: bfloat16 [4096, 64, 128], P(('gx', 'gy')), may hold values from -0.5 to 0.5
- transfer: bfloat16 [4096, 64, 64], P(('gx', 'gy')), may hold values from -0.75 to 0.75
- send_lists: int32 [128, 17, 16], P(('gx', 'gy')), may hold values from 0 to 31
- relay_refs: int32 [4096, 32], P(('gx', 'gy')), may hold values from 0 to 271, as said below
- leaf_coupling: bfloat16 [4096, 32, 64, 64], P(('gx', 'gy')), may hold values from -0.25 to 0.25
- coarse_refs: int32 [512, 32], P(('gx', 'gy')), may hold values from 0 to 511
- coarse_coupling: bfloat16 [512, 32, 64, 64], P(('gx', 'gy')), may hold values from -0.125 to 0.125
Outputs:
- potential: float32 [16, 524288], P(None, ('gx', 'gy'))
Inputs may be any that keep to these rules, and one draw needn't show every extreme that they name: `near_offsets`: each leaf's offsets are distinct and the first is 0; a partner outside the leaves contributes nothing. `relay_refs`: a value never names an owner l // 32 + value // 16 - 8 outside 0 to 127; within the rows of each device's 32 leaves every other value is used at least once.
All inputs are finite; a program needn't handle non-finite values.
Results may differ from a plain program's by a relative error of at most 0.0065.
Values may be sent and summed in bfloat16 or wider, within the bound.
No kernel may reach another device: no remote copies, remote signals or barrier semaphores. Data moves between devices by JAX's collectives and lax.ppermute only.
A program may use at most 128 MiB of HBM per device.

v0:
```python
import math

import jax
import jax.numpy as jnp
from jax import lax
from jax.sharding import PartitionSpec as P

REACH = 8
WINDOW = 8


core_square = 0.0004
four_pi = 4.0 * math.pi


def from_behind(shard, axis, by):
    devices = lax.axis_size(axis)
    pairs = [(i, i + by) for i in range(devices) if 0 <= i + by < devices]
    return lax.ppermute(shard, axis, pairs)


def near_field(densities, points, weights, near_offsets):
    rhs_count = densities.shape[0]
    leaf_count = near_offsets.shape[0]
    leaf_size = densities.shape[1] // leaf_count
    packed = jnp.concatenate([densities.astype(jnp.float32), points, weights[None, :]], axis=0)
    rim_cells = REACH * leaf_size
    from_below = from_behind(packed[:, -rim_cells:].astype(jnp.bfloat16), ("gx", "gy"), 1).astype(
        jnp.float32
    )
    from_above = from_behind(packed[:, :rim_cells], ("gx", "gy"), -1)
    extended = jnp.concatenate([from_below, packed, from_above], axis=1).reshape(
        rhs_count + 4, leaf_count + 2 * REACH, leaf_size
    )
    row_points = points.reshape(3, leaf_count, leaf_size)
    partners = jnp.arange(leaf_count, dtype=jnp.int32)[:, None] + REACH + near_offsets

    def near_block(block_index):
        partner_rows = lax.dynamic_slice_in_dim(partners, block_index * 8, 8, 0)
        partner_data = jnp.take(extended, partner_rows, axis=1)
        own_points = lax.dynamic_slice_in_dim(row_points, block_index * 8, 8, 1)
        distance = jnp.zeros((8, leaf_size, partner_rows.shape[1], leaf_size), jnp.float32)
        for component in range(3):
            offset_part = (
                own_points[component][:, :, None, None]
                - partner_data[rhs_count + component][:, None, :, :]
            )
            distance = distance + offset_part * offset_part
        kernel = (
            partner_data[rhs_count + 3][:, None, :, :]
            / (four_pi * jnp.sqrt(distance + core_square))
        ).astype(jnp.bfloat16)
        partner_values = partner_data[:rhs_count].astype(jnp.bfloat16)
        return jnp.einsum(
            "lisj,rlsj->rli", kernel, partner_values, preferred_element_type=jnp.float32
        )

    blocks_out = lax.map(near_block, jnp.arange(leaf_count // 8, dtype=jnp.int32))
    return jnp.transpose(blocks_out, (1, 0, 2, 3)).reshape(rhs_count, leaf_count * leaf_size)


def local(
    densities,
    points,
    weights,
    near_offsets,
    leaf_basis,
    transfer,
    send_lists,
    relay_refs,
    leaf_coupling,
    coarse_refs,
    coarse_coupling,
):
    near_part = near_field(densities, points, weights, near_offsets)
    rhs_count = densities.shape[0]
    leaf_count, basis_rank, leaf_size = leaf_basis.shape
    values = densities.reshape(rhs_count, leaf_count, leaf_size)
    coeff0 = jnp.einsum(
        "lkm,rlm->lrk", leaf_basis, values, preferred_element_type=jnp.float32
    ).astype(jnp.bfloat16)
    capacity = send_lists.shape[2]
    outgoing = jnp.take(coeff0, send_lists[0], axis=0)
    pieces = []
    for window_index in range(2 * WINDOW + 1):
        offset = window_index - WINDOW
        if offset == 0:
            pieces.append(outgoing[WINDOW])
        else:
            pieces.append(from_behind(outgoing[2 * WINDOW - window_index], ("gx", "gy"), -offset))
    received = jnp.stack(pieces, axis=0)
    received = received.reshape((2 * WINDOW + 1) * capacity, rhs_count, basis_rank)
    picked = jnp.take(received, relay_refs, axis=0)
    local0 = jnp.einsum("lsab,lsrb->lra", leaf_coupling, picked, preferred_element_type=jnp.float32)
    groups = leaf_count // 8
    transfer_groups = transfer.reshape(groups, 8, basis_rank, basis_rank)
    coeff1 = jnp.einsum(
        "qcab,qcra->qrb",
        transfer_groups,
        coeff0.reshape(groups, 8, rhs_count, basis_rank),
        preferred_element_type=jnp.float32,
    ).astype(jnp.bfloat16)
    everyone = lax.all_gather(coeff1, ("gx", "gy"), axis=0, tiled=True)
    coarse_picked = jnp.take(everyone, coarse_refs, axis=0)
    local1 = jnp.einsum(
        "qsab,qsrb->qra", coarse_coupling, coarse_picked, preferred_element_type=jnp.float32
    ).astype(jnp.bfloat16)
    downward = jnp.einsum(
        "qcab,qrb->qcra", transfer_groups, local1, preferred_element_type=jnp.float32
    ).reshape(leaf_count, rhs_count, basis_rank)
    leaf_field = (local0 + downward).astype(jnp.bfloat16)
    far_field = jnp.einsum(
        "lkm,lrk->rlm", leaf_basis, leaf_field, preferred_element_type=jnp.float32
    ).reshape(rhs_count, leaf_count * leaf_size)
    return far_field + near_part


def solution(mesh):
    in_specs = (
        P(None, ("gx", "gy")),
        P(None, ("gx", "gy")),
        P(("gx", "gy")),
        P(("gx", "gy"), None),
        P(("gx", "gy"), None, None),
        P(("gx", "gy"), None, None),
        P(("gx", "gy"), None, None),
        P(("gx", "gy"), None),
        P(("gx", "gy"), None, None, None),
        P(("gx", "gy"), None),
        P(("gx", "gy"), None, None, None),
    )
    out_specs = P(None, ("gx", "gy"))
    return jax.shard_map(local, mesh=mesh, in_specs=in_specs, out_specs=out_specs, check_vma=False)
```

profile of v0, /device:TPU:98, one launch (start us, length us, event | category | flops | bytes accessed | tf_op | source)
XLA Modules:
  0.0 185.1 jit_solution(14313337086683560467)
XLA Ops:
  9.1 4.3 %collective-permute-start.17 = (f32[20,1024]{1,0:T(8,128)}, f32[20,1024]{1,0:T(8,128)}, u32[]{:S(2)}, u32[]{:S(2)}) collective-permute-start(f32[20,1024]{1,0:T(8,128)} %pad_maximum_fusion.2), channel_id=1, source_target_pairs={{1,0},{2,1},{3,2},{4,3},{5,4},{6,5},{7,6},{8,7},{9,8},{10,9},{11,1... | collective-permute-start | bytes 245768 | tf_op jit(solution)/shard_map/ppermute | solution.py:19
  15.0 1.9 %collective-permute-start.16 = (bf16[20,1024]{1,0:T(8,128)(2,1)}, bf16[20,1024]{1,0:T(8,128)(2,1)}, u32[]{:S(2)}, u32[]{:S(2)}) collective-permute-start(bf16[20,1024]{1,0:T(8,128)(2,1)} %slice.154), channel_id=1, source_target_pairs={{0,1},{1,2},{2,3},{3,4},{4,5},{5,6},{6,7},{7,8},{8,9},{9,10},{10,1... | collective-permute-start | bytes 122888 | tf_op jit(solution)/shard_map/ppermute | solution.py:19
  18.4 2.0 %gather_fusion.1 = bf16[272,16,64]{2,1,0:T(8,128)(2,1)S(1)} fusion(bf16[32,16,64]{2,1,0:T(8,128)(2,1)S(1)} %convolution_convert_fusion, s32[1024]{0:T(1024)S(1)} %pad_clamp_fusion.2), kind=kCustom, calls=%fused_computation.1 | custom fusion | bytes 1115200 | tf_op jit(solution)/shard_map/jit(_take)/gather | solution.py:83
  22.7 5.6 %collective-permute-start = (bf16[16,16,64]{2,1,0:T(8,128)(2,1)S(1)}, bf16[16,16,64]{2,1,0:T(8,128)(2,1)S(1)}, u32[]{:S(2)}, u32[]{:S(2)}) collective-permute-start(bf16[16,16,64]{2,1,0:T(8,128)(2,1)S(1)} %get-tuple-element.91), channel_id=1, source_target_pairs={{0,8},{1,9},{2,10},{3,11},{4,12},{5,13},{6,14},{7,15},{8,16},{9,17... | collective-permute-start | bytes 98312 | tf_op jit(solution)/shard_map/ppermute | solution.py:19
  28.3 4.3 %collective-permute-start.1 = (bf16[16,16,64]{2,1,0:T(8,128)(2,1)}, bf16[16,16,64]{2,1,0:T(8,128)(2,1)}, u32[]{:S(2)}, u32[]{:S(2)}) collective-permute-start(bf16[16,16,64]{2,1,0:T(8,128)(2,1)} %get-tuple-element.90), channel_id=1, source_target_pairs={{0,7},{1,8},{2,9},{3,10},{4,11},{5,12},{6,13},{7,14},{8,15},{9,16}... | collective-permute-start | bytes 98312 | tf_op jit(solution)/shard_map/ppermute | solution.py:19
  32.6 1.9 %collective-permute-start.2 = (bf16[16,16,64]{2,1,0:T(8,128)(2,1)}, bf16[16,16,64]{2,1,0:T(8,128)(2,1)}, u32[]{:S(2)}, u32[]{:S(2)}) collective-permute-start(bf16[16,16,64]{2,1,0:T(8,128)(2,1)} %get-tuple-element.89), channel_id=1, source_target_pairs={{0,6},{1,7},{2,8},{3,9},{4,10},{5,11},{6,12},{7,13},{8,14},{9,15},... | collective-permute-start | bytes 98312 | tf_op jit(solution)/shard_map/ppermute | solution.py:19
  37.8 2.0 %collective-permute-start.3 = (bf16[16,16,64]{2,1,0:T(8,128)(2,1)}, bf16[16,16,64]{2,1,0:T(8,128)(2,1)S(1)}, u32[]{:S(2)}, u32[]{:S(2)}) collective-permute-start(bf16[16,16,64]{2,1,0:T(8,128)(2,1)} %get-tuple-element.88), channel_id=1, source_target_pairs={{0,5},{1,6},{2,7},{3,8},{4,9},{5,10},{6,11},{7,12},{8,13},{9,14},{... | collective-permute-start | bytes 98312 | tf_op jit(solution)/shard_map/ppermute | solution.py:19
  40.7 4.2 %collective-permute-start.4 = (bf16[16,16,64]{2,1,0:T(8,128)(2,1)S(1)}, bf16[16,16,64]{2,1,0:T(8,128)(2,1)S(1)}, u32[]{:S(2)}, u32[]{:S(2)}) collective-permute-start(bf16[16,16,64]{2,1,0:T(8,128)(2,1)S(1)} %get-tuple-element.87), channel_id=1, source_target_pairs={{0,4},{1,5},{2,6},{3,7},{4,8},{5,9},{6,10},{7,11},{8,12},{9,13},{1... | collective-permute-start | bytes 98312 | tf_op jit(solution)/shard_map/ppermute | solution.py:19
  45.8 1.9 %collective-permute-start.5 = (bf16[16,16,64]{2,1,0:T(8,128)(2,1)S(1)}, bf16[16,16,64]{2,1,0:T(8,128)(2,1)S(1)}, u32[]{:S(2)}, u32[]{:S(2)}) collective-permute-start(bf16[16,16,64]{2,1,0:T(8,128)(2,1)S(1)} %get-tuple-element.86), channel_id=1, source_target_pairs={{0,3},{1,4},{2,5},{3,6},{4,7},{5,8},{6,9},{7,10},{8,11},{9,12},{10... | collective-permute-start | bytes 98312 | tf_op jit(solution)/shard_map/ppermute | solution.py:19
  48.6 3.8 %collective-permute-start.6 = (bf16[16,16,64]{2,1,0:T(8,128)(2,1)S(1)}, bf16[16,16,64]{2,1,0:T(8,128)(2,1)S(1)}, u32[]{:S(2)}, u32[]{:S(2)}) collective-permute-start(bf16[16,16,64]{2,1,0:T(8,128)(2,1)S(1)} %get-tuple-element.85), channel_id=1, source_target_pairs={{0,2},{1,3},{2,4},{3,5},{4,6},{5,7},{6,8},{7,9},{8,10},{9,11},{10,... | collective-permute-start | bytes 98312 | tf_op jit(solution)/shard_map/ppermute | solution.py:19
  52.4 3.5 %collective-permute-start.7 = (bf16[16,16,64]{2,1,0:T(8,128)(2,1)S(1)}, bf16[16,16,64]{2,1,0:T(8,128)(2,1)S(1)}, u32[]{:S(2)}, u32[]{:S(2)}) collective-permute-start(bf16[16,16,64]{2,1,0:T(8,128)(2,1)S(1)} %get-tuple-element.84), channel_id=1, source_target_pairs={{0,1},{1,2},{2,3},{3,4},{4,5},{5,6},{6,7},{7,8},{8,9},{9,10},{10,1... | collective-permute-start | bytes 98312 | tf_op jit(solution)/shard_map/ppermute | solution.py:19
  56.0 2.7 %collective-permute-done.6 = bf16[16,16,64]{2,1,0:T(8,128)(2,1)S(1)} collective-permute-done((bf16[16,16,64]{2,1,0:T(8,128)(2,1)S(1)}, bf16[16,16,64]{2,1,0:T(8,128)(2,1)S(1)}, u32[]{:S(2)}, u32[]{:S(2)}) %collective-permute-start.6) | collective-permute-done | bytes 32800 | tf_op jit(solution)/shard_map/ppermute | solution.py:19
  60.3 1.8 slice_bitcast_fusion
  62.1 1.9 %collective-permute-start.8 = (bf16[16,16,64]{2,1,0:T(8,128)(2,1)}, bf16[16,16,64]{2,1,0:T(8,128)(2,1)}, u32[]{:S(2)}, u32[]{:S(2)}) collective-permute-start(bf16[16,16,64]{2,1,0:T(8,128)(2,1)} %get-tuple-element.82), channel_id=1, source_target_pairs={{1,0},{2,1},{3,2},{4,3},{5,4},{6,5},{7,6},{8,7},{9,8},{10,9},{11,1... | collective-permute-start | bytes 98312 | tf_op jit(solution)/shard_map/ppermute | solution.py:19
  65.2 3.5 %collective-permute-start.9 = (bf16[16,16,64]{2,1,0:T(8,128)(2,1)}, bf16[16,16,64]{2,1,0:T(8,128)(2,1)S(1)}, u32[]{:S(2)}, u32[]{:S(2)}) collective-permute-start(bf16[16,16,64]{2,1,0:T(8,128)(2,1)} %get-tuple-element.81), channel_id=1, source_target_pairs={{2,0},{3,1},{4,2},{5,3},{6,4},{7,5},{8,6},{9,7},{10,8},{11,9},{12,... | collective-permute-start | bytes 98312 | tf_op jit(solution)/shard_map/ppermute | solution.py:19
  68.8 3.6 %collective-permute-start.10 = (bf16[16,16,64]{2,1,0:T(8,128)(2,1)}, bf16[16,16,64]{2,1,0:T(8,128)(2,1)S(1)}, u32[]{:S(2)}, u32[]{:S(2)}) collective-permute-start(bf16[16,16,64]{2,1,0:T(8,128)(2,1)} %get-tuple-element.80), channel_id=1, source_target_pairs={{3,0},{4,1},{5,2},{6,3},{7,4},{8,5},{9,6},{10,7},{11,8},{12,9},{13... | collective-permute-start | bytes 98312 | tf_op jit(solution)/shard_map/ppermute | solution.py:19
  72.4 3.9 %collective-permute-start.11 = (bf16[16,16,64]{2,1,0:T(8,128)(2,1)}, bf16[16,16,64]{2,1,0:T(8,128)(2,1)S(1)}, u32[]{:S(2)}, u32[]{:S(2)}) collective-permute-start(bf16[16,16,64]{2,1,0:T(8,128)(2,1)} %get-tuple-element.79), channel_id=1, source_target_pairs={{4,0},{5,1},{6,2},{7,3},{8,4},{9,5},{10,6},{11,7},{12,8},{13,9},{1... | collective-permute-start | bytes 98312 | tf_op jit(solution)/shard_map/ppermute | solution.py:19
  77.7 1.9 %collective-permute-start.12 = (bf16[16,16,64]{2,1,0:T(8,128)(2,1)S(1)}, bf16[16,16,64]{2,1,0:T(8,128)(2,1)S(1)}, u32[]{:S(2)}, u32[]{:S(2)}) collective-permute-start(bf16[16,16,64]{2,1,0:T(8,128)(2,1)S(1)} %get-tuple-element.78), channel_id=1, source_target_pairs={{5,0},{6,1},{7,2},{8,3},{9,4},{10,5},{11,6},{12,7},{13,8},{14,9},{... | collective-permute-start | bytes 98312 | tf_op jit(solution)/shard_map/ppermute | solution.py:19
  80.4 4.6 %collective-permute-start.13 = (bf16[16,16,64]{2,1,0:T(8,128)(2,1)S(1)}, bf16[16,16,64]{2,1,0:T(8,128)(2,1)S(1)}, u32[]{:S(2)}, u32[]{:S(2)}) collective-permute-start(bf16[16,16,64]{2,1,0:T(8,128)(2,1)S(1)} %get-tuple-element.77), channel_id=1, source_target_pairs={{6,0},{7,1},{8,2},{9,3},{10,4},{11,5},{12,6},{13,7},{14,8},{15,9},... | collective-permute-start | bytes 98312 | tf_op jit(solution)/shard_map/ppermute | solution.py:19
  85.1 6.5 %collective-permute-start.14 = (bf16[16,16,64]{2,1,0:T(8,128)(2,1)S(1)}, bf16[16,16,64]{2,1,0:T(8,128)(2,1)S(1)}, u32[]{:S(2)}, u32[]{:S(2)}) collective-permute-start(bf16[16,16,64]{2,1,0:T(8,128)(2,1)S(1)} %get-tuple-element.76), channel_id=1, source_target_pairs={{7,0},{8,1},{9,2},{10,3},{11,4},{12,5},{13,6},{14,7},{15,8},{16,9}... | collective-permute-start | bytes 98312 | tf_op jit(solution)/shard_map/ppermute | solution.py:19
  91.7 1.9 %collective-permute-start.15 = (bf16[16,16,64]{2,1,0:T(8,128)(2,1)S(1)}, bf16[16,16,64]{2,1,0:T(8,128)(2,1)S(1)}, u32[]{:S(2)}, u32[]{:S(2)}) collective-permute-start(bf16[16,16,64]{2,1,0:T(8,128)(2,1)S(1)} %get-tuple-element.75), channel_id=1, source_target_pairs={{8,0},{9,1},{10,2},{11,3},{12,4},{13,5},{14,6},{15,7},{16,8},{17,9... | collective-permute-start | bytes 98312 | tf_op jit(solution)/shard_map/ppermute | solution.py:19
  93.7 6.2 %collective-permute-done.15 = bf16[16,16,64]{2,1,0:T(8,128)(2,1)S(1)} collective-permute-done((bf16[16,16,64]{2,1,0:T(8,128)(2,1)S(1)}, bf16[16,16,64]{2,1,0:T(8,128)(2,1)S(1)}, u32[]{:S(2)}, u32[]{:S(2)}) %collective-permute-start.15) | collective-permute-done | bytes 32800 | tf_op jit(solution)/shard_map/ppermute | solution.py:19
  100.0 8.6 %gather_fusion.2 = bf16[1024,16,64]{2,1,0:T(8,128)(2,1)} fusion(bf16[272,16,64]{2,1,0:T(8,128)(2,1)S(1)} %bitcast.188, s32[1024]{0:T(1024)} %broadcast_clamp_fusion), kind=kCustom, calls=%fused_computation.2 | custom fusion | bytes 4198400 | tf_op jit(solution)/shard_map/jit(_take)/gather | solution.py:93
  110.8 51.6 %while.10 = (s32[]{:T(128)}, f32[4,16,8,128]{3,1,2,0:T(8,128)}, s32[4]{0:T(128)S(1)}, s32[32,13]{1,0:T(8,128)}, f32[20,48,128]{2,0,1:T(8,128)}, /*index=5*/f32[3...) while((s32[]{:T(128)}, f32[4,16,8,128]{3,1,2,0:T(8,128)}, ...), condition=%wide.region_1.2_spmd, body=%wide.region_0.1_spmd.sunk | while | flops 75241080 | bytes 10120079 | solution.py:58
  112.9 1.7 gather_fusion
  116.7 7.0 %fusion.48 = f32[4,16,8,128]{3,1,2,0:T(8,128)} fusion(f32[4,16,8,128]{3,1,2,0:T(8,128)} %get-tuple-element.168, s32[]{:T(128)S(6)} %copy.94, f32[8,13,128]{2,1,0:T(8,128)S(1)} %get-tuple-element.146, f32[8,128]{1,0:T(8,128)S(1)} %get-tuple-element.147, f32[8,13,128]{2,1,0:T(8,128)S(1)} %get-tuple-element.148, f32[8,128]{1,0:T(8,128)S(1)} %get-tuple-element.149, ...), kind=kOutput, calls=%fused_computation.8.clone.1 | convolution fusion | flops 74973184 | bytes 716804 | tf_op jit(solution)/shard_map/while/body/eval_jaxpr/lisj,rlsj->rli/dot_general | solution.py:54
  129.6 7.0 %fusion.48 = f32[4,16,8,128]{3,1,2,0:T(8,128)} fusion(f32[4,16,8,128]{3,1,2,0:T(8,128)} %get-tuple-element.168, s32[]{:T(128)S(6)} %copy.94, f32[8,13,128]{2,1,0:T(8,128)S(1)} %get-tuple-element.146, f32[8,128]{1,0:T(8,128)S(1)} %get-tuple-element.147, f32[8,13,128]{2,1,0:T(8,128)S(1)} %get-tuple-element.148, f32[8,128]{1,0:T(8,128)S(1)} %get-tuple-element.149, ...), kind=kOutput, calls=%fused_computation.8.clone.1 | convolution fusion | flops 74973184 | bytes 716804 | tf_op jit(solution)/shard_map/while/body/eval_jaxpr/lisj,rlsj->rli/dot_general | solution.py:54
  142.5 7.0 %fusion.48 = f32[4,16,8,128]{3,1,2,0:T(8,128)} fusion(f32[4,16,8,128]{3,1,2,0:T(8,128)} %get-tuple-element.168, s32[]{:T(128)S(6)} %copy.94, f32[8,13,128]{2,1,0:T(8,128)S(1)} %get-tuple-element.146, f32[8,128]{1,0:T(8,128)S(1)} %get-tuple-element.147, f32[8,13,128]{2,1,0:T(8,128)S(1)} %get-tuple-element.148, f32[8,128]{1,0:T(8,128)S(1)} %get-tuple-element.149, ...), kind=kOutput, calls=%fused_computation.8.clone.1 | convolution fusion | flops 74973184 | bytes 716804 | tf_op jit(solution)/shard_map/while/body/eval_jaxpr/lisj,rlsj->rli/dot_general | solution.py:54
  155.4 7.0 %fusion.48 = f32[4,16,8,128]{3,1,2,0:T(8,128)} fusion(f32[4,16,8,128]{3,1,2,0:T(8,128)} %get-tuple-element.168, s32[]{:T(128)S(6)} %copy.94, f32[8,13,128]{2,1,0:T(8,128)S(1)} %get-tuple-element.146, f32[8,128]{1,0:T(8,128)S(1)} %get-tuple-element.147, f32[8,13,128]{2,1,0:T(8,128)S(1)} %get-tuple-element.148, f32[8,128]{1,0:T(8,128)S(1)} %get-tuple-element.149, ...), kind=kOutput, calls=%fused_computation.8.clone.1 | convolution fusion | flops 74973184 | bytes 716804 | tf_op jit(solution)/shard_map/while/body/eval_jaxpr/lisj,rlsj->rli/dot_general | solution.py:54
  163.6 2.3 %gather_fusion.3 = bf16[128,16,64]{2,1,0:T(8,128)(2,1)S(1)} fusion(bf16[512,16,64]{2,1,0:T(8,128)(2,1)} %all-gather.2.cloned.1.call-done, s32[1024]{0:T(1024)S(1)} %copy-done.14), kind=kCustom, calls=%fused_computation.3 | custom fusion | bytes 524800 | tf_op jit(solution)/shard_map/jit(_take)/gather | solution.py:104
  165.9 1.8 fusion.21
  167.7 9.7 %convolution_bitcast_fusion = f32[32,2,8,128]{3,2,1,0:T(8,128)S(1)} fusion(bf16[32,64,128]{2,1,0:T(8,128)(2,1)} %param.17, f32[32,16,64]{2,1,0:T(8,128)} %bitcast.199, bf16[32,32,64,64]{3,2,1,0:T(8,128)(2,1)} %param.21, bf16[32,32,16,64]{3,2,1,0:T(8,128)(2,1)} %bitcast.191, pred[32,32]{1,0:T(8,128)(4,1)S(1)} %copy-done.17), kind=kOutput, calls=%fused_computation.26 | convolution fusion | flops 143720448 | bytes 11404288 | tf_op jit(solution)/shard_map/lkm,lrk->rlm/dot_general | solution.py:112
  (153 shorter events, 42.1 us)
Async XLA Ops:
  6.5 159.3 %copy-start = (bf16[4,32,64,64]{3,2,1,0:T(8,128)(2,1)S(1)}, bf16[4,32,64,64]{3,2,1,0:T(8,128)(2,1)}, u32[]{:S(2)}) copy-start(bf16[4,32,64,64]{3,2,1,0:T(8,128)(2,1)} %param.23) | copy-start | bytes 3145732
  6.5 10.4 %copy-start.9 = (bf16[16,4096]{1,0:T(8,128)(2,1)S(1)}, bf16[16,4096]{1,0:T(8,128)(2,1)}, u32[]{:S(2)}) copy-start(bf16[16,4096]{1,0:T(8,128)(2,1)} %param.13) | copy-start | bytes 393220
  6.5 10.4 %copy-start.8 = (bf16[32,64,128]{2,1,0:T(8,128)(2,1)S(1)}, bf16[32,64,128]{2,1,0:T(8,128)(2,1)}, u32[]{:S(2)}) copy-start(bf16[32,64,128]{2,1,0:T(8,128)(2,1)} %param.17) | copy-start | bytes 1572868
  6.5 10.7 %copy-start.5 = (bf16[32,64,64]{2,1,0:T(8,128)(2,1)S(1)}, bf16[32,64,64]{2,1,0:T(8,128)(2,1)}, u32[]{:S(2)}) copy-start(bf16[32,64,64]{2,1,0:T(8,128)(2,1)} %param.18) | copy-start | bytes 786436
  6.5 157.0 %all-gather.2.cloned.1.call-start = ((), (), s32[]{:S(2)}) async-start(), calls=%async_computation | async-start | bytes 2113536 | tf_op jit(solution)/shard_map/all_gather | solution.py:103
  7.7 7.3 %copy-start.3 = (f32[16,4096]{1,0:T(8,128)}, f32[16,4096]{1,0:T(8,128)S(1)}, u32[]{:S(2)}) copy-start(f32[16,4096]{1,0:T(8,128)S(1)} %convert_element_type.27) | copy-start | bytes 786436
  9.1 9.1 %copy-start.13 = (s32[1,17,16]{1,2,0:T(8,128)S(1)}, s32[1,17,16]{1,2,0:T(8,128)}, u32[]{:S(2)}) copy-start(s32[1,17,16]{1,2,0:T(8,128)} %param.19) | copy-start | bytes 3268
  9.1 99.5 %collective-permute-start.17 = (f32[20,1024]{1,0:T(8,128)}, f32[20,1024]{1,0:T(8,128)}, u32[]{:S(2)}, u32[]{:S(2)}) collective-permute-start(f32[20,1024]{1,0:T(8,128)} %pad_maximum_fusion.2), channel_id=1, source_target_pairs={{1,0},{2,1},{3,2},{4,3},{5,4},{6,5},{7,6},{8,7},{9,8},{10,9},{11,1... | collective-permute-start | bytes 245768 | tf_op jit(solution)/shard_map/ppermute | solution.py:19
  15.0 57.4 %collective-permute-start.16 = (bf16[20,1024]{1,0:T(8,128)(2,1)}, bf16[20,1024]{1,0:T(8,128)(2,1)}, u32[]{:S(2)}, u32[]{:S(2)}) collective-permute-start(bf16[20,1024]{1,0:T(8,128)(2,1)} %slice.154), channel_id=1, source_target_pairs={{0,1},{1,2},{2,3},{3,4},{4,5},{5,6},{6,7},{7,8},{8,9},{9,10},{10,1... | collective-permute-start | bytes 122888 | tf_op jit(solution)/shard_map/ppermute | solution.py:19
  20.5 14.1 %copy-start.11 = (s32[32,32]{1,0:T(8,128)S(1)}, s32[32,32]{1,0:T(8,128)}, u32[]{:S(2)}) copy-start(s32[32,32]{1,0:T(8,128)} %param.20) | copy-start | bytes 12292
  20.5 14.7 %copy-start.15 = (s32[32,13]{0,1:T(8,128)S(1)}, s32[32,13]{0,1:T(8,128)}, u32[]{:S(2)}) copy-start(s32[32,13]{0,1:T(8,128)} %param.16) | copy-start | bytes 4996
  22.0 13.3 %copy-start.16 = (s32[4,32]{1,0:T(4,128)S(1)}, s32[4,32]{1,0:T(4,128)}, u32[]{:S(2)}) copy-start(s32[4,32]{1,0:T(4,128)} %param.22) | copy-start | bytes 1540
  22.7 14.5 %collective-permute-start = (bf16[16,16,64]{2,1,0:T(8,128)(2,1)S(1)}, bf16[16,16,64]{2,1,0:T(8,128)(2,1)S(1)}, u32[]{:S(2)}, u32[]{:S(2)}) collective-permute-start(bf16[16,16,64]{2,1,0:T(8,128)(2,1)S(1)} %get-tuple-element.91), channel_id=1, source_target_pairs={{0,8},{1,9},{2,10},{3,11},{4,12},{5,13},{6,14},{7,15},{8,16},{9,17... | collective-permute-start | bytes 98312 | tf_op jit(solution)/shard_map/ppermute | solution.py:19
  28.3 12.4 %collective-permute-start.1 = (bf16[16,16,64]{2,1,0:T(8,128)(2,1)}, bf16[16,16,64]{2,1,0:T(8,128)(2,1)}, u32[]{:S(2)}, u32[]{:S(2)}) collective-permute-start(bf16[16,16,64]{2,1,0:T(8,128)(2,1)} %get-tuple-element.90), channel_id=1, source_target_pairs={{0,7},{1,8},{2,9},{3,10},{4,11},{5,12},{6,13},{7,14},{8,15},{9,16}... | collective-permute-start | bytes 98312 | tf_op jit(solution)/shard_map/ppermute | solution.py:19
  32.6 13.2 %collective-permute-start.2 = (bf16[16,16,64]{2,1,0:T(8,128)(2,1)}, bf16[16,16,64]{2,1,0:T(8,128)(2,1)}, u32[]{:S(2)}, u32[]{:S(2)}) collective-permute-start(bf16[16,16,64]{2,1,0:T(8,128)(2,1)} %get-tuple-element.89), channel_id=1, source_target_pairs={{0,6},{1,7},{2,8},{3,9},{4,10},{5,11},{6,12},{7,13},{8,14},{9,15},... | collective-permute-start | bytes 98312 | tf_op jit(solution)/shard_map/ppermute | solution.py:19
  37.8 26.8 %copy-start.7 = (f32[3,4096]{1,0:T(4,128)S(1)}, f32[3,4096]{1,0:T(4,128)}, u32[]{:S(2)}) copy-start(f32[3,4096]{1,0:T(4,128)} %param.14) | copy-start | bytes 147460
  37.8 10.8 %collective-permute-start.3 = (bf16[16,16,64]{2,1,0:T(8,128)(2,1)}, bf16[16,16,64]{2,1,0:T(8,128)(2,1)S(1)}, u32[]{:S(2)}, u32[]{:S(2)}) collective-permute-start(bf16[16,16,64]{2,1,0:T(8,128)(2,1)} %get-tuple-element.88), channel_id=1, source_target_pairs={{0,5},{1,6},{2,7},{3,8},{4,9},{5,10},{6,11},{7,12},{8,13},{9,14},{... | collective-permute-start | bytes 98312 | tf_op jit(solution)/shard_map/ppermute | solution.py:19
  40.7 11.7 %collective-permute-start.4 = (bf16[16,16,64]{2,1,0:T(8,128)(2,1)S(1)}, bf16[16,16,64]{2,1,0:T(8,128)(2,1)S(1)}, u32[]{:S(2)}, u32[]{:S(2)}) collective-permute-start(bf16[16,16,64]{2,1,0:T(8,128)(2,1)S(1)} %get-tuple-element.87), channel_id=1, source_target_pairs={{0,4},{1,5},{2,6},{3,7},{4,8},{5,9},{6,10},{7,11},{8,12},{9,13},{1... | collective-permute-start | bytes 98312 | tf_op jit(solution)/shard_map/ppermute | solution.py:19
  45.8 10.1 %collective-permute-start.5 = (bf16[16,16,64]{2,1,0:T(8,128)(2,1)S(1)}, bf16[16,16,64]{2,1,0:T(8,128)(2,1)S(1)}, u32[]{:S(2)}, u32[]{:S(2)}) collective-permute-start(bf16[16,16,64]{2,1,0:T(8,128)(2,1)S(1)} %get-tuple-element.86), channel_id=1, source_target_pairs={{0,3},{1,4},{2,5},{3,6},{4,7},{5,8},{6,9},{7,10},{8,11},{9,12},{10... | collective-permute-start | bytes 98312 | tf_op jit(solution)/shard_map/ppermute | solution.py:19
  48.6 10.1 %collective-permute-start.6 = (bf16[16,16,64]{2,1,0:T(8,128)(2,1)S(1)}, bf16[16,16,64]{2,1,0:T(8,128)(2,1)S(1)}, u32[]{:S(2)}, u32[]{:S(2)}) collective-permute-start(bf16[16,16,64]{2,1,0:T(8,128)(2,1)S(1)} %get-tuple-element.85), channel_id=1, source_target_pairs={{0,2},{1,3},{2,4},{3,5},{4,6},{5,7},{6,8},{7,9},{8,10},{9,11},{10,... | collective-permute-start | bytes 98312 | tf_op jit(solution)/shard_map/ppermute | solution.py:19
  52.4 7.8 %collective-permute-start.7 = (bf16[16,16,64]{2,1,0:T(8,128)(2,1)S(1)}, bf16[16,16,64]{2,1,0:T(8,128)(2,1)S(1)}, u32[]{:S(2)}, u32[]{:S(2)}) collective-permute-start(bf16[16,16,64]{2,1,0:T(8,128)(2,1)S(1)} %get-tuple-element.84), channel_id=1, source_target_pairs={{0,1},{1,2},{2,3},{3,4},{4,5},{5,6},{6,7},{7,8},{8,9},{9,10},{10,1... | collective-permute-start | bytes 98312 | tf_op jit(solution)/shard_map/ppermute | solution.py:19
  62.1 15.6 %collective-permute-start.8 = (bf16[16,16,64]{2,1,0:T(8,128)(2,1)}, bf16[16,16,64]{2,1,0:T(8,128)(2,1)}, u32[]{:S(2)}, u32[]{:S(2)}) collective-permute-start(bf16[16,16,64]{2,1,0:T(8,128)(2,1)} %get-tuple-element.82), channel_id=1, source_target_pairs={{1,0},{2,1},{3,2},{4,3},{5,4},{6,5},{7,6},{8,7},{9,8},{10,9},{11,1... | collective-permute-start | bytes 98312 | tf_op jit(solution)/shard_map/ppermute | solution.py:19
  65.2 15.2 %collective-permute-start.9 = (bf16[16,16,64]{2,1,0:T(8,128)(2,1)}, bf16[16,16,64]{2,1,0:T(8,128)(2,1)S(1)}, u32[]{:S(2)}, u32[]{:S(2)}) collective-permute-start(bf16[16,16,64]{2,1,0:T(8,128)(2,1)} %get-tuple-element.81), channel_id=1, source_target_pairs={{2,0},{3,1},{4,2},{5,3},{6,4},{7,5},{8,6},{9,7},{10,8},{11,9},{12,... | collective-permute-start | bytes 98312 | tf_op jit(solution)/shard_map/ppermute | solution.py:19
  68.8 16.3 %collective-permute-start.10 = (bf16[16,16,64]{2,1,0:T(8,128)(2,1)}, bf16[16,16,64]{2,1,0:T(8,128)(2,1)S(1)}, u32[]{:S(2)}, u32[]{:S(2)}) collective-permute-start(bf16[16,16,64]{2,1,0:T(8,128)(2,1)} %get-tuple-element.80), channel_id=1, source_target_pairs={{3,0},{4,1},{5,2},{6,3},{7,4},{8,5},{9,6},{10,7},{11,8},{12,9},{13... | collective-permute-start | bytes 98312 | tf_op jit(solution)/shard_map/ppermute | solution.py:19
  72.4 19.3 %collective-permute-start.11 = (bf16[16,16,64]{2,1,0:T(8,128)(2,1)}, bf16[16,16,64]{2,1,0:T(8,128)(2,1)S(1)}, u32[]{:S(2)}, u32[]{:S(2)}) collective-permute-start(bf16[16,16,64]{2,1,0:T(8,128)(2,1)} %get-tuple-element.79), channel_id=1, source_target_pairs={{4,0},{5,1},{6,2},{7,3},{8,4},{9,5},{10,6},{11,7},{12,8},{13,9},{1... | collective-permute-start | bytes 98312 | tf_op jit(solution)/shard_map/ppermute | solution.py:19
  77.7 16.0 %collective-permute-start.12 = (bf16[16,16,64]{2,1,0:T(8,128)(2,1)S(1)}, bf16[16,16,64]{2,1,0:T(8,128)(2,1)S(1)}, u32[]{:S(2)}, u32[]{:S(2)}) collective-permute-start(bf16[16,16,64]{2,1,0:T(8,128)(2,1)S(1)} %get-tuple-element.78), channel_id=1, source_target_pairs={{5,0},{6,1},{7,2},{8,3},{9,4},{10,5},{11,6},{12,7},{13,8},{14,9},{... | collective-permute-start | bytes 98312 | tf_op jit(solution)/shard_map/ppermute | solution.py:19
  80.4 13.2 %collective-permute-start.13 = (bf16[16,16,64]{2,1,0:T(8,128)(2,1)S(1)}, bf16[16,16,64]{2,1,0:T(8,128)(2,1)S(1)}, u32[]{:S(2)}, u32[]{:S(2)}) collective-permute-start(bf16[16,16,64]{2,1,0:T(8,128)(2,1)S(1)} %get-tuple-element.77), channel_id=1, source_target_pairs={{6,0},{7,1},{8,2},{9,3},{10,4},{11,5},{12,6},{13,7},{14,8},{15,9},... | collective-permute-start | bytes 98312 | tf_op jit(solution)/shard_map/ppermute | solution.py:19
  85.1 8.6 %collective-permute-start.14 = (bf16[16,16,64]{2,1,0:T(8,128)(2,1)S(1)}, bf16[16,16,64]{2,1,0:T(8,128)(2,1)S(1)}, u32[]{:S(2)}, u32[]{:S(2)}) collective-permute-start(bf16[16,16,64]{2,1,0:T(8,128)(2,1)S(1)} %get-tuple-element.76), channel_id=1, source_target_pairs={{7,0},{8,1},{9,2},{10,3},{11,4},{12,5},{13,6},{14,7},{15,8},{16,9}... | collective-permute-start | bytes 98312 | tf_op jit(solution)/shard_map/ppermute | solution.py:19
  91.7 8.3 %collective-permute-start.15 = (bf16[16,16,64]{2,1,0:T(8,128)(2,1)S(1)}, bf16[16,16,64]{2,1,0:T(8,128)(2,1)S(1)}, u32[]{:S(2)}, u32[]{:S(2)}) collective-permute-start(bf16[16,16,64]{2,1,0:T(8,128)(2,1)S(1)} %get-tuple-element.75), channel_id=1, source_target_pairs={{8,0},{9,1},{10,2},{11,3},{12,4},{13,5},{14,6},{15,7},{16,8},{17,9... | collective-permute-start | bytes 98312 | tf_op jit(solution)/shard_map/ppermute | solution.py:19
  100.0 8.7 %copy-start.4 = (f32[16,4096]{1,0:T(8,128)S(1)}, f32[16,4096]{1,0:T(8,128)}, u32[]{:S(2)}) copy-start(f32[16,4096]{1,0:T(8,128)} %copy-done.3) | copy-start | bytes 786436
  100.0 8.7 %copy-start.10 = (f32[4096]{0:T(1024)S(1)}, f32[4096]{0:T(1024)}, u32[]{:S(2)}) copy-start(f32[4096]{0:T(1024)} %param.15) | copy-start | bytes 49156
  110.8 52.7 %copy-start.14 = (s32[1024]{0:T(1024)S(1)}, s32[1024]{0:T(1024)}, u32[]{:S(2)}) copy-start(s32[1024]{0:T(1024)} %pad_clamp_fusion.1) | copy-start | bytes 12292
  (9 other events, 14.6 us)
Sparse Core Ops, SparseCore 0:
  18.3 67.4 all-gather.1
where the time goes:
time: 187 us; the launch traced here: 185 us
  starting transfers between devices  61.4 us (33%)
  local copies, waits for them, and re-layouts  42 us (22%)
  matrix products  40.8 us (22%)
  between operations  13.9 us (7%)
  other arithmetic  13.8 us (7%)
  waiting for transfers between devices  10.5 us (6%)
  loops' own time  2.73 us (1%)
    ppermute x18, starting transfers between devices, from_behind(): return lax.ppermute(shard, axis, pairs)  61.4 us
    dot_general x4, matrix products, near_block(): jnp.einsum('lisj,rlsj->rli', kernel, partner_values, preferred_element_ty...  28.1 us
    ppermute x18, waiting for transfers between devices, from_behind(): return lax.ppermute(shard, axis, pairs)  10.5 us
    dot_general x1, matrix products, local(): jnp.einsum('lkm,lrk->rlm', leaf_basis, leaf_field, preferred_element_type...  9.65 us
    gather x1, local copies, waits for them, and re-layouts, local(): picked = jnp.take(received, relay_refs, axis=0)  8.65 us
    gather x4, local copies, waits for them, and re-layouts, near_block(): partner_data = jnp.take(extended, partner_rows, axis=1)  6.81 us
    unnamed x54, local copies, waits for them, and re-layouts  6.06 us
    while x8, local copies, waits for them, and re-layouts  4.23 us
  transfers between devices with their start and end apart: 19, of which 3 were waited for; matrix products, arithmetic and copies ran while one was open for 40% of the time, Pallas kernels for 0%

commit v1 on v0

v1 whole, which is shorter than its diff:
```python
import functools
import math

import jax
import jax.numpy as jnp
from jax import lax
from jax.experimental import pallas as pl
from jax.experimental.pallas import tpu as pltpu
from jax.sharding import PartitionSpec as P

AXES = ("gx", "gy")
REACH = 8
WINDOW = 8
ROW = 8
core_square = 0.0004
four_pi = 4.0 * math.pi
f32 = jnp.float32
bf16 = jnp.bfloat16
VMEM_LIMIT = 40 << 20

SMEM = pl.BlockSpec(memory_space=pltpu.SMEM)
VMEM = pl.BlockSpec(memory_space=pltpu.VMEM)


def nt(a, b):
    return lax.dot_general(a, b, (((1,), (1,)), ((), ())), preferred_element_type=f32)


def low_half(shape):
    return lax.broadcasted_iota(jnp.int32, shape, len(shape) - 1) < 64


def pieces(x):
    first = x.astype(bf16)
    rest = x - first.astype(f32)
    second = rest.astype(bf16)
    third = (rest - second.astype(f32)).astype(bf16)
    return first, second, third


def upward_kernel(
    column_ref, lists_ref, dens_ref, points_ref, weights_ref, basis_ref, transfer_ref,
    pack_ref, below_ref, above_ref, own_ref, up_ref, down_ref, coarse_ref, both_ref,
):
    leaves = basis_ref.shape[0]
    rim = REACH * 128
    for part in range(4):
        span = pl.ds(part * 1024, 1024)
        scaled = dens_ref[:, span].astype(f32) * (weights_ref[:, span] * (1.0 / four_pi))
        pack_ref[0:16, span] = scaled.astype(bf16)
        one, two, three = pieces(points_ref[:, span])
        rows = jnp.concatenate(
            [one.astype(f32), two.astype(f32), three.astype(f32), jnp.zeros((7, 1024), f32)], axis=0
        )
        pack_ref[16:32, span] = rows.astype(bf16)
    below_ref[...] = pack_ref[:, -rim:]
    above_ref[...] = pack_ref[:, :rim]

    coarse = []
    for group in range(leaves // 8):
        total = jnp.zeros((16, 64), f32)
        for child in range(8):
            leaf = group * 8 + child
            basis = basis_ref[leaf]
            twice = nt(dens_ref[:, leaf * 128 : (leaf + 1) * 128], jnp.concatenate([basis, basis], axis=0))
            rounded = twice.astype(bf16)
            both_ref[leaf] = rounded
            total += jnp.dot(rounded[:, :64], transfer_ref[leaf], preferred_element_type=f32)
        coarse.append(total)
    for pair in range(len(coarse) // 2):
        tile = jnp.concatenate([coarse[2 * pair], coarse[2 * pair + 1]], axis=1).astype(bf16)
        coarse_ref[:, pair] = jnp.broadcast_to(tile[None], (coarse_ref.shape[0], 16, 128))

    column = column_ref[0]
    mask = low_half((16, 128))

    def fill(target, carry):
        for ref, window in (
            (own_ref, target - column + WINDOW),
            (up_ref, jnp.minimum(target - column + 2 * WINDOW, 2 * WINDOW)),
            (down_ref, jnp.maximum(target - column, 0)),
        ):
            for slot in range(8):
                ref[target, slot] = jnp.where(
                    mask, both_ref[lists_ref[slot, window]], both_ref[lists_ref[slot + 8, window]]
                )
        return carry

    lax.fori_loop(0, ROW, fill, 0)


def upward(column, lists, densities, points, weights, basis, transfer):
    count = densities.shape[1]
    leaves = basis.shape[0]
    block = jax.ShapeDtypeStruct((ROW, 8, 16, 128), bf16)
    return pl.pallas_call(
        upward_kernel,
        name="upward",
        out_shape=(
            jax.ShapeDtypeStruct((32, count), bf16),
            jax.ShapeDtypeStruct((32, REACH * 128), bf16),
            jax.ShapeDtypeStruct((32, REACH * 128), bf16),
            block, block, block,
            jax.ShapeDtypeStruct((128, leaves // 16, 16, 128), bf16),
        ),
        in_specs=[SMEM, SMEM, VMEM, VMEM, VMEM, VMEM, VMEM],
        out_specs=[VMEM] * 7,
        scratch_shapes=[pltpu.VMEM((leaves, 16, 128), bf16)],
        compiler_params=pltpu.CompilerParams(vmem_limit_bytes=VMEM_LIMIT),
        cost_estimate=pl.CostEstimate(flops=20_000_000, bytes_accessed=4 << 20, transcendentals=0),
    )(column, lists, densities, points, weights, basis, transfer)


def near_kernel(first, leaves, offsets_ref, pack_ref, below_ref, above_ref, near_ref, left_ref, right_ref, wide_ref):
    rim = REACH * 128
    inner = pack_ref.shape[1]

    def build(source, at, start, width, own):
        wide_ref[:, pl.ds(at, width)] = source[0:16, pl.ds(start, width)]
        rows = source[16:32, pl.ds(start, width)].astype(f32)
        one, two, three = rows[0:3], rows[3:6], rows[6:9]
        whole = (one + two) + three
        square = whole[0:1] * whole[0:1] + whole[1:2] * whole[1:2] + whole[2:3] * whole[2:3]
        ones = jnp.ones((3, width), f32)
        m1, m2, m3 = (p.astype(f32) for p in pieces(square))
        fill = jnp.zeros((8, width), f32)
        right = jnp.concatenate(
            [one, two, one, two, three, one, ones, m1, m2, m3, fill], axis=0
        )
        right_ref[:, pl.ds(at, width)] = right.astype(bf16)
        if own:
            n1, n2, n3 = (p.astype(f32) for p in pieces(square + core_square))
            left = jnp.concatenate(
                [-2 * one, -2 * one, -2 * two, -2 * two, -2 * one, -2 * three, n1, n2, n3, ones, fill], axis=0
            )
            left_ref[:, pl.ds(start, width)] = left.astype(bf16)

    for part in range(rim // 512):
        build(below_ref, part * 512, part * 512, 512, False)
        build(above_ref, rim + inner + part * 512, part * 512, 512, False)
    for part in range(inner // 512):
        build(pack_ref, rim + part * 512, part * 512, 512, True)

    slots = offsets_ref.shape[0]

    def one_leaf(step, carry):
        leaf = first + step
        own = left_ref[:, pl.ds(pl.multiple_of(leaf * 128, 128), 128)]
        total = jnp.zeros((16, 128), f32)
        for slot in range(0, slots, 2):
            spans = [
                pl.ds(pl.multiple_of((leaf + REACH + offsets_ref[s, leaf]) * 128, 128), 128)
                for s in range(slot, min(slot + 2, slots))
            ]
            right = jnp.concatenate([right_ref[:, span] for span in spans], axis=1)
            wide = jnp.concatenate([wide_ref[:, span] for span in spans], axis=1)
            square = lax.dot_general(own, right, (((0,), (0,)), ((), ())), preferred_element_type=f32)
            total += nt(wide, lax.rsqrt(square).astype(bf16))
        near_ref[:, pl.ds(pl.multiple_of(step * 128, 128), 128)] = total
        return carry

    lax.fori_loop(0, leaves, one_leaf, 0)


def near_field(offsets, pack, below, above, first, leaves):
    count = pack.shape[1]
    wide = count + 2 * REACH * 128
    points = leaves * 128 * offsets.shape[0] * 128
    return pl.pallas_call(
        functools.partial(near_kernel, first, leaves),
        name="near",
        out_shape=jax.ShapeDtypeStruct((16, leaves * 128), f32),
        in_specs=[SMEM, VMEM, VMEM, VMEM],
        out_specs=VMEM,
        scratch_shapes=[
            pltpu.VMEM((32, count), bf16),
            pltpu.VMEM((32, wide), bf16),
            pltpu.VMEM((16, wide), bf16),
        ],
        compiler_params=pltpu.CompilerParams(vmem_limit_bytes=VMEM_LIMIT),
        cost_estimate=pl.CostEstimate(flops=points * 96, bytes_accessed=1 << 20, transcendentals=points),
    )(offsets, pack, below, above)


def spread_matrix():
    row = lax.broadcasted_iota(jnp.int32, (128, 256), 0)
    col = lax.broadcasted_iota(jnp.int32, (128, 256), 1)
    hit = ((row // 64) == (col // 128)) & ((row % 64) == (col % 64))
    return jnp.where(hit, 1.0, 0.0).astype(bf16)


def coupled(coupling_ref, block, slots, pick):
    mask = low_half((16, 128))
    rows = [jnp.where(mask, pick(s), pick(s + 1)) for s in range(0, slots, 2)]
    left = jnp.concatenate(rows, axis=1)
    right = jnp.concatenate([coupling_ref[block, s] for s in range(slots)], axis=1)
    return nt(left, right)


def leaf_kernel(column_ref, refs_ref, swapped_ref, below_ref, above_ref, coupling_ref, local_ref, table_ref):
    step = pl.program_id(0)
    per_step, slots = coupling_ref.shape[:2]

    @pl.when(step == 0)
    def _():
        column = column_ref[0]
        spread = spread_matrix()

        def put(window, tiles):
            out = jnp.dot(tiles.reshape(8 * 16, 128), spread, preferred_element_type=f32).astype(bf16)
            out = out.reshape(8, 16, 256)
            table_ref[pl.ds(window * 16, 8)] = out[:, :, :128]
            table_ref[pl.ds(window * 16 + 8, 8)] = out[:, :, 128:]

        put(0, below_ref[column])
        put(2 * WINDOW, above_ref[column])
        for window in range(1, 2 * WINDOW):
            place = column + window
            owner = lax.rem(place, ROW)
            crossed = jnp.where((place >= ROW) & (place < 2 * ROW), 0, 1)
            put(window, swapped_ref[owner, crossed])

    for block in range(per_step):
        leaf = step * per_step + block
        local_ref[block] = coupled(
            coupling_ref, block, slots, lambda s: table_ref[refs_ref[leaf, s]]
        )


def leaf_local(column, refs, swapped, below, above, coupling):
    leaves, slots = coupling.shape[:2]
    per_step = 4
    table = (2 * WINDOW + 1) * 16
    return pl.pallas_call(
        leaf_kernel,
        name="leaf_local",
        out_shape=jax.ShapeDtypeStruct((leaves, 16, 64), f32),
        grid_spec=pltpu.PrefetchScalarGridSpec(
            num_scalar_prefetch=2,
            grid=(leaves // per_step,),
            in_specs=[
                VMEM, VMEM, VMEM,
                pl.BlockSpec((per_step, slots, 64, 64), lambda i, *_: (i, 0, 0, 0)),
            ],
            out_specs=pl.BlockSpec((per_step, 16, 64), lambda i, *_: (i, 0, 0)),
            scratch_shapes=[pltpu.VMEM((table, 16, 128), bf16)],
        ),
        compiler_params=pltpu.CompilerParams(vmem_limit_bytes=VMEM_LIMIT),
        cost_estimate=pl.CostEstimate(flops=leaves * slots * 64 * 64 * 32, bytes_accessed=18 << 20, transcendentals=0),
    )(column, refs, swapped, below, above, coupling)


def downward_kernel(
    refs_ref, coarse_ref, coupling_ref, transfer_ref, basis_ref, local_ref, near_ref, out_ref, picked_ref
):
    groups, slots = coupling_ref.shape[:2]
    mask = low_half((16, 128))
    for group in range(groups):
        for slot in range(slots):
            ref = refs_ref[group, slot]
            tile = coarse_ref[ref // 4, lax.rem(ref, 4) // 2]
            keep = mask == (lax.rem(ref, 2) == 0)
            picked_ref[group * slots + slot] = jnp.where(keep, tile, jnp.zeros_like(tile))
    row = lax.broadcasted_iota(jnp.int32, (128, 128), 0)
    col = lax.broadcasted_iota(jnp.int32, (128, 128), 1)
    fold = jnp.where((row % 64) == (col % 64), 1.0, 0.0).astype(bf16)
    for group in range(groups):
        tiles = picked_ref[pl.ds(group * slots, slots)].reshape(slots * 16, 128)
        both = jnp.dot(tiles, fold, preferred_element_type=f32).astype(bf16).reshape(slots, 16, 128)
        local1 = coupled(coupling_ref, group, slots, lambda s: both[s]).astype(bf16)
        for child in range(8):
            leaf = group * 8 + child
            field = (local_ref[leaf] + nt(local1, transfer_ref[leaf])).astype(bf16)
            span = slice(leaf * 128, (leaf + 1) * 128)
            out_ref[:, span] = near_ref[:, span] + jnp.dot(
                field, basis_ref[leaf], preferred_element_type=f32
            )


def downward(refs, coarse, coupling, transfer, basis, local0, near):
    groups, slots = coupling.shape[:2]
    return pl.pallas_call(
        downward_kernel,
        name="downward",
        out_shape=jax.ShapeDtypeStruct(near.shape, f32),
        in_specs=[SMEM] + [VMEM] * 6,
        out_specs=VMEM,
        scratch_shapes=[pltpu.VMEM((groups * slots, 16, 128), bf16)],
        compiler_params=pltpu.CompilerParams(vmem_limit_bytes=VMEM_LIMIT),
        cost_estimate=pl.CostEstimate(flops=60_000_000, bytes_accessed=4 << 20, transcendentals=0),
    )(refs, coarse, coupling, transfer, basis, local0, near)


def shifted(shard, by, devices):
    return lax.ppermute(shard, AXES, [(i, i + by) for i in range(devices) if 0 <= i + by < devices])


def local(
    densities, points, weights, near_offsets, leaf_basis, transfer, send_lists, relay_refs, leaf_coupling,
    coarse_refs, coarse_coupling,
):
    devices = lax.axis_size(AXES)
    column = lax.rem(lax.axis_index("gy").astype(jnp.int32), ROW).reshape(1)
    rows = [[row * ROW + i for i in range(ROW)] for row in range(devices // ROW)]
    pack, rim_last, rim_first, own, up, down, coarse = upward(
        column, send_lists[0].T, densities, points, weights[None, :], leaf_basis, transfer
    )
    everyone = lax.all_to_all(coarse, AXES, 0, 0, tiled=True)
    from_below = shifted(rim_last, 1, devices)
    from_above = shifted(rim_first, -1, devices)
    lists_below = shifted(up, ROW, devices)
    lists_above = shifted(down, -ROW, devices)
    crossing = jnp.where(
        jnp.arange(ROW, dtype=jnp.int32)[:, None, None, None] < column[0], lists_below, lists_above
    )
    swapped = lax.all_to_all(
        jnp.stack([own, crossing], axis=1), AXES, 0, 0, axis_index_groups=rows, tiled=True
    )
    near = near_field(near_offsets.T, pack, from_below, from_above, 0, near_offsets.shape[0])
    local0 = leaf_local(column, relay_refs, swapped, lists_below, lists_above, leaf_coupling)
    return downward(coarse_refs, everyone, coarse_coupling, transfer, leaf_basis, local0, near)


def solution(mesh):
    in_specs = (
        P(None, AXES),
        P(None, AXES),
        P(AXES),
        P(AXES, None),
        P(AXES, None, None),
        P(AXES, None, None),
        P(AXES, None, None),
        P(AXES, None),
        P(AXES, None, None, None),
        P(AXES, None),
        P(AXES, None, None, None),
    )
    return jax.shard_map(local, mesh=mesh, in_specs=in_specs, out_specs=P(None, AXES), check_vma=False)
```

time: 187 us -> 115 us (0.61)
  the two profiles are of different devices: /device:TPU:98 before, /device:TPU:4 now
where the time goes in v1:
time: 115 us; the launch traced here: 114 us
  Pallas kernels  49.5 us (43%)
  starting transfers between devices  26.5 us (23%)
  blocking collectives  14.7 us (13%)
  waiting for transfers between devices  14.3 us (12%)
  local copies, waits for them, and re-layouts  9.28 us (8%)
    pallas_call x1, Pallas kernels, near_field(): pl.pallas_call(functools.partial(near_kernel, first, leaves), name='near'...  28.2 us
    ppermute x4, starting transfers between devices, shifted(): lax.ppermute(shard, AXES, [(i, i + by) for i in range(devices) if 0 <= i...  17.7 us
    all_to_all x1, blocking collectives, local(): lax.all_to_all(jnp.stack([own, crossing], axis=1), AXES, 0, 0, axis_index...  14.7 us
    ppermute x4, waiting for transfers between devices, shifted(): lax.ppermute(shard, AXES, [(i, i + by) for i in range(devices) if 0 <= i...  14.2 us
    pallas_call x1, Pallas kernels, leaf_local(): pl.pallas_call(leaf_kernel, name='leaf_local', out_shape=jax.ShapeDtypeSt...  10.6 us
    unnamed x32, local copies, waits for them, and re-layouts  9.24 us
    all_to_all x1, starting transfers between devices, local(): everyone = lax.all_to_all(coarse, AXES, 0, 0, tiled=True)  8.78 us
    pallas_call x1, Pallas kernels, downward(): pl.pallas_call(downward_kernel, name='downward', out_shape=jax.ShapeDtype...  7.25 us
  transfers between devices with their start and end apart: 5, of which 3 were waited for; matrix products, arithmetic and copies ran while one was open for 0% of the time, Pallas kernels for 34%

profile of v1, /device:TPU:4, one launch (start us, length us, event | category | flops | bytes accessed | tf_op | source)
XLA Modules:
  0.0 114.5 jit_solution(1363034926107257430)
XLA Ops:
  0.0 1.1 copy-done
  1.1 1.0 copy-done.2
  2.1 0.9 copy-done.8
  3.0 0.8 copy-done.9
  3.8 0.7 copy-done.10
  4.6 0.7 copy-done.12
  5.3 3.5 %upward.1 = (bf16[32,4096]{1,0:T(8,128)(2,1)S(1)}, bf16[32,1024]{1,0:T(8,128)(2,1)S(1)}, bf16[32,1024]{1,0:T(8,128)(2,1)S(1)}, bf16[8,8,16,128]{3,2,1,0:T(8,128)...) custom-call(s32[1]{0:T(128)} %bitcast.column_ref, ...), custom_call_target="tpu_custom_call" | custom-call | flops 20000000 | bytes 4194304 | tf_op jit(solution)/shard_map/upward/pallas_call | solution.py:96
  8.7 0.0 copy-start.14
  8.8 0.0 copy-start.5
  8.8 3.8 %collective-permute-start = (bf16[8,8,16,128]{3,2,1,0:T(8,128)(2,1)S(1)}, bf16[8,8,16,128]{3,2,1,0:T(8,128)(2,1)S(1)}, u32[]{:S(2)}, u32[]{:S(2)}) collective-permute-start(bf16[8,8,16,128]{3,2,1,0:T(8,128)(2,1)S(1)} %get-tuple-element.14), channel_id=1, source_target_pairs={{0,8},{1,9},{2,10},{3,11},{4,12},{5,13},{6,14},{7,15},{8,16},{9,17... | collective-permute-start | bytes 786440 | tf_op jit(solution)/shard_map/ppermute | solution.py:295
  12.6 4.1 %collective-permute-start.1 = (bf16[8,8,16,128]{3,2,1,0:T(8,128)(2,1)S(1)}, bf16[8,8,16,128]{3,2,1,0:T(8,128)(2,1)S(1)}, u32[]{:S(2)}, u32[]{:S(2)}) collective-permute-start(bf16[8,8,16,128]{3,2,1,0:T(8,128)(2,1)S(1)} %get-tuple-element.15), channel_id=1, source_target_pairs={{8,0},{9,1},{10,2},{11,3},{12,4},{13,5},{14,6},{15,7},{16,8},{17,9... | collective-permute-start | bytes 786440 | tf_op jit(solution)/shard_map/ppermute | solution.py:295
  16.8 4.2 %collective-permute-done.below_ref = bf16[8,8,16,128]{3,2,1,0:T(8,128)(2,1)S(1)} collective-permute-done((bf16[8,8,16,128]{3,2,1,0:T(8,128)(2,1)S(1)}, bf16[8,8,16,128]{3,2,1,0:T(8,128)(2,1)S(1)}, u32[]{:S(2)}, u32[]{:S(2)}) %collective-permute-start) | collective-permute-done | bytes 262176 | tf_op jit(solution)/shard_map/ppermute | solution.py:295
  21.0 1.5 %collective-permute-done.1.above_ref = bf16[8,8,16,128]{3,2,1,0:T(8,128)(2,1)S(1)} collective-permute-done((bf16[8,8,16,128]{3,2,1,0:T(8,128)(2,1)S(1)}, bf16[8,8,16,128]{3,2,1,0:T(8,128)(2,1)S(1)}, u32[]{:S(2)}, u32[]{:S(2)}) %collective-permute-start.1) | collective-permute-done | bytes 262176 | tf_op jit(solution)/shard_map/ppermute | solution.py:295
  22.4 0.1 select_bitcast_fusion
  22.5 0.1 pad_maximum_fusion
  22.7 14.7 %all_to_all.10.swapped_ref = bf16[8,2,8,16,128]{4,3,2,1,0:T(8,128)(2,1)S(1)} all-to-all(bf16[8,2,8,16,128]{4,3,2,1,0:T(8,128)(2,1)S(1)} %copy.13), channel_id=1, replica_groups={{0,1,2,3,4,5,6,7},{8,9,10,11,12,13,14,15},{16,17,18,19,20,21,22,23},{24..., dimensions={0} | all-to-all | bytes 1048576 | tf_op jit(solution)/shard_map/all_to_all | solution.py:316
  37.3 0.0 copy-done.5
  37.3 8.8 %all-to-all-start = ((bf16[128,2,16,128]{3,2,1,0:T(8,128)(2,1)}), bf16[128,2,16,128]{3,2,1,0:T(8,128)(2,1)S(1)}, u32[]{:S(2)}, u32[]{:S(2)}) async-start(bf16[128,2,16,128]{3,2,1,0:T(8,128)(2,1)} %copy-done.5), calls=%async_computation | async-start | bytes 2097152 | tf_op jit(solution)/shard_map/all_to_all | solution.py:308
  46.1 2.1 %collective-permute-start.2 = (bf16[32,1024]{1,0:T(8,128)(2,1)}, bf16[32,1024]{1,0:T(8,128)(2,1)S(1)}, u32[]{:S(2)}, u32[]{:S(2)}) collective-permute-start(bf16[32,1024]{1,0:T(8,128)(2,1)} %copy-done.14), channel_id=1, source_target_pairs={{0,1},{1,2},{2,3},{3,4},{4,5},{5,6},{6,7},{7,8},{8,9},{9,10},{10,1... | collective-permute-start | bytes 196616 | tf_op jit(solution)/shard_map/ppermute | solution.py:295
  48.2 7.7 %collective-permute-start.3 = (bf16[32,1024]{1,0:T(8,128)(2,1)S(1)}, bf16[32,1024]{1,0:T(8,128)(2,1)S(1)}, u32[]{:S(2)}, u32[]{:S(2)}) collective-permute-start(bf16[32,1024]{1,0:T(8,128)(2,1)S(1)} %get-tuple-element.18), channel_id=1, source_target_pairs={{1,0},{2,1},{3,2},{4,3},{5,4},{6,5},{7,6},{8,7},{9,8},{10,9},{11,1... | collective-permute-start | bytes 196616 | tf_op jit(solution)/shard_map/ppermute | solution.py:295
  55.9 8.6 %collective-permute-done.2.below_ref = bf16[32,1024]{1,0:T(8,128)(2,1)S(1)} collective-permute-done((bf16[32,1024]{1,0:T(8,128)(2,1)}, bf16[32,1024]{1,0:T(8,128)(2,1)S(1)}, u32[]{:S(2)}, u32[]{:S(2)}) %collective-permute-start.2) | collective-permute-done | bytes 65568 | tf_op jit(solution)/shard_map/ppermute | solution.py:295
  64.5 0.0 collective-permute-done.3.above_ref
  64.5 0.7 copy-done.15
  65.2 28.2 %near.1.near_ref = f32[16,4096]{1,0:T(8,128)S(1)} custom-call(s32[13,32]{1,0:T(8,128)S(1)} %bitcast.12, bf16[32,4096]{1,0:T(8,128)(2,1)S(1)} %get-tuple-element.16.pack_ref, bf16[32,1024]{1,0:T(8,128)(2,1)S(1)} %collective-permute-done.2.below_ref, bf16[32,1024]{1,0:T(8,128)(2,1)S(1)} %collective-permute-done.3.above_ref), custom_call_target="tpu_custom_call" | custom-call | flops 654311424 | bytes 1048576 | tf_op jit(solution)/shard_map/near/pallas_call | solution.py:169
  93.4 0.7 copy-done.6
  94.1 10.6 %leaf_local.1.local_ref = f32[32,16,64]{2,1,0:T(8,128)S(1)} custom-call(s32[1]{0:T(128)} %bitcast.column_ref, s32[32,32]{1,0:T(8,128)S(1)} %copy-done.11, bf16[8,2,8,16,128]{4,3,2,1,0:T(8,128)(2,1)S(1)} %all_to_all.10.swapped_ref, bf16[8,8,16,128]{3,2,1,0:T(8,128)(2,1)S(1)} %collective-permute-done.below_ref, ...), custom_call_target="tpu_custom_call" | custom-call | flops 134217728 | bytes 18874368 | tf_op jit(solution)/shard_map/leaf_local/pallas_call | solution.py:234
  104.7 0.0 all-to-all-done.coarse_ref
  104.7 0.0 copy-done.1
  104.7 0.0 copy-start.4
  104.7 1.6 %copy-done.4 = bf16[4,32,64,64]{3,2,1,0:T(8,128)(2,1)S(1)} copy-done((bf16[4,32,64,64]{3,2,1,0:T(8,128)(2,1)S(1)}, bf16[4,32,64,64]{3,2,1,0:T(8,128)(2,1)}, u32[]{:S(2)}) %copy-start.4) | copy-done | bytes 1048600
  106.3 0.9 copy-done.7
  107.3 7.2 %downward.1 = f32[16,4096]{1,0:T(8,128)} custom-call(s32[4,32]{1,0:T(4,128)S(1)} %copy-done.13, bf16[128,2,16,128]{3,2,1,0:T(8,128)(2,1)S(1)} %all-to-all-done.coarse_ref, bf16[4,32,64,64]{3,2,1,0:T(8,128)(2,1)S(1)} %copy-done.4, bf16[32,64,64]{2,1,0:T(8,128)(2,1)S(1)} %copy-done.3, bf16[32,64,128]{2,1,0:T(8,128)(2,1)S(1)} %copy-done.1, ...), custom_call_target="tpu_custom_call" | custom-call | flops 60000000 | bytes 4194304 | tf_op jit(solution)/shard_map/downward/pallas_call | solution.py:282
  (19 shorter events, 0.1 us)
Async XLA Ops:
  0.0 94.1 %copy-start.11 = (s32[32,32]{1,0:T(8,128)S(1)}, s32[32,32]{1,0:T(8,128)}, u32[]{:S(2)}) copy-start(s32[32,32]{1,0:T(8,128)} %refs_ref.2) | copy-start | bytes 12292
  0.0 1.1 copy-start
  1.1 1.0 copy-start.2
  2.1 0.9 copy-start.8
  3.0 0.8 copy-start.9
  3.8 0.7 copy-start.10
  4.6 0.7 copy-start.12
  8.7 13.9 %copy-start.14 = (bf16[32,1024]{1,0:T(8,128)(2,1)}, bf16[32,1024]{1,0:T(8,128)(2,1)S(1)}, u32[]{:S(2)}) copy-start(bf16[32,1024]{1,0:T(8,128)(2,1)S(1)} %get-tuple-element.17) | copy-start | bytes 196612
  8.8 28.6 %copy-start.5 = (bf16[128,2,16,128]{3,2,1,0:T(8,128)(2,1)}, bf16[128,2,16,128]{3,2,1,0:T(8,128)(2,1)S(1)}, u32[]{:S(2)}) copy-start(bf16[128,2,16,128]{3,2,1,0:T(8,128)(2,1)S(1)} %get-tuple-element.12) | copy-start | bytes 3145732
  8.8 12.2 %collective-permute-start = (bf16[8,8,16,128]{3,2,1,0:T(8,128)(2,1)S(1)}, bf16[8,8,16,128]{3,2,1,0:T(8,128)(2,1)S(1)}, u32[]{:S(2)}, u32[]{:S(2)}) collective-permute-start(bf16[8,8,16,128]{3,2,1,0:T(8,128)(2,1)S(1)} %get-tuple-element.14), channel_id=1, source_target_pairs={{0,8},{1,9},{2,10},{3,11},{4,12},{5,13},{6,14},{7,15},{8,16},{9,17... | collective-permute-start | bytes 786440 | tf_op jit(solution)/shard_map/ppermute | solution.py:295
  12.6 9.8 %collective-permute-start.1 = (bf16[8,8,16,128]{3,2,1,0:T(8,128)(2,1)S(1)}, bf16[8,8,16,128]{3,2,1,0:T(8,128)(2,1)S(1)}, u32[]{:S(2)}, u32[]{:S(2)}) collective-permute-start(bf16[8,8,16,128]{3,2,1,0:T(8,128)(2,1)S(1)} %get-tuple-element.15), channel_id=1, source_target_pairs={{8,0},{9,1},{10,2},{11,3},{12,4},{13,5},{14,6},{15,7},{16,8},{17,9... | collective-permute-start | bytes 786440 | tf_op jit(solution)/shard_map/ppermute | solution.py:295
  37.3 67.3 %copy-start.1 = (bf16[32,64,128]{2,1,0:T(8,128)(2,1)S(1)}, bf16[32,64,128]{2,1,0:T(8,128)(2,1)}, u32[]{:S(2)}) copy-start(bf16[32,64,128]{2,1,0:T(8,128)(2,1)} %basis_ref.3) | copy-start | bytes 1572868
  37.3 67.4 %copy-start.3 = (bf16[32,64,64]{2,1,0:T(8,128)(2,1)S(1)}, bf16[32,64,64]{2,1,0:T(8,128)(2,1)}, u32[]{:S(2)}) copy-start(bf16[32,64,64]{2,1,0:T(8,128)(2,1)} %transfer_ref.3) | copy-start | bytes 786436
  37.3 67.4 %copy-start.13 = (s32[4,32]{1,0:T(4,128)S(1)}, s32[4,32]{1,0:T(4,128)}, u32[]{:S(2)}) copy-start(s32[4,32]{1,0:T(4,128)} %refs_ref.3) | copy-start | bytes 1540
  37.3 67.3 %all-to-all-start = ((bf16[128,2,16,128]{3,2,1,0:T(8,128)(2,1)}), bf16[128,2,16,128]{3,2,1,0:T(8,128)(2,1)S(1)}, u32[]{:S(2)}, u32[]{:S(2)}) async-start(bf16[128,2,16,128]{3,2,1,0:T(8,128)(2,1)} %copy-done.5), calls=%async_computation | async-start | bytes 2097152 | tf_op jit(solution)/shard_map/all_to_all | solution.py:308
  46.1 18.3 %collective-permute-start.2 = (bf16[32,1024]{1,0:T(8,128)(2,1)}, bf16[32,1024]{1,0:T(8,128)(2,1)S(1)}, u32[]{:S(2)}, u32[]{:S(2)}) collective-permute-start(bf16[32,1024]{1,0:T(8,128)(2,1)} %copy-done.14), channel_id=1, source_target_pairs={{0,1},{1,2},{2,3},{3,4},{4,5},{5,6},{6,7},{7,8},{8,9},{9,10},{10,1... | collective-permute-start | bytes 196616 | tf_op jit(solution)/shard_map/ppermute | solution.py:295
  48.2 16.3 %collective-permute-start.3 = (bf16[32,1024]{1,0:T(8,128)(2,1)S(1)}, bf16[32,1024]{1,0:T(8,128)(2,1)S(1)}, u32[]{:S(2)}, u32[]{:S(2)}) collective-permute-start(bf16[32,1024]{1,0:T(8,128)(2,1)S(1)} %get-tuple-element.18), channel_id=1, source_target_pairs={{1,0},{2,1},{3,2},{4,3},{5,4},{6,5},{7,6},{8,7},{9,8},{10,9},{11,1... | collective-permute-start | bytes 196616 | tf_op jit(solution)/shard_map/ppermute | solution.py:295
  64.5 0.7 copy-start.15
  93.4 0.7 copy-start.6
  104.7 1.6 %copy-start.4 = (bf16[4,32,64,64]{3,2,1,0:T(8,128)(2,1)S(1)}, bf16[4,32,64,64]{3,2,1,0:T(8,128)(2,1)}, u32[]{:S(2)}) copy-start(bf16[4,32,64,64]{3,2,1,0:T(8,128)(2,1)} %coupling_ref.3) | copy-start | bytes 3145732
  106.3 0.9 copy-start.7

commit v2 on v1

v2 whole, which is shorter than its diff:
```python
import functools
import math

import jax
import jax.numpy as jnp
from jax import lax
from jax.experimental import pallas as pl
from jax.experimental.pallas import tpu as pltpu
from jax.sharding import PartitionSpec as P

AXES = ("gx", "gy")
REACH = 8
WINDOW = 8
ROW = 8
core_square = 0.0004
four_pi = 4.0 * math.pi
f32 = jnp.float32
bf16 = jnp.bfloat16

SMEM = pl.BlockSpec(memory_space=pltpu.SMEM)
HBM = pl.BlockSpec(memory_space=pltpu.HBM)
VMEM = pl.BlockSpec(memory_space=pltpu.VMEM)


def nt(a, b):
    return lax.dot_general(a, b, (((1,), (1,)), ((), ())), preferred_element_type=f32)


def low_half(shape):
    return lax.broadcasted_iota(jnp.int32, shape, len(shape) - 1) < 64


def pieces(x):
    first = x.astype(bf16)
    rest = x - first.astype(f32)
    second = rest.astype(bf16)
    third = (rest - second.astype(f32)).astype(bf16)
    return first, second, third


def upward_kernel(
    column_ref, lists_ref, dens_hbm, points_hbm, weights_hbm, basis_hbm, transfer_hbm,
    pack_ref, below_ref, above_ref, own_ref, up_ref, down_ref, coarse_ref,
    dens_ref, points_ref, weights_ref, basis_ref, transfer_ref, both_ref, sems,
):
    copies = [
        pltpu.make_async_copy(source, target, sems.at[i])
        for i, (source, target) in enumerate((
            (dens_hbm, dens_ref), (points_hbm, points_ref), (weights_hbm, weights_ref),
            (basis_hbm, basis_ref), (transfer_hbm, transfer_ref),
        ))
    ]
    for copy in copies:
        copy.start()
    for copy in copies[:3]:
        copy.wait()
    leaves = basis_ref.shape[0]
    rim = REACH * 128
    for part in range(4):
        span = pl.ds(part * 1024, 1024)
        scaled = dens_ref[:, span].astype(f32) * (weights_ref[:, span] * (1.0 / four_pi))
        pack_ref[0:16, span] = scaled.astype(bf16)
        one, two, three = pieces(points_ref[:, span])
        rows = jnp.concatenate(
            [one.astype(f32), two.astype(f32), three.astype(f32), jnp.zeros((7, 1024), f32)], axis=0
        )
        pack_ref[16:32, span] = rows.astype(bf16)
    below_ref[...] = pack_ref[:, -rim:]
    above_ref[...] = pack_ref[:, :rim]

    for copy in copies[3:]:
        copy.wait()
    coarse = []
    for group in range(leaves // 8):
        total = jnp.zeros((16, 64), f32)
        for child in range(8):
            leaf = group * 8 + child
            basis = basis_ref[leaf]
            twice = nt(dens_ref[:, leaf * 128 : (leaf + 1) * 128], jnp.concatenate([basis, basis], axis=0))
            rounded = twice.astype(bf16)
            both_ref[leaf] = rounded
            total += jnp.dot(rounded[:, :64], transfer_ref[leaf], preferred_element_type=f32)
        coarse.append(total)
    for pair in range(len(coarse) // 2):
        tile = jnp.concatenate([coarse[2 * pair], coarse[2 * pair + 1]], axis=1).astype(bf16)
        coarse_ref[:, pair] = jnp.broadcast_to(tile[None], (coarse_ref.shape[0], 16, 128))

    column = column_ref[0]
    mask = low_half((16, 128))

    def fill(target, carry):
        for ref, window in (
            (own_ref, target - column + WINDOW),
            (up_ref, jnp.minimum(target - column + 2 * WINDOW, 2 * WINDOW)),
            (down_ref, jnp.maximum(target - column, 0)),
        ):
            for slot in range(8):
                ref[target, slot] = jnp.where(
                    mask, both_ref[lists_ref[slot, window]], both_ref[lists_ref[slot + 8, window]]
                )
        return carry

    lax.fori_loop(0, ROW, fill, 0)


def upward(column, lists, densities, points, weights, basis, transfer, row_count):
    count = densities.shape[1]
    leaves = basis.shape[0]
    block = jax.ShapeDtypeStruct((ROW, 8, 16, 128), bf16)
    return pl.pallas_call(
        upward_kernel,
        name="upward",
        out_shape=(
            jax.ShapeDtypeStruct((32, count), bf16),
            jax.ShapeDtypeStruct((32, REACH * 128), bf16),
            jax.ShapeDtypeStruct((32, REACH * 128), bf16),
            block, block, block,
            jax.ShapeDtypeStruct((row_count, leaves // 16, 16, 128), bf16),
        ),
        in_specs=[SMEM, SMEM] + [HBM] * 5,
        out_specs=[VMEM] * 7,
        scratch_shapes=[
            pltpu.VMEM(densities.shape, bf16),
            pltpu.VMEM(points.shape, f32),
            pltpu.VMEM(weights.shape, f32),
            pltpu.VMEM(basis.shape, bf16),
            pltpu.VMEM(transfer.shape, bf16),
            pltpu.VMEM((leaves, 16, 128), bf16),
            pltpu.SemaphoreType.DMA((5,)),
        ],
        compiler_params=pltpu.CompilerParams(vmem_limit_bytes=12 << 20),
        cost_estimate=pl.CostEstimate(flops=20_000_000, bytes_accessed=4 << 20, transcendentals=0),
    )(column, lists, *(pltpu.with_memory_space_constraint(x, pltpu.HBM) for x in (densities, points, weights, basis, transfer)))


def near_kernel(
    offsets_ref, pack_ref, below_ref, above_ref, coupling_hbm,
    near_hbm, packed_hbm, near_ref, left_ref, right_ref, wide_ref, buffer_ref, packed_ref, sems, out_sems,
):
    rim = REACH * 128
    inner = pack_ref.shape[1]
    leaves, tiles = coupling_hbm.shape[:2]
    per_step = buffer_ref.shape[1]
    steps = leaves // per_step

    def fetch(step, slot):
        return pltpu.make_async_copy(
            coupling_hbm.at[pl.ds(step * per_step, per_step)], buffer_ref.at[slot], sems.at[slot]
        )

    def flush(step, slot):
        return pltpu.make_async_copy(
            packed_ref.at[slot], packed_hbm.at[pl.ds(step * per_step, per_step)], out_sems.at[slot]
        )

    fetch(0, 0).start()

    def build(source, at, start, width, own):
        wide_ref[:, pl.ds(at, width)] = source[0:16, pl.ds(start, width)]
        rows = source[16:32, pl.ds(start, width)].astype(f32)
        one, two, three = rows[0:3], rows[3:6], rows[6:9]
        whole = (one + two) + three
        square = whole[0:1] * whole[0:1] + whole[1:2] * whole[1:2] + whole[2:3] * whole[2:3]
        ones = jnp.ones((3, width), f32)
        m1, m2, m3 = (p.astype(f32) for p in pieces(square))
        fill = jnp.zeros((8, width), f32)
        right = jnp.concatenate([one, two, one, two, three, one, ones, m1, m2, m3, fill], axis=0)
        right_ref[:, pl.ds(at, width)] = right.astype(bf16)
        if own:
            n1, n2, n3 = (p.astype(f32) for p in pieces(square + core_square))
            left = jnp.concatenate(
                [-2 * one, -2 * one, -2 * two, -2 * two, -2 * one, -2 * three, n1, n2, n3, ones, fill], axis=0
            )
            left_ref[:, pl.ds(start, width)] = left.astype(bf16)

    for part in range(rim // 512):
        build(below_ref, part * 512, part * 512, 512, False)
        build(above_ref, rim + inner + part * 512, part * 512, 512, False)
    for part in range(inner // 512):
        build(pack_ref, rim + part * 512, part * 512, 512, True)

    slots = offsets_ref.shape[0]

    def one_leaf(leaf):
        own = left_ref[:, pl.ds(pl.multiple_of(leaf * 128, 128), 128)]
        total = jnp.zeros((16, 128), f32)
        for slot in range(0, slots, 2):
            spans = [
                pl.ds(pl.multiple_of((leaf + REACH + offsets_ref[s, leaf]) * 128, 128), 128)
                for s in range(slot, min(slot + 2, slots))
            ]
            right = jnp.concatenate([right_ref[:, span] for span in spans], axis=1)
            wide = jnp.concatenate([wide_ref[:, span] for span in spans], axis=1)
            square = lax.dot_general(own, right, (((0,), (0,)), ((), ())), preferred_element_type=f32)
            total += nt(wide, lax.rsqrt(square).astype(bf16))
        near_ref[:, pl.ds(pl.multiple_of(leaf * 128, 128), 128)] = total

    def one_step(step, carry):
        slot = lax.rem(step, 2)
        fetch(step, slot).wait()

        @pl.when(step + 1 < steps)
        def _():
            fetch(step + 1, 1 - slot).start()

        @pl.when(step >= 2)
        def _():
            flush(step - 2, slot).wait()

        for inside in range(per_step):
            leaf = step * per_step + inside
            one_leaf(leaf)
            for tile in range(0, tiles, 2):
                packed_ref[slot, inside, :, tile * 64 : (tile + 2) * 64] = jnp.concatenate(
                    [buffer_ref[slot, inside, tile], buffer_ref[slot, inside, tile + 1]], axis=1
                )
        flush(step, slot).start()
        return carry

    lax.fori_loop(0, steps, one_step, 0)
    last = pltpu.make_async_copy(near_ref, near_hbm, out_sems.at[2])
    last.start()
    for step in range(steps - 2, steps):
        flush(step, step % 2).wait()
    last.wait()


def near_field(offsets, pack, below, above, coupling):
    count = pack.shape[1]
    wide = count + 2 * REACH * 128
    leaves, tiles = coupling.shape[:2]
    per_step = 4
    points = count * offsets.shape[0] * 128
    return pl.pallas_call(
        near_kernel,
        name="near",
        out_shape=(
            pltpu.HBM((16, count), f32),
            pltpu.HBM((leaves, 64, tiles * 64), bf16),
        ),
        in_specs=[SMEM, VMEM, VMEM, VMEM, HBM],
        out_specs=[HBM, HBM],
        scratch_shapes=[
            pltpu.VMEM((16, count), f32),
            pltpu.VMEM((32, count), bf16),
            pltpu.VMEM((32, wide), bf16),
            pltpu.VMEM((16, wide), bf16),
            pltpu.VMEM((2, per_step) + coupling.shape[1:], bf16),
            pltpu.VMEM((2, per_step, 64, tiles * 64), bf16),
            pltpu.SemaphoreType.DMA((2,)),
            pltpu.SemaphoreType.DMA((3,)),
        ],
        compiler_params=pltpu.CompilerParams(vmem_limit_bytes=24 << 20),
        cost_estimate=pl.CostEstimate(flops=points * 96, bytes_accessed=28 << 20, transcendentals=points),
    )(offsets, pack, below, above, pltpu.with_memory_space_constraint(coupling, pltpu.HBM))


def assemble_kernel(column_ref, own_ref, below_ref, above_ref, coarse_ref, out_ref):
    column = column_ref[0]
    rows, pairs = coarse_ref.shape[:2]
    for target in range(out_ref.shape[0]):
        out_ref[target, 0:8] = own_ref[target]
        crossed = jnp.where(target < column, 0, 1)

        @pl.when(crossed == 0)
        def _():
            out_ref[target, 8:16] = below_ref[target]

        @pl.when(crossed == 1)
        def _():
            out_ref[target, 8:16] = above_ref[target]

        out_ref[target, 16:] = coarse_ref[...].reshape(rows * pairs, 16, 128)


def assemble(column, own, below, above, coarse):
    rows, pairs = coarse.shape[:2]
    return pl.pallas_call(
        assemble_kernel,
        name="assemble",
        out_shape=jax.ShapeDtypeStruct((ROW, 16 + rows * pairs, 16, 128), bf16),
        in_specs=[SMEM] + [VMEM] * 4,
        out_specs=VMEM,
        compiler_params=pltpu.CompilerParams(vmem_limit_bytes=8 << 20),
        cost_estimate=pl.CostEstimate(flops=0, bytes_accessed=3 << 20, transcendentals=0),
    )(column, own, below, above, coarse)


def spread_matrix():
    row = lax.broadcasted_iota(jnp.int32, (128, 256), 0)
    col = lax.broadcasted_iota(jnp.int32, (128, 256), 1)
    hit = ((row // 64) == (col // 128)) & ((row % 64) == (col % 64))
    return jnp.where(hit, 1.0, 0.0).astype(bf16)


def paired(slots, pick):
    mask = low_half((16, 128))
    return jnp.concatenate([jnp.where(mask, pick(s), pick(s + 1)) for s in range(0, slots, 2)], axis=1)


def finish_kernel(
    column_ref, leaf_refs, group_refs, swapped_ref, below_ref, above_ref,
    coupling_hbm, transfer_hbm, basis_hbm, near_hbm, packed_hbm,
    out_ref, coupling_ref, transfer_ref, basis_ref, near_ref, packed_ref, table_ref, picked_ref, local1_ref, sems,
):
    copies = [
        pltpu.make_async_copy(source, target, sems.at[i])
        for i, (source, target) in enumerate((
            (coupling_hbm, coupling_ref), (transfer_hbm, transfer_ref), (basis_hbm, basis_ref),
            (near_hbm, near_ref), (packed_hbm, packed_ref),
        ))
    ]
    for copy in copies:
        copy.start()
    groups, slots = coupling_ref.shape[:2]
    mask = low_half((16, 128))
    column = column_ref[0]
    spread = spread_matrix()

    def put(window, tiles):
        out = jnp.dot(tiles.reshape(8 * 16, 128), spread, preferred_element_type=f32).astype(bf16)
        out = out.reshape(8, 16, 256)
        table_ref[pl.ds(window * 16, 8)] = out[:, :, :128]
        table_ref[pl.ds(window * 16 + 8, 8)] = out[:, :, 128:]

    put(0, below_ref[column])
    put(2 * WINDOW, above_ref[column])
    for window in range(1, 2 * WINDOW):
        place = column + window
        owner = place & (ROW - 1)
        crossed = jnp.where((place >= ROW) & (place < 2 * ROW), 0, 8)
        put(window, swapped_ref[owner, pl.ds(pl.multiple_of(crossed, 8), 8)])

    for group in range(groups):
        for slot in range(slots):
            ref = group_refs[group, slot]
            tile = swapped_ref[(ref >> 2) & (ROW - 1), 16 + ((ref >> 5) << 1) + ((ref >> 1) & 1)]
            keep = mask == ((ref & 1) == 0)
            picked_ref[group * slots + slot] = jnp.where(keep, tile, jnp.zeros_like(tile))
    row = lax.broadcasted_iota(jnp.int32, (128, 128), 0)
    col = lax.broadcasted_iota(jnp.int32, (128, 128), 1)
    fold = jnp.where((row % 64) == (col % 64), 1.0, 0.0).astype(bf16)
    copies[0].wait()
    for group in range(groups):
        tiles = picked_ref[pl.ds(group * slots, slots)].reshape(slots * 16, 128)
        both = jnp.dot(tiles, fold, preferred_element_type=f32).astype(bf16).reshape(slots, 16, 128)
        wide = jnp.concatenate([coupling_ref[group, s] for s in range(slots)], axis=1)
        local1_ref[group] = nt(paired(slots, lambda s: both[s]), wide).astype(bf16)

    for copy in copies[1:]:
        copy.wait()

    def one_group(group, carry):
        for child in range(8):
            leaf = group * 8 + child
            field = nt(paired(slots, lambda s: table_ref[leaf_refs[leaf, s]]), packed_ref[leaf])
            field = (field + nt(local1_ref[group], transfer_ref[leaf])).astype(bf16)
            span = pl.ds(pl.multiple_of(leaf * 128, 128), 128)
            out_ref[:, span] = near_ref[:, span] + jnp.dot(field, basis_ref[leaf], preferred_element_type=f32)
        return carry

    lax.fori_loop(0, groups, one_group, 0)


def finish(column, leaf_refs, group_refs, swapped, below, above, packed, coupling, transfer, basis, near):
    groups, slots = coupling.shape[:2]
    return pl.pallas_call(
        finish_kernel,
        name="finish",
        out_shape=jax.ShapeDtypeStruct(near.shape, f32),
        in_specs=[SMEM] * 3 + [VMEM] * 3 + [HBM] * 5,
        out_specs=VMEM,
        scratch_shapes=[
            pltpu.VMEM(coupling.shape, bf16),
            pltpu.VMEM(transfer.shape, bf16),
            pltpu.VMEM(basis.shape, bf16),
            pltpu.VMEM(near.shape, f32),
            pltpu.VMEM(packed.shape, bf16),
            pltpu.VMEM(((2 * WINDOW + 1) * 16, 16, 128), bf16),
            pltpu.VMEM((groups * slots, 16, 128), bf16),
            pltpu.VMEM((groups, 16, 64), bf16),
            pltpu.SemaphoreType.DMA((5,)),
        ],
        compiler_params=pltpu.CompilerParams(vmem_limit_bytes=24 << 20),
        cost_estimate=pl.CostEstimate(flops=200_000_000, bytes_accessed=14 << 20, transcendentals=0),
    )(
        column, leaf_refs, group_refs, swapped, below, above,
        *(pltpu.with_memory_space_constraint(x, pltpu.HBM) for x in (coupling, transfer, basis, near, packed)),
    )


def shifted(shard, by, devices):
    return lax.ppermute(shard, AXES, [(i, i + by) for i in range(devices) if 0 <= i + by < devices])


def local(
    densities, points, weights, near_offsets, leaf_basis, transfer, send_lists, relay_refs, leaf_coupling,
    coarse_refs, coarse_coupling,
):
    devices = lax.axis_size(AXES)
    column = lax.rem(lax.axis_index("gy").astype(jnp.int32), ROW).reshape(1)
    rows = [[row * ROW + i for i in range(ROW)] for row in range(devices // ROW)]
    columns = [[col + ROW * i for i in range(devices // ROW)] for col in range(ROW)]
    pack, rim_last, rim_first, own, up, down, coarse = upward(
        column, send_lists[0].T, densities, points, weights[None, :], leaf_basis, transfer, devices // ROW
    )
    coarse_rows = lax.all_to_all(coarse, AXES, 0, 0, axis_index_groups=columns, tiled=True)
    lists_below = shifted(up, ROW, devices)
    lists_above = shifted(down, -ROW, devices)
    from_below = shifted(rim_last, 1, devices)
    from_above = shifted(rim_first, -1, devices)
    payload = assemble(column, own, lists_below, lists_above, coarse_rows)
    payload, from_below, from_above = lax.optimization_barrier((payload, from_below, from_above))
    swapped = lax.all_to_all(payload, AXES, 0, 0, axis_index_groups=rows, tiled=True)
    near, packed = near_field(near_offsets.T, pack, from_below, from_above, leaf_coupling)
    return finish(
        column, relay_refs, coarse_refs, swapped, lists_below, lists_above, packed, coarse_coupling, transfer,
        leaf_basis, near,
    )


def solution(mesh):
    in_specs = (
        P(None, AXES),
        P(None, AXES),
        P(AXES),
        P(AXES, None),
        P(AXES, None, None),
        P(AXES, None, None),
        P(AXES, None, None),
        P(AXES, None),
        P(AXES, None, None, None),
        P(AXES, None),
        P(AXES, None, None, None),
    )
    return jax.shard_map(local, mesh=mesh, in_specs=in_specs, out_specs=P(None, AXES), check_vma=False)
```

time: 115 us -> 74 us (0.64)
  the two profiles are of different devices: /device:TPU:4 before, /device:TPU:1 now
where the time goes in v2:
time: 74 us; the launch traced here: 73.2 us
  Pallas kernels  39.2 us (53%)
  starting transfers between devices  26.8 us (36%)
  waiting for transfers between devices  6.42 us (9%)
    pallas_call x1, Pallas kernels, near_field(): pl.pallas_call(near_kernel, name='near', out_shape=(pltpu.HBM((16, count)...  16.6 us
    pallas_call x1, Pallas kernels, finish(): pl.pallas_call(finish_kernel, name='finish', out_shape=jax.ShapeDtypeStru...  15.9 us
    ppermute x4, starting transfers between devices, shifted(): lax.ppermute(shard, AXES, [(i, i + by) for i in range(devices) if 0 <= i...  12.2 us
    all_to_all x1, starting transfers between devices, local(): lax.all_to_all(coarse, AXES, 0, 0, axis_index_groups=columns, tiled=True)  8.04 us
    all_to_all x1, starting transfers between devices, local(): lax.all_to_all(payload, AXES, 0, 0, axis_index_groups=rows, tiled=True)  6.51 us
    pallas_call x1, Pallas kernels, upward(): pl.pallas_call(upward_kernel, name='upward', out_shape=(jax.ShapeDtypeStr...  5.43 us
    all_to_all x1, waiting for transfers between devices, local(): lax.all_to_all(payload, AXES, 0, 0, axis_index_groups=rows, tiled=True)  4.08 us
    ppermute x4, waiting for transfers between devices, shifted(): lax.ppermute(shard, AXES, [(i, i + by) for i in range(devices) if 0 <= i...  2.18 us
  transfers between devices with their start and end apart: 6, of which 3 were waited for; matrix products, arithmetic and copies ran while one was open for 0% of the time, Pallas kernels for 24%

profile of v2, /device:TPU:1, one launch (start us, length us, event | category | flops | bytes accessed | tf_op | source)
XLA Modules:
  0.0 73.2 jit_solution(7486980758516057600)
XLA Ops:
  0.0 0.0 copy-start.1
  0.0 0.7 copy-done.1
  0.7 5.4 %upward.1 = (bf16[32,4096]{1,0:T(8,128)(2,1)S(1)}, bf16[32,1024]{1,0:T(8,128)(2,1)S(1)}, bf16[32,1024]{1,0:T(8,128)(2,1)S(1)}, bf16[8,8,16,128]{3,2,1,0:T(8,128)...) custom-call(s32[1]{0:T(128)} %bitcast.column_ref, ...), custom_call_target="tpu_custom_call" | custom-call | flops 20000000 | bytes 4194304 | tf_op jit(solution)/shard_map/upward/pallas_call | solution.py:110
  6.1 4.4 %collective-permute-start = (bf16[8,8,16,128]{3,2,1,0:T(8,128)(2,1)S(1)}, bf16[8,8,16,128]{3,2,1,0:T(8,128)(2,1)S(1)}, u32[]{:S(2)}, u32[]{:S(2)}) collective-permute-start(bf16[8,8,16,128]{3,2,1,0:T(8,128)(2,1)S(1)} %get-tuple-element.18), channel_id=1, source_target_pairs={{0,8},{1,9},{2,10},{3,11},{4,12},{5,13},{6,14},{7,15},{8,16},{9,17... | collective-permute-start | bytes 786440 | tf_op jit(solution)/shard_map/ppermute | solution.py:393
  10.5 1.3 %collective-permute-start.1 = (bf16[8,8,16,128]{3,2,1,0:T(8,128)(2,1)S(1)}, bf16[8,8,16,128]{3,2,1,0:T(8,128)(2,1)S(1)}, u32[]{:S(2)}, u32[]{:S(2)}) collective-permute-start(bf16[8,8,16,128]{3,2,1,0:T(8,128)(2,1)S(1)} %get-tuple-element.19), channel_id=1, source_target_pairs={{8,0},{9,1},{10,2},{11,3},{12,4},{13,5},{14,6},{15,7},{16,8},{17,9... | collective-permute-start | bytes 786440 | tf_op jit(solution)/shard_map/ppermute | solution.py:393
  11.8 8.0 %all-to-all-start = ((bf16[16,2,16,128]{3,2,1,0:T(8,128)(2,1)}), bf16[16,2,16,128]{3,2,1,0:T(8,128)(2,1)S(1)}, u32[]{:S(2)}, u32[]{:S(2)}) async-start(bf16[16,2,16,128]{3,2,1,0:T(8,128)(2,1)} %get-tuple-element.20), calls=%async_computation | async-start | bytes 262144 | tf_op jit(solution)/shard_map/all_to_all | solution.py:407
  19.9 4.6 %collective-permute-start.2 = (bf16[32,1024]{1,0:T(8,128)(2,1)S(1)}, bf16[32,1024]{1,0:T(8,128)(2,1)S(1)}, u32[]{:S(2)}, u32[]{:S(2)}) collective-permute-start(bf16[32,1024]{1,0:T(8,128)(2,1)S(1)} %get-tuple-element.21), channel_id=1, source_target_pairs={{0,1},{1,2},{2,3},{3,4},{4,5},{5,6},{6,7},{7,8},{8,9},{9,10},{10,1... | collective-permute-start | bytes 196616 | tf_op jit(solution)/shard_map/ppermute | solution.py:393
  24.5 1.9 %collective-permute-start.3 = (bf16[32,1024]{1,0:T(8,128)(2,1)S(1)}, bf16[32,1024]{1,0:T(8,128)(2,1)S(1)}, u32[]{:S(2)}, u32[]{:S(2)}) collective-permute-start(bf16[32,1024]{1,0:T(8,128)(2,1)S(1)} %get-tuple-element.22), channel_id=1, source_target_pairs={{1,0},{2,1},{3,2},{4,3},{5,4},{6,5},{7,6},{8,7},{9,8},{10,9},{11,1... | collective-permute-start | bytes 196616 | tf_op jit(solution)/shard_map/ppermute | solution.py:393
  26.4 0.2 all-to-all-done.coarse_ref
  26.6 0.0 collective-permute-done.below_ref
  26.6 0.0 collective-permute-done.1.above_ref
  26.6 1.3 %assemble.1 = bf16[8,48,16,128]{3,2,1,0:T(8,128)(2,1)} custom-call(s32[1]{0:T(128)} %bitcast.column_ref, bf16[8,8,16,128]{3,2,1,0:T(8,128)(2,1)S(1)} %get-tuple-element.17.own_ref, bf16[8,8,16,128]{3,2,1,0:T(8,128)(2,1)S(1)} %collective-permute-done.below_ref, bf16[8,8,16,128]{3,2,1,0:T(8,128)(2,1)S(1)} %collective-permute-done.1.above_ref, ...), custom_call_target="tpu_custom_call" | custom-call | bytes 3145728 | tf_op jit(solution)/shard_map/assemble/pallas_call | solution.py:278
  27.9 0.0 copy-start.2
  27.9 0.0 collective-permute-done.2.below_ref
  27.9 2.2 %collective-permute-done.3.above_ref = bf16[32,1024]{1,0:T(8,128)(2,1)S(1)} collective-permute-done((bf16[32,1024]{1,0:T(8,128)(2,1)S(1)}, bf16[32,1024]{1,0:T(8,128)(2,1)S(1)}, u32[]{:S(2)}, u32[]{:S(2)}) %collective-permute-start.3) | collective-permute-done | bytes 65568 | tf_op jit(solution)/shard_map/ppermute | solution.py:393
  30.1 6.5 %all-to-all-start.1 = ((bf16[8,48,16,128]{3,2,1,0:T(8,128)(2,1)}), bf16[8,48,16,128]{3,2,1,0:T(8,128)(2,1)S(1)}, u32[]{:S(2)}, u32[]{:S(2)}) async-start(bf16[8,48,16,128]{3,2,1,0:T(8,128)(2,1)} %assemble.1), calls=%async_computation.1 | async-start | bytes 3145728 | tf_op jit(solution)/shard_map/all_to_all | solution.py:414
  36.6 0.0 copy-done.2
  36.6 0.0 copy-start
  36.6 0.0 copy-start.3
  36.6 16.6 %near.1 = (f32[16,4096]{1,0:T(8,128)}, bf16[32,64,2048]{2,1,0:T(8,128)(2,1)}) custom-call(s32[13,32]{1,0:T(8,128)S(1)} %bitcast.7, bf16[32,4096]{1,0:T(8,128)(2,1)S(1)} %get-tuple-element.24.pack_ref, bf16[32,1024]{1,0:T(8,128)(2,1)S(1)} %collective-permute-done.2.below_ref, bf16[32,1024]{1,0:T(8,128)(2,1)S(1)} %collective-permute-done.3.above_ref, ...), custom_call_target="tpu_custom_call" | custom-call | flops 654311424 | bytes 29360128 | tf_op jit(solution)/shard_map/near/pallas_call | solution.py:234
  53.2 4.1 %all-to-all-done.1.swapped_ref = bf16[8,48,16,128]{3,2,1,0:T(8,128)(2,1)S(1)} async-done(((bf16[8,48,16,128]{3,2,1,0:T(8,128)(2,1)}), bf16[8,48,16,128]{3,2,1,0:T(8,128)(2,1)S(1)}, u32[]{:S(2)}, u32[]{:S(2)}) %all-to-all-start.1) | async-done | bytes 1572896 | tf_op jit(solution)/shard_map/all_to_all | solution.py:414
  57.3 0.0 copy-done
  57.3 0.0 copy-done.3
  57.3 15.9 %finish.1 = f32[16,4096]{1,0:T(8,128)} custom-call(s32[1]{0:T(128)} %bitcast.column_ref, s32[32,32]{1,0:T(8,128)S(1)} %copy-done, s32[4,32]{1,0:T(4,128)S(1)} %copy-done.3, bf16[8,48,16,128]{3,2,1,0:T(8,128)(2,1)S(1)} %all-to-all-done.1.swapped_ref, bf16[8,8,16,128]{3,2,1,0:T(8,128)(2,1)S(1)} %collective-permute-done.below_ref, ...), custom_call_target="tpu_custom_call" | custom-call | flops 200000000 | bytes 14680064 | tf_op jit(solution)/shard_map/finish/pallas_call | solution.py:367
Async XLA Ops:
  0.0 0.7 copy-start.1
  6.1 20.4 %collective-permute-start = (bf16[8,8,16,128]{3,2,1,0:T(8,128)(2,1)S(1)}, bf16[8,8,16,128]{3,2,1,0:T(8,128)(2,1)S(1)}, u32[]{:S(2)}, u32[]{:S(2)}) collective-permute-start(bf16[8,8,16,128]{3,2,1,0:T(8,128)(2,1)S(1)} %get-tuple-element.18), channel_id=1, source_target_pairs={{0,8},{1,9},{2,10},{3,11},{4,12},{5,13},{6,14},{7,15},{8,16},{9,17... | collective-permute-start | bytes 786440 | tf_op jit(solution)/shard_map/ppermute | solution.py:393
  10.5 16.0 %collective-permute-start.1 = (bf16[8,8,16,128]{3,2,1,0:T(8,128)(2,1)S(1)}, bf16[8,8,16,128]{3,2,1,0:T(8,128)(2,1)S(1)}, u32[]{:S(2)}, u32[]{:S(2)}) collective-permute-start(bf16[8,8,16,128]{3,2,1,0:T(8,128)(2,1)S(1)} %get-tuple-element.19), channel_id=1, source_target_pairs={{8,0},{9,1},{10,2},{11,3},{12,4},{13,5},{14,6},{15,7},{16,8},{17,9... | collective-permute-start | bytes 786440 | tf_op jit(solution)/shard_map/ppermute | solution.py:393
  11.8 14.7 %all-to-all-start = ((bf16[16,2,16,128]{3,2,1,0:T(8,128)(2,1)}), bf16[16,2,16,128]{3,2,1,0:T(8,128)(2,1)S(1)}, u32[]{:S(2)}, u32[]{:S(2)}) async-start(bf16[16,2,16,128]{3,2,1,0:T(8,128)(2,1)} %get-tuple-element.20), calls=%async_computation | async-start | bytes 262144 | tf_op jit(solution)/shard_map/all_to_all | solution.py:407
  19.9 8.0 %collective-permute-start.2 = (bf16[32,1024]{1,0:T(8,128)(2,1)S(1)}, bf16[32,1024]{1,0:T(8,128)(2,1)S(1)}, u32[]{:S(2)}, u32[]{:S(2)}) collective-permute-start(bf16[32,1024]{1,0:T(8,128)(2,1)S(1)} %get-tuple-element.21), channel_id=1, source_target_pairs={{0,1},{1,2},{2,3},{3,4},{4,5},{5,6},{6,7},{7,8},{8,9},{9,10},{10,1... | collective-permute-start | bytes 196616 | tf_op jit(solution)/shard_map/ppermute | solution.py:393
  24.5 5.6 %collective-permute-start.3 = (bf16[32,1024]{1,0:T(8,128)(2,1)S(1)}, bf16[32,1024]{1,0:T(8,128)(2,1)S(1)}, u32[]{:S(2)}, u32[]{:S(2)}) collective-permute-start(bf16[32,1024]{1,0:T(8,128)(2,1)S(1)} %get-tuple-element.22), channel_id=1, source_target_pairs={{1,0},{2,1},{3,2},{4,3},{5,4},{6,5},{7,6},{8,7},{9,8},{10,9},{11,1... | collective-permute-start | bytes 196616 | tf_op jit(solution)/shard_map/ppermute | solution.py:393
  27.9 8.7 %copy-start.2 = (s32[32,13]{0,1:T(8,128)S(1)}, s32[32,13]{0,1:T(8,128)}, u32[]{:S(2)}) copy-start(s32[32,13]{0,1:T(8,128)} %param.14) | copy-start | bytes 4996
  30.1 27.2 %all-to-all-start.1 = ((bf16[8,48,16,128]{3,2,1,0:T(8,128)(2,1)}), bf16[8,48,16,128]{3,2,1,0:T(8,128)(2,1)S(1)}, u32[]{:S(2)}, u32[]{:S(2)}) async-start(bf16[8,48,16,128]{3,2,1,0:T(8,128)(2,1)} %assemble.1), calls=%async_computation.1 | async-start | bytes 3145728 | tf_op jit(solution)/shard_map/all_to_all | solution.py:414
  36.6 20.7 %copy-start = (s32[32,32]{1,0:T(8,128)S(1)}, s32[32,32]{1,0:T(8,128)}, u32[]{:S(2)}) copy-start(s32[32,32]{1,0:T(8,128)} %leaf_refs.1) | copy-start | bytes 12292
  36.6 20.7 %copy-start.3 = (s32[4,32]{1,0:T(4,128)S(1)}, s32[4,32]{1,0:T(4,128)}, u32[]{:S(2)}) copy-start(s32[4,32]{1,0:T(4,128)} %group_refs.1) | copy-start | bytes 1540

commit v3 on v2

--- a/solution.py
+++ b/solution.py
@@ -11,6 +11,7 @@
 AXES = ("gx", "gy")
 REACH = 8
 WINDOW = 8
+DEPTH = 2
 ROW = 8
 core_square = 0.0004
 four_pi = 4.0 * math.pi
@@ -72,12 +73,13 @@
         copy.wait()
     coarse = []
     for group in range(leaves // 8):
+        members = range(group * 8, group * 8 + 8)
+        twice = [
+            nt(dens_ref[:, leaf * 128 : (leaf + 1) * 128], jnp.concatenate([basis_ref[leaf]] * 2, axis=0)).astype(bf16)
+            for leaf in members
+        ]
         total = jnp.zeros((16, 64), f32)
-        for child in range(8):
-            leaf = group * 8 + child
-            basis = basis_ref[leaf]
-            twice = nt(dens_ref[:, leaf * 128 : (leaf + 1) * 128], jnp.concatenate([basis, basis], axis=0))
-            rounded = twice.astype(bf16)
+        for leaf, rounded in zip(members, twice):
             both_ref[leaf] = rounded
             total += jnp.dot(rounded[:, :64], transfer_ref[leaf], preferred_element_type=f32)
         coarse.append(total)
@@ -134,26 +136,33 @@
 
 
 def near_kernel(
-    offsets_ref, pack_ref, below_ref, above_ref, coupling_hbm,
-    near_hbm, packed_hbm, near_ref, left_ref, right_ref, wide_ref, buffer_ref, packed_ref, sems, out_sems,
+    first, leaves, offsets_ref, pack_ref, below_ref, above_ref, coupling_hbm,
+    near_hbm, packed_hbm, near_ref, left_ref, right_ref, wide_ref, buffer_ref, packed_ref, sems, out_sems, last_sem,
 ):
     rim = REACH * 128
     inner = pack_ref.shape[1]
-    leaves, tiles = coupling_hbm.shape[:2]
+    tiles = coupling_hbm.shape[1]
     per_step = buffer_ref.shape[1]
     steps = leaves // per_step
 
     def fetch(step, slot):
-        return pltpu.make_async_copy(
-            coupling_hbm.at[pl.ds(step * per_step, per_step)], buffer_ref.at[slot], sems.at[slot]
-        )
+        return [
+            pltpu.make_async_copy(
+                coupling_hbm.at[first + step * per_step + i], buffer_ref.at[slot, i], sems.at[slot, i]
+            )
+            for i in range(per_step)
+        ]
 
     def flush(step, slot):
-        return pltpu.make_async_copy(
-            packed_ref.at[slot], packed_hbm.at[pl.ds(step * per_step, per_step)], out_sems.at[slot]
-        )
-
-    fetch(0, 0).start()
+        return [
+            pltpu.make_async_copy(
+                packed_ref.at[slot, i], packed_hbm.at[step * per_step + i], out_sems.at[slot, i]
+            )
+            for i in range(per_step)
+        ]
+
+    for copy in fetch(0, 0):
+        copy.start()
 
     def build(source, at, start, width, own):
         wide_ref[:, pl.ds(at, width)] = source[0:16, pl.ds(start, width)]
@@ -181,83 +190,93 @@
 
     slots = offsets_ref.shape[0]
 
-    def one_leaf(leaf):
+    def squares(leaf, slot):
         own = left_ref[:, pl.ds(pl.multiple_of(leaf * 128, 128), 128)]
-        total = jnp.zeros((16, 128), f32)
-        for slot in range(0, slots, 2):
-            spans = [
-                pl.ds(pl.multiple_of((leaf + REACH + offsets_ref[s, leaf]) * 128, 128), 128)
-                for s in range(slot, min(slot + 2, slots))
-            ]
-            right = jnp.concatenate([right_ref[:, span] for span in spans], axis=1)
-            wide = jnp.concatenate([wide_ref[:, span] for span in spans], axis=1)
-            square = lax.dot_general(own, right, (((0,), (0,)), ((), ())), preferred_element_type=f32)
-            total += nt(wide, lax.rsqrt(square).astype(bf16))
-        near_ref[:, pl.ds(pl.multiple_of(leaf * 128, 128), 128)] = total
+        spans = [
+            pl.ds(pl.multiple_of((leaf + REACH + offsets_ref[s, leaf]) * 128, 128), 128)
+            for s in range(slot, min(slot + 2, slots))
+        ]
+        right = jnp.concatenate([right_ref[:, span] for span in spans], axis=1)
+        wide = jnp.concatenate([wide_ref[:, span] for span in spans], axis=1)
+        return wide, lax.dot_general(own, right, (((0,), (0,)), ((), ())), preferred_element_type=f32)
 
     def one_step(step, carry):
         slot = lax.rem(step, 2)
-        fetch(step, slot).wait()
+        for copy in fetch(step, slot):
+            copy.wait()
 
         @pl.when(step + 1 < steps)
         def _():
-            fetch(step + 1, 1 - slot).start()
+            for copy in fetch(step + 1, 1 - slot):
+                copy.start()
 
         @pl.when(step >= 2)
         def _():
-            flush(step - 2, slot).wait()
-
-        for inside in range(per_step):
+            for copy in flush(step - 2, slot):
+                copy.wait()
+
+        work = [(inside, s) for inside in range(per_step) for s in range(0, slots, 2)]
+        totals = [jnp.zeros((16, 128), f32)] * per_step
+        ahead = [squares(first + step * per_step + inside, s) for inside, s in work[:DEPTH]]
+        for at, (inside, s) in enumerate(work):
             leaf = step * per_step + inside
-            one_leaf(leaf)
-            for tile in range(0, tiles, 2):
+            if at + DEPTH < len(work):
+                later, other = work[at + DEPTH]
+                ahead.append(squares(first + step * per_step + later, other))
+            wide, square = ahead.pop(0)
+            totals[inside] += nt(wide, lax.rsqrt(square).astype(bf16))
+            for tile in range(s * 2, min(s * 2 + 4, tiles), 2) if s < slots - 1 else range(s * 2, tiles, 2):
                 packed_ref[slot, inside, :, tile * 64 : (tile + 2) * 64] = jnp.concatenate(
                     [buffer_ref[slot, inside, tile], buffer_ref[slot, inside, tile + 1]], axis=1
                 )
-        flush(step, slot).start()
+            if s + 2 >= slots:
+                near_ref[:, pl.ds(pl.multiple_of(leaf * 128, 128), 128)] = totals[inside]
+        for copy in flush(step, slot):
+            copy.start()
         return carry
 
     lax.fori_loop(0, steps, one_step, 0)
-    last = pltpu.make_async_copy(near_ref, near_hbm, out_sems.at[2])
+    last = pltpu.make_async_copy(near_ref, near_hbm, last_sem)
     last.start()
     for step in range(steps - 2, steps):
-        flush(step, step % 2).wait()
+        for copy in flush(step, step % 2):
+            copy.wait()
     last.wait()
 
 
-def near_field(offsets, pack, below, above, coupling):
+def near_field(offsets, pack, below, above, coupling, first, leaves):
     count = pack.shape[1]
     wide = count + 2 * REACH * 128
-    leaves, tiles = coupling.shape[:2]
+    tiles = coupling.shape[1]
     per_step = 4
-    points = count * offsets.shape[0] * 128
+    points = leaves * 128 * offsets.shape[0] * 128
     return pl.pallas_call(
-        near_kernel,
+        functools.partial(near_kernel, first, leaves),
         name="near",
         out_shape=(
-            pltpu.HBM((16, count), f32),
+            pltpu.HBM((16, leaves * 128), f32),
             pltpu.HBM((leaves, 64, tiles * 64), bf16),
         ),
         in_specs=[SMEM, VMEM, VMEM, VMEM, HBM],
         out_specs=[HBM, HBM],
         scratch_shapes=[
-            pltpu.VMEM((16, count), f32),
+            pltpu.VMEM((16, leaves * 128), f32),
             pltpu.VMEM((32, count), bf16),
             pltpu.VMEM((32, wide), bf16),
             pltpu.VMEM((16, wide), bf16),
             pltpu.VMEM((2, per_step) + coupling.shape[1:], bf16),
             pltpu.VMEM((2, per_step, 64, tiles * 64), bf16),
-            pltpu.SemaphoreType.DMA((2,)),
-            pltpu.SemaphoreType.DMA((3,)),
+            pltpu.SemaphoreType.DMA((2, per_step)),
+            pltpu.SemaphoreType.DMA((2, per_step)),
+            pltpu.SemaphoreType.DMA,
         ],
         compiler_params=pltpu.CompilerParams(vmem_limit_bytes=24 << 20),
-        cost_estimate=pl.CostEstimate(flops=points * 96, bytes_accessed=28 << 20, transcendentals=points),
+        cost_estimate=pl.CostEstimate(flops=points * 96, bytes_accessed=14 << 20, transcendentals=points),
     )(offsets, pack, below, above, pltpu.with_memory_space_constraint(coupling, pltpu.HBM))
 
 
-def assemble_kernel(column_ref, own_ref, below_ref, above_ref, coarse_ref, out_ref):
+def assemble_kernel(column_ref, own_ref, below_ref, above_ref, out_ref):
     column = column_ref[0]
-    rows, pairs = coarse_ref.shape[:2]
     for target in range(out_ref.shape[0]):
         out_ref[target, 0:8] = own_ref[target]
         crossed = jnp.where(target < column, 0, 1)
@@ -270,20 +289,17 @@
         def _():
             out_ref[target, 8:16] = above_ref[target]
 
-        out_ref[target, 16:] = coarse_ref[...].reshape(rows * pairs, 16, 128)
-
-
-def assemble(column, own, below, above, coarse):
-    rows, pairs = coarse.shape[:2]
+
+def assemble(column, own, below, above):
     return pl.pallas_call(
         assemble_kernel,
         name="assemble",
-        out_shape=jax.ShapeDtypeStruct((ROW, 16 + rows * pairs, 16, 128), bf16),
-        in_specs=[SMEM] + [VMEM] * 4,
+        out_shape=jax.ShapeDtypeStruct((ROW, 16, 16, 128), bf16),
+        in_specs=[SMEM] + [VMEM] * 3,
         out_specs=VMEM,
         compiler_params=pltpu.CompilerParams(vmem_limit_bytes=8 << 20),
-        cost_estimate=pl.CostEstimate(flops=0, bytes_accessed=3 << 20, transcendentals=0),
-    )(column, own, below, above, coarse)
+        cost_estimate=pl.CostEstimate(flops=0, bytes_accessed=1 << 20, transcendentals=0),
+    )(column, own, below, above)
 
 
 def spread_matrix():
@@ -298,22 +314,23 @@
     return jnp.concatenate([jnp.where(mask, pick(s), pick(s + 1)) for s in range(0, slots, 2)], axis=1)
 
 
-def finish_kernel(
-    column_ref, leaf_refs, group_refs, swapped_ref, below_ref, above_ref,
-    coupling_hbm, transfer_hbm, basis_hbm, near_hbm, packed_hbm,
-    out_ref, coupling_ref, transfer_ref, basis_ref, near_ref, packed_ref, table_ref, picked_ref, local1_ref, sems,
+def leaf_kernel(
+    column_ref, leaf_refs, swapped_ref, below_ref, above_ref, one_hbm, two_hbm, out_ref, packed_ref, table_ref, sems,
 ):
-    copies = [
-        pltpu.make_async_copy(source, target, sems.at[i])
-        for i, (source, target) in enumerate((
-            (coupling_hbm, coupling_ref), (transfer_hbm, transfer_ref), (basis_hbm, basis_ref),
-            (near_hbm, near_ref), (packed_hbm, packed_ref),
-        ))
-    ]
+    leaves, slots = leaf_refs.shape
+    half = leaves // 2
+    chunks = sems.shape[0]
+    size = leaves // chunks
+    copies = []
+    for chunk in range(chunks):
+        source, start = (one_hbm, chunk * size) if chunk * size < half else (two_hbm, chunk * size - half)
+        copies.append(
+            pltpu.make_async_copy(
+                source.at[pl.ds(start, size)], packed_ref.at[pl.ds(chunk * size, size)], sems.at[chunk]
+            )
+        )
     for copy in copies:
         copy.start()
-    groups, slots = coupling_ref.shape[:2]
-    mask = low_half((16, 128))
     column = column_ref[0]
     spread = spread_matrix()
 
@@ -330,62 +347,102 @@
         owner = place & (ROW - 1)
         crossed = jnp.where((place >= ROW) & (place < 2 * ROW), 0, 8)
         put(window, swapped_ref[owner, pl.ds(pl.multiple_of(crossed, 8), 8)])
-
+    for chunk in range(chunks):
+        copies[chunk].wait()
+        for leaf in range(chunk * size, (chunk + 1) * size):
+            out_ref[leaf] = nt(paired(slots, lambda s: table_ref[leaf_refs[leaf, s]]), packed_ref[leaf])
+
+
+def leaf_local(column, leaf_refs, swapped, below, above, one, two):
+    leaves, slots = leaf_refs.shape
+    return pl.pallas_call(
+        leaf_kernel,
+        name="leaf_local",
+        out_shape=jax.ShapeDtypeStruct((leaves, 16, 64), f32),
+        in_specs=[SMEM] * 2 + [VMEM] * 3 + [HBM] * 2,
+        out_specs=VMEM,
+        scratch_shapes=[
+            pltpu.VMEM((leaves,) + one.shape[1:], bf16),
+            pltpu.VMEM(((2 * WINDOW + 1) * 16, 16, 128), bf16),
+            pltpu.SemaphoreType.DMA((8,)),
+        ],
+        compiler_params=pltpu.CompilerParams(vmem_limit_bytes=16 << 20),
+        cost_estimate=pl.CostEstimate(flops=140_000_000, bytes_accessed=9 << 20, transcendentals=0),
+    )(column, leaf_refs, swapped, below, above, *(pltpu.with_memory_space_constraint(x, pltpu.HBM) for x in (one, two)))
+
+
+def downward_kernel(
+    group_refs, coarse_ref, local_ref, coupling_hbm, transfer_hbm, basis_hbm, one_hbm, two_hbm,
+    out_ref, coupling_ref, transfer_ref, basis_ref, near_ref, picked_ref, sems,
+):
+    groups, slots = coupling_ref.shape[:2]
+    half = near_ref.shape[1] // 2
+    copies = [
+        pltpu.make_async_copy(source, target, sems.at[i])
+        for i, (source, target) in enumerate((
+            (coupling_hbm, coupling_ref), (transfer_hbm, transfer_ref), (basis_hbm, basis_ref),
+            (one_hbm, near_ref.at[:, :half]), (two_hbm, near_ref.at[:, half:]),
+        ))
+    ]
+    for copy in copies:
+        copy.start()
+    mask = low_half((16, 128))
     for group in range(groups):
         for slot in range(slots):
             ref = group_refs[group, slot]
-            tile = swapped_ref[(ref >> 2) & (ROW - 1), 16 + ((ref >> 5) << 1) + ((ref >> 1) & 1)]
+            tile = coarse_ref[ref >> 2, (ref >> 1) & 1]
             keep = mask == ((ref & 1) == 0)
             picked_ref[group * slots + slot] = jnp.where(keep, tile, jnp.zeros_like(tile))
     row = lax.broadcasted_iota(jnp.int32, (128, 128), 0)
     col = lax.broadcasted_iota(jnp.int32, (128, 128), 1)
     fold = jnp.where((row % 64) == (col % 64), 1.0, 0.0).astype(bf16)
+    both = [
+        jnp.dot(
+            picked_ref[pl.ds(group * slots, slots)].reshape(slots * 16, 128), fold, preferred_element_type=f32
+        ).astype(bf16).reshape(slots, 16, 128)
+        for group in range(groups)
+    ]
     copies[0].wait()
-    for group in range(groups):
-        tiles = picked_ref[pl.ds(group * slots, slots)].reshape(slots * 16, 128)
-        both = jnp.dot(tiles, fold, preferred_element_type=f32).astype(bf16).reshape(slots, 16, 128)
-        wide = jnp.concatenate([coupling_ref[group, s] for s in range(slots)], axis=1)
-        local1_ref[group] = nt(paired(slots, lambda s: both[s]), wide).astype(bf16)
-
+    local1 = [
+        nt(
+            paired(slots, lambda s: both[group][s]),
+            jnp.concatenate([coupling_ref[group, s] for s in range(slots)], axis=1),
+        ).astype(bf16)
+        for group in range(groups)
+    ]
     for copy in copies[1:]:
         copy.wait()
-
-    def one_group(group, carry):
-        for child in range(8):
-            leaf = group * 8 + child
-            field = nt(paired(slots, lambda s: table_ref[leaf_refs[leaf, s]]), packed_ref[leaf])
-            field = (field + nt(local1_ref[group], transfer_ref[leaf])).astype(bf16)
-            span = pl.ds(pl.multiple_of(leaf * 128, 128), 128)
+    for group in range(groups):
+        leaves = range(group * 8, group * 8 + 8)
+        passed = [nt(local1[group], transfer_ref[leaf]) for leaf in leaves]
+        rounded = [(local_ref[leaf] + one).astype(bf16) for leaf, one in zip(leaves, passed)]
+        for leaf, field in zip(leaves, rounded):
+            span = slice(leaf * 128, (leaf + 1) * 128)
             out_ref[:, span] = near_ref[:, span] + jnp.dot(field, basis_ref[leaf], preferred_element_type=f32)
-        return carry
-
-    lax.fori_loop(0, groups, one_group, 0)
-
-
-def finish(column, leaf_refs, group_refs, swapped, below, above, packed, coupling, transfer, basis, near):
+
+
+def downward(group_refs, coarse, local0, coupling, transfer, basis, one, two):
     groups, slots = coupling.shape[:2]
+    count = one.shape[1] + two.shape[1]
     return pl.pallas_call(
-        finish_kernel,
-        name="finish",
-        out_shape=jax.ShapeDtypeStruct(near.shape, f32),
-        in_specs=[SMEM] * 3 + [VMEM] * 3 + [HBM] * 5,
+        downward_kernel,
+        name="downward",
+        out_shape=jax.ShapeDtypeStruct((16, count), f32),
+        in_specs=[SMEM] + [VMEM] * 2 + [HBM] * 5,
         out_specs=VMEM,
         scratch_shapes=[
             pltpu.VMEM(coupling.shape, bf16),
             pltpu.VMEM(transfer.shape, bf16),
             pltpu.VMEM(basis.shape, bf16),
-            pltpu.VMEM(near.shape, f32),
-            pltpu.VMEM(packed.shape, bf16),
-            pltpu.VMEM(((2 * WINDOW + 1) * 16, 16, 128), bf16),
+            pltpu.VMEM((16, count), f32),
             pltpu.VMEM((groups * slots, 16, 128), bf16),
-            pltpu.VMEM((groups, 16, 64), bf16),
             pltpu.SemaphoreType.DMA((5,)),
         ],
-        compiler_params=pltpu.CompilerParams(vmem_limit_bytes=24 << 20),
-        cost_estimate=pl.CostEstimate(flops=200_000_000, bytes_accessed=14 << 20, transcendentals=0),
+        compiler_params=pltpu.CompilerParams(vmem_limit_bytes=16 << 20),
+        cost_estimate=pl.CostEstimate(flops=60_000_000, bytes_accessed=5 << 20, transcendentals=0),
     )(
-        column, leaf_refs, group_refs, swapped, below, above,
-        *(pltpu.with_memory_space_constraint(x, pltpu.HBM) for x in (coupling, transfer, basis, near, packed)),
+        group_refs, coarse, local0,
+        *(pltpu.with_memory_space_constraint(x, pltpu.HBM) for x in (coupling, transfer, basis, one, two)),
     )
 
 
@@ -400,22 +457,28 @@
     devices = lax.axis_size(AXES)
     column = lax.rem(lax.axis_index("gy").astype(jnp.int32), ROW).reshape(1)
     rows = [[row * ROW + i for i in range(ROW)] for row in range(devices // ROW)]
-    columns = [[col + ROW * i for i in range(devices // ROW)] for col in range(ROW)]
     pack, rim_last, rim_first, own, up, down, coarse = upward(
-        column, send_lists[0].T, densities, points, weights[None, :], leaf_basis, transfer, devices // ROW
-    )
-    coarse_rows = lax.all_to_all(coarse, AXES, 0, 0, axis_index_groups=columns, tiled=True)
+        column, send_lists[0].T, densities, points, weights[None, :], leaf_basis, transfer, devices
+    )
     lists_below = shifted(up, ROW, devices)
     lists_above = shifted(down, -ROW, devices)
     from_below = shifted(rim_last, 1, devices)
     from_above = shifted(rim_first, -1, devices)
-    payload = assemble(column, own, lists_below, lists_above, coarse_rows)
-    payload, from_below, from_above = lax.optimization_barrier((payload, from_below, from_above))
+    payload, from_below, from_above = lax.optimization_barrier(
+        (assemble(column, own, lists_below, lists_above), from_below, from_above)
+    )
     swapped = lax.all_to_all(payload, AXES, 0, 0, axis_index_groups=rows, tiled=True)
-    near, packed = near_field(near_offsets.T, pack, from_below, from_above, leaf_coupling)
-    return finish(
-        column, relay_refs, coarse_refs, swapped, lists_below, lists_above, packed, coarse_coupling, transfer,
-        leaf_basis, near,
+    offsets = near_offsets.T
+    half = near_offsets.shape[0] // 2
+    near_one, packed_one = near_field(offsets, pack, from_below, from_above, leaf_coupling, 0, half)
+    swapped, coarse, pack, near_one, packed_one = lax.optimization_barrier(
+        (swapped, coarse, pack, near_one, packed_one)
+    )
+    everyone = lax.all_to_all(coarse, AXES, 0, 0, tiled=True)
+    near_two, packed_two = near_field(offsets, pack, from_below, from_above, leaf_coupling, half, half)
+    local0 = leaf_local(column, relay_refs, swapped, lists_below, lists_above, packed_one, packed_two)
+    return downward(
+        coarse_refs, everyone, local0, coarse_coupling, transfer, leaf_basis, near_one, near_two
     )
 
 

time: 74 us -> 75.4 us (1.019)
  starting transfers between devices: 26.8 us -> 31.5 us
  Pallas kernels: 39.2 us -> 34.6 us
    all_to_all x1, starting transfers between devices: 8.04 us -> 12.6 us  [local(): everyone = lax.all_to_all(coarse, AXES, 0, 0, tiled=True)]
    all_to_all x1, waiting for transfers between devices: 4.08 us -> 0.01 us  [local(): lax.all_to_all(payload, AXES, 0, 0, axis_index_groups=rows, tiled=True)]
    all_to_all x1, waiting for transfers between devices: 0.15 us -> 4.18 us  [local(): everyone = lax.all_to_all(coarse, AXES, 0, 0, tiled=True)]
    pallas_call x2 -> x4, Pallas kernels: 32.5 us -> 28.9 us  [the longest x2 18.6 us: near_field(): pl.pallas_call(functools.partial(near_kernel, first, leaves), name='near'...]
  transfers between devices with their start and end apart: 6 -> 6, of which waited for: 3 -> 3; matrix products, arithmetic and copies ran while one was open for 0% -> 0% of each run, Pallas kernels for 24% -> 33%
where the time goes in v3:
time: 75.4 us; the launch traced here: 74.7 us
  Pallas kernels  34.6 us (46%)
  starting transfers between devices  31.5 us (42%)
  waiting for transfers between devices  6.98 us (9%)
  local copies, waits for them, and re-layouts  1.41 us (2%)
    pallas_call x2, Pallas kernels, near_field(): pl.pallas_call(functools.partial(near_kernel, first, leaves), name='near'...  18.6 us
    all_to_all x1, starting transfers between devices, local(): everyone = lax.all_to_all(coarse, AXES, 0, 0, tiled=True)  12.6 us
    ppermute x4, starting transfers between devices, shifted(): lax.ppermute(shard, AXES, [(i, i + by) for i in range(devices) if 0 <= i...  11.6 us
    all_to_all x1, starting transfers between devices, local(): lax.all_to_all(payload, AXES, 0, 0, axis_index_groups=rows, tiled=True)  7.24 us
    pallas_call x1, Pallas kernels, leaf_local(): pl.pallas_call(leaf_kernel, name='leaf_local', out_shape=jax.ShapeDtypeSt...  5.51 us
    pallas_call x1, Pallas kernels, upward(): pl.pallas_call(upward_kernel, name='upward', out_shape=(jax.ShapeDtypeStr...  4.87 us
    pallas_call x1, Pallas kernels, downward(): pl.pallas_call(downward_kernel, name='downward', out_shape=jax.ShapeDtype...  4.81 us
    all_to_all x1, waiting for transfers between devices, local(): everyone = lax.all_to_all(coarse, AXES, 0, 0, tiled=True)  4.18 us
  transfers between devices with their start and end apart: 6, of which 3 were waited for; matrix products, arithmetic and copies ran while one was open for 0% of the time, Pallas kernels for 33%

profile of v3, /device:TPU:1, one launch (start us, length us, event | category | flops | bytes accessed | tf_op | source)
XLA Modules:
  0.0 74.7 jit_solution(1756859603107292916)
XLA Ops:
  0.0 0.0 copy-start.3
  0.0 0.7 copy-done.3
  0.7 4.9 %upward.1 = (bf16[32,4096]{1,0:T(8,128)(2,1)S(1)}, bf16[32,1024]{1,0:T(8,128)(2,1)S(1)}, bf16[32,1024]{1,0:T(8,128)(2,1)S(1)}, bf16[8,8,16,128]{3,2,1,0:T(8,128)...) custom-call(s32[1]{0:T(128)} %bitcast.column_ref, ...), custom_call_target="tpu_custom_call" | custom-call | flops 20000000 | bytes 4194304 | tf_op jit(solution)/shard_map/upward/pallas_call | solution.py:112
  5.6 4.4 %collective-permute-start = (bf16[8,8,16,128]{3,2,1,0:T(8,128)(2,1)S(1)}, bf16[8,8,16,128]{3,2,1,0:T(8,128)(2,1)S(1)}, u32[]{:S(2)}, u32[]{:S(2)}) collective-permute-start(bf16[8,8,16,128]{3,2,1,0:T(8,128)(2,1)S(1)} %get-tuple-element.25), channel_id=1, source_target_pairs={{0,8},{1,9},{2,10},{3,11},{4,12},{5,13},{6,14},{7,15},{8,16},{9,17... | collective-permute-start | bytes 786440 | tf_op jit(solution)/shard_map/ppermute | solution.py:450
  10.0 1.3 %collective-permute-start.1 = (bf16[8,8,16,128]{3,2,1,0:T(8,128)(2,1)S(1)}, bf16[8,8,16,128]{3,2,1,0:T(8,128)(2,1)S(1)}, u32[]{:S(2)}, u32[]{:S(2)}) collective-permute-start(bf16[8,8,16,128]{3,2,1,0:T(8,128)(2,1)S(1)} %get-tuple-element.26), channel_id=1, source_target_pairs={{8,0},{9,1},{10,2},{11,3},{12,4},{13,5},{14,6},{15,7},{16,8},{17,9... | collective-permute-start | bytes 786440 | tf_op jit(solution)/shard_map/ppermute | solution.py:450
  11.3 4.0 %collective-permute-start.2 = (bf16[32,1024]{1,0:T(8,128)(2,1)S(1)}, bf16[32,1024]{1,0:T(8,128)(2,1)S(1)}, u32[]{:S(2)}, u32[]{:S(2)}) collective-permute-start(bf16[32,1024]{1,0:T(8,128)(2,1)S(1)} %get-tuple-element.27), channel_id=1, source_target_pairs={{0,1},{1,2},{2,3},{3,4},{4,5},{5,6},{6,7},{7,8},{8,9},{9,10},{10,1... | collective-permute-start | bytes 196616 | tf_op jit(solution)/shard_map/ppermute | solution.py:450
  15.3 1.9 %collective-permute-start.3 = (bf16[32,1024]{1,0:T(8,128)(2,1)S(1)}, bf16[32,1024]{1,0:T(8,128)(2,1)S(1)}, u32[]{:S(2)}, u32[]{:S(2)}) collective-permute-start(bf16[32,1024]{1,0:T(8,128)(2,1)S(1)} %get-tuple-element.28), channel_id=1, source_target_pairs={{1,0},{2,1},{3,2},{4,3},{5,4},{6,5},{7,6},{8,7},{9,8},{10,9},{11,1... | collective-permute-start | bytes 196616 | tf_op jit(solution)/shard_map/ppermute | solution.py:450
  17.2 0.0 collective-permute-done.below_ref
  17.3 1.8 %collective-permute-done.1.above_ref = bf16[8,8,16,128]{3,2,1,0:T(8,128)(2,1)S(1)} collective-permute-done((bf16[8,8,16,128]{3,2,1,0:T(8,128)(2,1)S(1)}, bf16[8,8,16,128]{3,2,1,0:T(8,128)(2,1)S(1)}, u32[]{:S(2)}, u32[]{:S(2)}) %collective-permute-start.1) | collective-permute-done | bytes 262176 | tf_op jit(solution)/shard_map/ppermute | solution.py:450
  19.1 0.9 %assemble.1 = bf16[8,16,16,128]{3,2,1,0:T(8,128)(2,1)} custom-call(s32[1]{0:T(128)} %bitcast.column_ref, bf16[8,8,16,128]{3,2,1,0:T(8,128)(2,1)S(1)} %get-tuple-element.24.own_ref, bf16[8,8,16,128]{3,2,1,0:T(8,128)(2,1)S(1)} %collective-permute-done.below_ref, bf16[8,8,16,128]{3,2,1,0:T(8,128)(2,1)S(1)} %collective-permute-done.1.above_ref), custom_call_target="tpu_custom_call" | custom-call | bytes 1048576 | tf_op jit(solution)/shard_map/assemble/pallas_call | solution.py:294
  19.9 0.0 collective-permute-done.2.below_ref
  19.9 1.0 %collective-permute-done.3.above_ref = bf16[32,1024]{1,0:T(8,128)(2,1)S(1)} collective-permute-done((bf16[32,1024]{1,0:T(8,128)(2,1)S(1)}, bf16[32,1024]{1,0:T(8,128)(2,1)S(1)}, u32[]{:S(2)}, u32[]{:S(2)}) %collective-permute-start.3) | collective-permute-done | bytes 65568 | tf_op jit(solution)/shard_map/ppermute | solution.py:450
  20.9 7.2 %all-to-all-start = ((bf16[8,16,16,128]{3,2,1,0:T(8,128)(2,1)}), bf16[8,16,16,128]{3,2,1,0:T(8,128)(2,1)S(1)}, u32[]{:S(2)}, u32[]{:S(2)}) async-start(bf16[8,16,16,128]{3,2,1,0:T(8,128)(2,1)} %assemble.1), calls=%async_computation | async-start | bytes 1048576 | tf_op jit(solution)/shard_map/all_to_all | solution.py:470
  28.1 0.0 copy-start
  28.1 0.7 copy-done
  28.8 0.0 copy-start.1
  28.8 9.3 %near.2 = (f32[16,2048]{1,0:T(8,128)}, bf16[16,64,2048]{2,1,0:T(8,128)(2,1)}) custom-call(s32[13,32]{1,0:T(8,128)S(1)} %bitcast.6, bf16[32,4096]{1,0:T(8,128)(2,1)S(1)} %get-tuple-element.39.pack_ref, bf16[32,1024]{1,0:T(8,128)(2,1)S(1)} %collective-permute-done.2.below_ref, bf16[32,1024]{1,0:T(8,128)(2,1)S(1)} %collective-permute-done.3.above_ref, ...), custom_call_target="tpu_custom_call" | custom-call | flops 327155712 | bytes 14680064 | tf_op jit(solution)/shard_map/near/pallas_call | solution.py:253
  38.1 0.0 all-to-all-done.swapped_ref
  38.1 12.6 %all-to-all-start.1 = ((bf16[128,2,16,128]{3,2,1,0:T(8,128)(2,1)}), bf16[128,2,16,128]{3,2,1,0:T(8,128)(2,1)S(1)}, u32[]{:S(2)}, u32[]{:S(2)}) async-start(bf16[128,2,16,128]{3,2,1,0:T(8,128)(2,1)} %get-tuple-element.36), calls=%async_computation.1 | async-start | bytes 2097152 | tf_op jit(solution)/shard_map/all_to_all | solution.py:477
  50.8 0.0 copy-done.1
  50.8 0.0 copy-start.2
  50.8 9.3 %near.3 = (f32[16,2048]{1,0:T(8,128)}, bf16[16,64,2048]{2,1,0:T(8,128)(2,1)}) custom-call(s32[13,32]{1,0:T(8,128)S(1)} %bitcast.7, bf16[32,4096]{1,0:T(8,128)(2,1)S(1)} %get-tuple-element.39.pack_ref, bf16[32,1024]{1,0:T(8,128)(2,1)S(1)} %collective-permute-done.2.below_ref, bf16[32,1024]{1,0:T(8,128)(2,1)S(1)} %collective-permute-done.3.above_ref, ...), custom_call_target="tpu_custom_call" | custom-call | flops 327155712 | bytes 14680064 | tf_op jit(solution)/shard_map/near/pallas_call | solution.py:253
  60.1 0.0 copy-done.2
  60.1 0.0 copy-start.4
  60.2 5.5 %leaf_local.1.local_ref = f32[32,16,64]{2,1,0:T(8,128)S(1)} custom-call(s32[1]{0:T(128)} %bitcast.column_ref, s32[32,32]{1,0:T(8,128)S(1)} %copy-done.2, bf16[8,16,16,128]{3,2,1,0:T(8,128)(2,1)S(1)} %all-to-all-done.swapped_ref, bf16[8,8,16,128]{3,2,1,0:T(8,128)(2,1)S(1)} %collective-permute-done.below_ref, ...), custom_call_target="tpu_custom_call" | custom-call | flops 140000000 | bytes 9437184 | tf_op jit(solution)/shard_map/leaf_local/pallas_call | solution.py:358
  65.7 4.2 %all-to-all-done.1.coarse_ref = bf16[128,2,16,128]{3,2,1,0:T(8,128)(2,1)S(1)} async-done(((bf16[128,2,16,128]{3,2,1,0:T(8,128)(2,1)}), bf16[128,2,16,128]{3,2,1,0:T(8,128)(2,1)S(1)}, u32[]{:S(2)}, u32[]{:S(2)}) %all-to-all-start.1) | async-done | bytes 1048608 | tf_op jit(solution)/shard_map/all_to_all | solution.py:477
  69.9 0.0 copy-done.4
  69.9 4.8 %downward.1 = f32[16,4096]{1,0:T(8,128)} custom-call(s32[4,32]{1,0:T(4,128)S(1)} %copy-done.4, bf16[128,2,16,128]{3,2,1,0:T(8,128)(2,1)S(1)} %all-to-all-done.1.coarse_ref, f32[32,16,64]{2,1,0:T(8,128)S(1)} %leaf_local.1.local_ref, bf16[4,32,64,64]{3,2,1,0:T(8,128)(2,1)} %coupling_hbm.5, bf16[32,64,64]{2,1,0:T(8,128)(2,1)} %transfer_hbm.3, ...), custom_call_target="tpu_custom_call" | custom-call | flops 60000000 | bytes 5242880 | tf_op jit(solution)/shard_map/downward/pallas_call | solution.py:427
Async XLA Ops:
  0.0 0.7 copy-start.3
  5.6 11.7 %collective-permute-start = (bf16[8,8,16,128]{3,2,1,0:T(8,128)(2,1)S(1)}, bf16[8,8,16,128]{3,2,1,0:T(8,128)(2,1)S(1)}, u32[]{:S(2)}, u32[]{:S(2)}) collective-permute-start(bf16[8,8,16,128]{3,2,1,0:T(8,128)(2,1)S(1)} %get-tuple-element.25), channel_id=1, source_target_pairs={{0,8},{1,9},{2,10},{3,11},{4,12},{5,13},{6,14},{7,15},{8,16},{9,17... | collective-permute-start | bytes 786440 | tf_op jit(solution)/shard_map/ppermute | solution.py:450
  10.0 9.1 %collective-permute-start.1 = (bf16[8,8,16,128]{3,2,1,0:T(8,128)(2,1)S(1)}, bf16[8,8,16,128]{3,2,1,0:T(8,128)(2,1)S(1)}, u32[]{:S(2)}, u32[]{:S(2)}) collective-permute-start(bf16[8,8,16,128]{3,2,1,0:T(8,128)(2,1)S(1)} %get-tuple-element.26), channel_id=1, source_target_pairs={{8,0},{9,1},{10,2},{11,3},{12,4},{13,5},{14,6},{15,7},{16,8},{17,9... | collective-permute-start | bytes 786440 | tf_op jit(solution)/shard_map/ppermute | solution.py:450
  11.3 8.7 %collective-permute-start.2 = (bf16[32,1024]{1,0:T(8,128)(2,1)S(1)}, bf16[32,1024]{1,0:T(8,128)(2,1)S(1)}, u32[]{:S(2)}, u32[]{:S(2)}) collective-permute-start(bf16[32,1024]{1,0:T(8,128)(2,1)S(1)} %get-tuple-element.27), channel_id=1, source_target_pairs={{0,1},{1,2},{2,3},{3,4},{4,5},{5,6},{6,7},{7,8},{8,9},{9,10},{10,1... | collective-permute-start | bytes 196616 | tf_op jit(solution)/shard_map/ppermute | solution.py:450
  15.3 5.6 %collective-permute-start.3 = (bf16[32,1024]{1,0:T(8,128)(2,1)S(1)}, bf16[32,1024]{1,0:T(8,128)(2,1)S(1)}, u32[]{:S(2)}, u32[]{:S(2)}) collective-permute-start(bf16[32,1024]{1,0:T(8,128)(2,1)S(1)} %get-tuple-element.28), channel_id=1, source_target_pairs={{1,0},{2,1},{3,2},{4,3},{5,4},{6,5},{7,6},{8,7},{9,8},{10,9},{11,1... | collective-permute-start | bytes 196616 | tf_op jit(solution)/shard_map/ppermute | solution.py:450
  20.9 17.2 %all-to-all-start = ((bf16[8,16,16,128]{3,2,1,0:T(8,128)(2,1)}), bf16[8,16,16,128]{3,2,1,0:T(8,128)(2,1)S(1)}, u32[]{:S(2)}, u32[]{:S(2)}) async-start(bf16[8,16,16,128]{3,2,1,0:T(8,128)(2,1)} %assemble.1), calls=%async_computation | async-start | bytes 1048576 | tf_op jit(solution)/shard_map/all_to_all | solution.py:470
  28.1 0.7 copy-start
  28.8 21.9 %copy-start.1 = (s32[32,13]{0,1:T(8,128)S(1)}, s32[32,13]{0,1:T(8,128)}, u32[]{:S(2)}) copy-start(s32[32,13]{0,1:T(8,128)} %param.14) | copy-start | bytes 4996
  38.1 31.7 %all-to-all-start.1 = ((bf16[128,2,16,128]{3,2,1,0:T(8,128)(2,1)}), bf16[128,2,16,128]{3,2,1,0:T(8,128)(2,1)S(1)}, u32[]{:S(2)}, u32[]{:S(2)}) async-start(bf16[128,2,16,128]{3,2,1,0:T(8,128)(2,1)} %get-tuple-element.36), calls=%async_computation.1 | async-start | bytes 2097152 | tf_op jit(solution)/shard_map/all_to_all | solution.py:477
  50.8 9.3 %copy-start.2 = (s32[32,32]{1,0:T(8,128)S(1)}, s32[32,32]{1,0:T(8,128)}, u32[]{:S(2)}) copy-start(s32[32,32]{1,0:T(8,128)} %leaf_refs.1) | copy-start | bytes 12292
  60.1 9.7 %copy-start.4 = (s32[4,32]{1,0:T(4,128)S(1)}, s32[4,32]{1,0:T(4,128)}, u32[]{:S(2)}) copy-start(s32[4,32]{1,0:T(4,128)} %group_refs.1) | copy-start | bytes 1540

commit v4 on v2

--- a/solution.py
+++ b/solution.py
@@ -11,6 +11,7 @@
 AXES = ("gx", "gy")
 REACH = 8
 WINDOW = 8
+DEPTH = 2
 ROW = 8
 core_square = 0.0004
 four_pi = 4.0 * math.pi
@@ -20,6 +21,14 @@
 SMEM = pl.BlockSpec(memory_space=pltpu.SMEM)
 HBM = pl.BlockSpec(memory_space=pltpu.HBM)
 VMEM = pl.BlockSpec(memory_space=pltpu.VMEM)
+
+
+def pinned(x):
+    return pltpu.with_memory_space_constraint(x, pltpu.HBM)
+
+
+def kept(x):
+    return pltpu.with_memory_space_constraint(x, pltpu.VMEM)
 
 
 def nt(a, b):
@@ -39,15 +48,15 @@
 
 
 def upward_kernel(
-    column_ref, lists_ref, dens_hbm, points_hbm, weights_hbm, basis_hbm, transfer_hbm,
+    column_ref, lists_hbm, dens_hbm, points_hbm, weights_hbm, basis_hbm, transfer_hbm,
     pack_ref, below_ref, above_ref, own_ref, up_ref, down_ref, coarse_ref,
-    dens_ref, points_ref, weights_ref, basis_ref, transfer_ref, both_ref, sems,
+    lists_ref, dens_ref, points_ref, weights_ref, basis_ref, transfer_ref, both_ref, sems,
 ):
     copies = [
         pltpu.make_async_copy(source, target, sems.at[i])
         for i, (source, target) in enumerate((
             (dens_hbm, dens_ref), (points_hbm, points_ref), (weights_hbm, weights_ref),
-            (basis_hbm, basis_ref), (transfer_hbm, transfer_ref),
+            (basis_hbm, basis_ref), (transfer_hbm, transfer_ref), (lists_hbm, lists_ref),
         ))
     ]
     for copy in copies:
@@ -72,12 +81,13 @@
         copy.wait()
     coarse = []
     for group in range(leaves // 8):
+        members = range(group * 8, group * 8 + 8)
+        twice = [
+            nt(dens_ref[:, leaf * 128 : (leaf + 1) * 128], jnp.concatenate([basis_ref[leaf]] * 2, axis=0)).astype(bf16)
+            for leaf in members
+        ]
         total = jnp.zeros((16, 64), f32)
-        for child in range(8):
-            leaf = group * 8 + child
-            basis = basis_ref[leaf]
-            twice = nt(dens_ref[:, leaf * 128 : (leaf + 1) * 128], jnp.concatenate([basis, basis], axis=0))
-            rounded = twice.astype(bf16)
+        for leaf, rounded in zip(members, twice):
             both_ref[leaf] = rounded
             total += jnp.dot(rounded[:, :64], transfer_ref[leaf], preferred_element_type=f32)
         coarse.append(total)
@@ -117,25 +127,28 @@
             block, block, block,
             jax.ShapeDtypeStruct((row_count, leaves // 16, 16, 128), bf16),
         ),
-        in_specs=[SMEM, SMEM] + [HBM] * 5,
+        in_specs=[SMEM] + [HBM] * 6,
         out_specs=[VMEM] * 7,
         scratch_shapes=[
+            pltpu.SMEM(lists.shape, jnp.int32),
             pltpu.VMEM(densities.shape, bf16),
             pltpu.VMEM(points.shape, f32),
             pltpu.VMEM(weights.shape, f32),
             pltpu.VMEM(basis.shape, bf16),
             pltpu.VMEM(transfer.shape, bf16),
             pltpu.VMEM((leaves, 16, 128), bf16),
-            pltpu.SemaphoreType.DMA((5,)),
+            pltpu.SemaphoreType.DMA((6,)),
         ],
         compiler_params=pltpu.CompilerParams(vmem_limit_bytes=12 << 20),
         cost_estimate=pl.CostEstimate(flops=20_000_000, bytes_accessed=4 << 20, transcendentals=0),
-    )(column, lists, *(pltpu.with_memory_space_constraint(x, pltpu.HBM) for x in (densities, points, weights, basis, transfer)))
+    )(column, *(pinned(x) for x in (lists, densities, points, weights, basis, transfer)))
 
 
 def near_kernel(
-    offsets_ref, pack_ref, below_ref, above_ref, coupling_hbm,
-    near_hbm, packed_hbm, near_ref, left_ref, right_ref, wide_ref, buffer_ref, packed_ref, sems, out_sems,
+    offsets_hbm, pack_ref, below_ref, above_ref, coupling_hbm, coarse_hbm,
+    near_hbm, packed_hbm, packed_coarse_ref,
+    offsets_ref, near_ref, left_ref, right_ref, wide_ref, buffer_ref, packed_ref, coarse_ref,
+    sems, out_sems, more_sems,
 ):
     rim = REACH * 128
     inner = pack_ref.shape[1]
@@ -144,16 +157,26 @@
     steps = leaves // per_step
 
     def fetch(step, slot):
-        return pltpu.make_async_copy(
-            coupling_hbm.at[pl.ds(step * per_step, per_step)], buffer_ref.at[slot], sems.at[slot]
-        )
+        return [
+            pltpu.make_async_copy(coupling_hbm.at[step * per_step + i], buffer_ref.at[slot, i], sems.at[slot, i])
+            for i in range(per_step)
+        ]
 
     def flush(step, slot):
-        return pltpu.make_async_copy(
-            packed_ref.at[slot], packed_hbm.at[pl.ds(step * per_step, per_step)], out_sems.at[slot]
-        )
-
-    fetch(0, 0).start()
+        return [
+            pltpu.make_async_copy(packed_ref.at[slot, i], packed_hbm.at[step * per_step + i], out_sems.at[slot, i])
+            for i in range(per_step)
+        ]
+
+    table = pltpu.make_async_copy(offsets_hbm, offsets_ref, more_sems.at[0])
+    upper = pltpu.make_async_copy(coarse_hbm, coarse_ref, more_sems.at[1])
+    table.start()
+    for copy in fetch(0, 0):
+        copy.start()
+    upper.start()
+
+    def merged(source, tile):
+        return jnp.concatenate([source[tile], source[tile + 1]], axis=1)
 
     def build(source, at, start, width, own):
         wide_ref[:, pl.ds(at, width)] = source[0:16, pl.ds(start, width)]
@@ -179,56 +202,69 @@
     for part in range(inner // 512):
         build(pack_ref, rim + part * 512, part * 512, 512, True)
 
+    table.wait()
     slots = offsets_ref.shape[0]
 
-    def one_leaf(leaf):
+    def squares(leaf, slot):
         own = left_ref[:, pl.ds(pl.multiple_of(leaf * 128, 128), 128)]
-        total = jnp.zeros((16, 128), f32)
-        for slot in range(0, slots, 2):
-            spans = [
-                pl.ds(pl.multiple_of((leaf + REACH + offsets_ref[s, leaf]) * 128, 128), 128)
-                for s in range(slot, min(slot + 2, slots))
-            ]
-            right = jnp.concatenate([right_ref[:, span] for span in spans], axis=1)
-            wide = jnp.concatenate([wide_ref[:, span] for span in spans], axis=1)
-            square = lax.dot_general(own, right, (((0,), (0,)), ((), ())), preferred_element_type=f32)
-            total += nt(wide, lax.rsqrt(square).astype(bf16))
-        near_ref[:, pl.ds(pl.multiple_of(leaf * 128, 128), 128)] = total
+        spans = [
+            pl.ds(pl.multiple_of((leaf + REACH + offsets_ref[s, leaf]) * 128, 128), 128)
+            for s in range(slot, min(slot + 2, slots))
+        ]
+        right = jnp.concatenate([right_ref[:, span] for span in spans], axis=1)
+        wide = jnp.concatenate([wide_ref[:, span] for span in spans], axis=1)
+        return wide, lax.dot_general(own, right, (((0,), (0,)), ((), ())), preferred_element_type=f32)
 
     def one_step(step, carry):
         slot = lax.rem(step, 2)
-        fetch(step, slot).wait()
+        for copy in fetch(step, slot):
+            copy.wait()
 
         @pl.when(step + 1 < steps)
         def _():
-            fetch(step + 1, 1 - slot).start()
+            for copy in fetch(step + 1, 1 - slot):
+                copy.start()
 
         @pl.when(step >= 2)
         def _():
-            flush(step - 2, slot).wait()
-
-        for inside in range(per_step):
+            for copy in flush(step - 2, slot):
+                copy.wait()
+
+        work = [(inside, s) for inside in range(per_step) for s in range(0, slots, 2)]
+        totals = [jnp.zeros((16, 128), f32)] * per_step
+        ahead = [squares(step * per_step + inside, s) for inside, s in work[:DEPTH]]
+        for at, (inside, s) in enumerate(work):
             leaf = step * per_step + inside
-            one_leaf(leaf)
-            for tile in range(0, tiles, 2):
-                packed_ref[slot, inside, :, tile * 64 : (tile + 2) * 64] = jnp.concatenate(
-                    [buffer_ref[slot, inside, tile], buffer_ref[slot, inside, tile + 1]], axis=1
-                )
-        flush(step, slot).start()
+            if at + DEPTH < len(work):
+                later, other = work[at + DEPTH]
+                ahead.append(squares(step * per_step + later, other))
+            wide, square = ahead.pop(0)
+            totals[inside] += nt(wide, lax.rsqrt(square).astype(bf16))
+            for tile in range(s * 2, min(s * 2 + 4, tiles) if s + 2 < slots else tiles, 2):
+                packed_ref[slot, inside, :, tile * 64 : (tile + 2) * 64] = merged(buffer_ref.at[slot, inside], tile)
+            if s + 2 >= slots:
+                near_ref[:, pl.ds(pl.multiple_of(leaf * 128, 128), 128)] = totals[inside]
+                flush(step, slot)[inside].start()
         return carry
 
     lax.fori_loop(0, steps, one_step, 0)
-    last = pltpu.make_async_copy(near_ref, near_hbm, out_sems.at[2])
+    last = pltpu.make_async_copy(near_ref, near_hbm, more_sems.at[2])
     last.start()
+    upper.wait()
+    for group in range(coarse_ref.shape[0]):
+        for tile in range(0, tiles, 2):
+            packed_coarse_ref[group, :, tile * 64 : (tile + 2) * 64] = merged(coarse_ref.at[group], tile)
     for step in range(steps - 2, steps):
-        flush(step, step % 2).wait()
+        for copy in flush(step, step % 2):
+            copy.wait()
     last.wait()
 
 
-def near_field(offsets, pack, below, above, coupling):
+def near_field(offsets, pack, below, above, coupling, coarse_coupling):
     count = pack.shape[1]
     wide = count + 2 * REACH * 128
     leaves, tiles = coupling.shape[:2]
+    groups = coarse_coupling.shape[0]
     per_step = 4
     points = count * offsets.shape[0] * 128
     return pl.pallas_call(
@@ -237,22 +273,26 @@
         out_shape=(
             pltpu.HBM((16, count), f32),
             pltpu.HBM((leaves, 64, tiles * 64), bf16),
+            pltpu.VMEM((groups, 64, tiles * 64), bf16),
         ),
-        in_specs=[SMEM, VMEM, VMEM, VMEM, HBM],
-        out_specs=[HBM, HBM],
+        in_specs=[HBM, VMEM, VMEM, VMEM, HBM, HBM],
+        out_specs=[HBM, HBM, VMEM],
         scratch_shapes=[
+            pltpu.SMEM(offsets.shape, jnp.int32),
             pltpu.VMEM((16, count), f32),
             pltpu.VMEM((32, count), bf16),
             pltpu.VMEM((32, wide), bf16),
             pltpu.VMEM((16, wide), bf16),
             pltpu.VMEM((2, per_step) + coupling.shape[1:], bf16),
             pltpu.VMEM((2, per_step, 64, tiles * 64), bf16),
-            pltpu.SemaphoreType.DMA((2,)),
+            pltpu.VMEM(coarse_coupling.shape, bf16),
+            pltpu.SemaphoreType.DMA((2, per_step)),
+            pltpu.SemaphoreType.DMA((2, per_step)),
             pltpu.SemaphoreType.DMA((3,)),
         ],
-        compiler_params=pltpu.CompilerParams(vmem_limit_bytes=24 << 20),
-        cost_estimate=pl.CostEstimate(flops=points * 96, bytes_accessed=28 << 20, transcendentals=points),
-    )(offsets, pack, below, above, pltpu.with_memory_space_constraint(coupling, pltpu.HBM))
+        compiler_params=pltpu.CompilerParams(vmem_limit_bytes=16 << 20),
+        cost_estimate=pl.CostEstimate(flops=points * 96, bytes_accessed=20 << 20, transcendentals=points),
+    )(pinned(offsets), pack, below, above, pinned(coupling), pinned(coarse_coupling))
 
 
 def assemble_kernel(column_ref, own_ref, below_ref, above_ref, coarse_ref, out_ref):
@@ -299,20 +339,26 @@
 
 
 def finish_kernel(
-    column_ref, leaf_refs, group_refs, swapped_ref, below_ref, above_ref,
-    coupling_hbm, transfer_hbm, basis_hbm, near_hbm, packed_hbm,
-    out_ref, coupling_ref, transfer_ref, basis_ref, near_ref, packed_ref, table_ref, picked_ref, local1_ref, sems,
+    column_ref, leaf_hbm, group_hbm, swapped_ref, below_ref, above_ref, coupling_ref,
+    packed_hbm, transfer_hbm, basis_hbm, near_hbm,
+    out_ref, leaf_refs, group_refs, packed_ref, near_ref, transfer_ref, basis_ref, table_ref, picked_ref, sems,
 ):
+    groups = coupling_ref.shape[0]
+    slots = coupling_ref.shape[2] // 64
     copies = [
         pltpu.make_async_copy(source, target, sems.at[i])
         for i, (source, target) in enumerate((
-            (coupling_hbm, coupling_ref), (transfer_hbm, transfer_ref), (basis_hbm, basis_ref),
-            (near_hbm, near_ref), (packed_hbm, packed_ref),
+            (group_hbm, group_refs), (leaf_hbm, leaf_refs), (transfer_hbm, transfer_ref), (basis_hbm, basis_ref),
+            (near_hbm, near_ref),
         ))
     ]
+    chunks = [
+        pltpu.make_async_copy(packed_hbm.at[pl.ds(i * 4, 4)], packed_ref.at[pl.ds(i * 4, 4)], sems.at[5 + i])
+        for i in range(2 * groups)
+    ]
+    copies[2:2] = chunks
     for copy in copies:
         copy.start()
-    groups, slots = coupling_ref.shape[:2]
     mask = low_half((16, 128))
     column = column_ref[0]
     spread = spread_matrix()
@@ -331,6 +377,7 @@
         crossed = jnp.where((place >= ROW) & (place < 2 * ROW), 0, 8)
         put(window, swapped_ref[owner, pl.ds(pl.multiple_of(crossed, 8), 8)])
 
+    copies[0].wait()
     for group in range(groups):
         for slot in range(slots):
             ref = group_refs[group, slot]
@@ -340,52 +387,55 @@
     row = lax.broadcasted_iota(jnp.int32, (128, 128), 0)
     col = lax.broadcasted_iota(jnp.int32, (128, 128), 1)
     fold = jnp.where((row % 64) == (col % 64), 1.0, 0.0).astype(bf16)
-    copies[0].wait()
+    both = [
+        jnp.dot(
+            picked_ref[pl.ds(group * slots, slots)].reshape(slots * 16, 128), fold, preferred_element_type=f32
+        ).astype(bf16).reshape(slots, 16, 128)
+        for group in range(groups)
+    ]
+    local1 = [
+        nt(paired(slots, lambda s: both[group][s]), coupling_ref[group]).astype(bf16) for group in range(groups)
+    ]
+    copies[1].wait()
+    for copy in copies[2 + len(chunks):]:
+        copy.wait()
     for group in range(groups):
-        tiles = picked_ref[pl.ds(group * slots, slots)].reshape(slots * 16, 128)
-        both = jnp.dot(tiles, fold, preferred_element_type=f32).astype(bf16).reshape(slots, 16, 128)
-        wide = jnp.concatenate([coupling_ref[group, s] for s in range(slots)], axis=1)
-        local1_ref[group] = nt(paired(slots, lambda s: both[s]), wide).astype(bf16)
-
-    for copy in copies[1:]:
-        copy.wait()
-
-    def one_group(group, carry):
-        for child in range(8):
-            leaf = group * 8 + child
-            field = nt(paired(slots, lambda s: table_ref[leaf_refs[leaf, s]]), packed_ref[leaf])
-            field = (field + nt(local1_ref[group], transfer_ref[leaf])).astype(bf16)
-            span = pl.ds(pl.multiple_of(leaf * 128, 128), 128)
+        chunks[2 * group].wait()
+        chunks[2 * group + 1].wait()
+        leaves = range(group * 8, group * 8 + 8)
+        fields = [nt(paired(slots, lambda s: table_ref[leaf_refs[leaf, s]]), packed_ref[leaf]) for leaf in leaves]
+        passed = [nt(local1[group], transfer_ref[leaf]) for leaf in leaves]
+        rounded = [(one + two).astype(bf16) for one, two in zip(fields, passed)]
+        for leaf, field in zip(leaves, rounded):
+            span = slice(leaf * 128, (leaf + 1) * 128)
             out_ref[:, span] = near_ref[:, span] + jnp.dot(field, basis_ref[leaf], preferred_element_type=f32)
-        return carry
-
-    lax.fori_loop(0, groups, one_group, 0)
 
 
 def finish(column, leaf_refs, group_refs, swapped, below, above, packed, coupling, transfer, basis, near):
-    groups, slots = coupling.shape[:2]
+    groups = coupling.shape[0]
+    slots = leaf_refs.shape[1]
     return pl.pallas_call(
         finish_kernel,
         name="finish",
         out_shape=jax.ShapeDtypeStruct(near.shape, f32),
-        in_specs=[SMEM] * 3 + [VMEM] * 3 + [HBM] * 5,
+        in_specs=[SMEM] + [HBM] * 2 + [VMEM] * 4 + [HBM] * 4,
         out_specs=VMEM,
         scratch_shapes=[
-            pltpu.VMEM(coupling.shape, bf16),
+            pltpu.SMEM(leaf_refs.shape, jnp.int32),
+            pltpu.SMEM(group_refs.shape, jnp.int32),
+            pltpu.VMEM(packed.shape, bf16),
+            pltpu.VMEM(near.shape, f32),
             pltpu.VMEM(transfer.shape, bf16),
             pltpu.VMEM(basis.shape, bf16),
-            pltpu.VMEM(near.shape, f32),
-            pltpu.VMEM(packed.shape, bf16),
             pltpu.VMEM(((2 * WINDOW + 1) * 16, 16, 128), bf16),
             pltpu.VMEM((groups * slots, 16, 128), bf16),
-            pltpu.VMEM((groups, 16, 64), bf16),
-            pltpu.SemaphoreType.DMA((5,)),
+            pltpu.SemaphoreType.DMA((5 + 2 * groups,)),
         ],
-        compiler_params=pltpu.CompilerParams(vmem_limit_bytes=24 << 20),
-        cost_estimate=pl.CostEstimate(flops=200_000_000, bytes_accessed=14 << 20, transcendentals=0),
+        compiler_params=pltpu.CompilerParams(vmem_limit_bytes=20 << 20),
+        cost_estimate=pl.CostEstimate(flops=200_000_000, bytes_accessed=4 << 20, transcendentals=0),
     )(
-        column, leaf_refs, group_refs, swapped, below, above,
-        *(pltpu.with_memory_space_constraint(x, pltpu.HBM) for x in (coupling, transfer, basis, near, packed)),
+        column, pinned(leaf_refs), pinned(group_refs), swapped, below, above,
+        kept(coupling), pinned(packed), pinned(transfer), pinned(basis), pinned(near),
     )
 
 
@@ -412,9 +462,11 @@
     payload = assemble(column, own, lists_below, lists_above, coarse_rows)
     payload, from_below, from_above = lax.optimization_barrier((payload, from_below, from_above))
     swapped = lax.all_to_all(payload, AXES, 0, 0, axis_index_groups=rows, tiled=True)
-    near, packed = near_field(near_offsets.T, pack, from_below, from_above, leaf_coupling)
+    near, packed, packed_coarse = near_field(
+        near_offsets.T, pack, from_below, from_above, leaf_coupling, coarse_coupling
+    )
     return finish(
-        column, relay_refs, coarse_refs, swapped, lists_below, lists_above, packed, coarse_coupling, transfer,
+        column, relay_refs, coarse_refs, swapped, lists_below, lists_above, packed, packed_coarse, transfer,
         leaf_basis, near,
     )
 

time: 74 us -> 66.1 us (0.89)
  Pallas kernels: 39.2 us -> 30.1 us
  waiting for transfers between devices: 6.42 us -> 8.51 us
    pallas_call x1, Pallas kernels: 15.9 us -> 10.4 us  [finish(): pl.pallas_call(finish_kernel, name='finish', out_shape=jax.ShapeDtypeStru...]
    all_to_all x1, waiting for transfers between devices: 4.08 us -> 6.18 us  [local(): lax.all_to_all(payload, AXES, 0, 0, axis_index_groups=rows, tiled=True)]
    pallas_call x1, Pallas kernels: 16.6 us -> 14.5 us  [near_field(): pl.pallas_call(near_kernel, name='near', out_shape=(pltpu.HBM((16, count)...]
    pallas_call x1, Pallas kernels: 5.43 us -> 3.77 us  [upward(): pl.pallas_call(upward_kernel, name='upward', out_shape=(jax.ShapeDtypeStr...]
where the time goes in v4:
time: 66.1 us; the launch traced here: 65.4 us
  Pallas kernels  30.1 us (46%)
  starting transfers between devices  26.8 us (41%)
  waiting for transfers between devices  8.51 us (13%)
    pallas_call x1, Pallas kernels, near_field(): pl.pallas_call(near_kernel, name='near', out_shape=(pltpu.HBM((16, count)...  14.5 us
    ppermute x4, starting transfers between devices, shifted(): lax.ppermute(shard, AXES, [(i, i + by) for i in range(devices) if 0 <= i...  12.2 us
    pallas_call x1, Pallas kernels, finish(): pl.pallas_call(finish_kernel, name='finish', out_shape=jax.ShapeDtypeStru...  10.4 us
    all_to_all x1, starting transfers between devices, local(): lax.all_to_all(coarse, AXES, 0, 0, axis_index_groups=columns, tiled=True)  8.04 us
    all_to_all x1, starting transfers between devices, local(): lax.all_to_all(payload, AXES, 0, 0, axis_index_groups=rows, tiled=True)  6.51 us
    all_to_all x1, waiting for transfers between devices, local(): lax.all_to_all(payload, AXES, 0, 0, axis_index_groups=rows, tiled=True)  6.18 us
    pallas_call x1, Pallas kernels, upward(): pl.pallas_call(upward_kernel, name='upward', out_shape=(jax.ShapeDtypeStr...  3.77 us
    ppermute x4, waiting for transfers between devices, shifted(): lax.ppermute(shard, AXES, [(i, i + by) for i in range(devices) if 0 <= i...  2.18 us
  transfers between devices with their start and end apart: 6, of which 3 were waited for; matrix products, arithmetic and copies ran while one was open for 0% of the time, Pallas kernels for 24%

profile of v4, /device:TPU:1, one launch (start us, length us, event | category | flops | bytes accessed | tf_op | source)
XLA Modules:
  0.0 65.4 jit_solution(3483161583743138068)
XLA Ops:
  0.0 3.8 %upward.1 = (bf16[32,4096]{1,0:T(8,128)(2,1)S(1)}, bf16[32,1024]{1,0:T(8,128)(2,1)S(1)}, bf16[32,1024]{1,0:T(8,128)(2,1)S(1)}, bf16[8,8,16,128]{3,2,1,0:T(8,128)...) custom-call(s32[1]{0:T(128)} %bitcast.column_ref, ...), custom_call_target="tpu_custom_call" | custom-call | flops 20000000 | bytes 4194304 | tf_op jit(solution)/shard_map/upward/pallas_call | solution.py:120
  3.8 4.4 %collective-permute-start = (bf16[8,8,16,128]{3,2,1,0:T(8,128)(2,1)S(1)}, bf16[8,8,16,128]{3,2,1,0:T(8,128)(2,1)S(1)}, u32[]{:S(2)}, u32[]{:S(2)}) collective-permute-start(bf16[8,8,16,128]{3,2,1,0:T(8,128)(2,1)S(1)} %get-tuple-element.19), channel_id=1, source_target_pairs={{0,8},{1,9},{2,10},{3,11},{4,12},{5,13},{6,14},{7,15},{8,16},{9,17... | collective-permute-start | bytes 786440 | tf_op jit(solution)/shard_map/ppermute | solution.py:443
  8.2 1.3 %collective-permute-start.1 = (bf16[8,8,16,128]{3,2,1,0:T(8,128)(2,1)S(1)}, bf16[8,8,16,128]{3,2,1,0:T(8,128)(2,1)S(1)}, u32[]{:S(2)}, u32[]{:S(2)}) collective-permute-start(bf16[8,8,16,128]{3,2,1,0:T(8,128)(2,1)S(1)} %get-tuple-element.20), channel_id=1, source_target_pairs={{8,0},{9,1},{10,2},{11,3},{12,4},{13,5},{14,6},{15,7},{16,8},{17,9... | collective-permute-start | bytes 786440 | tf_op jit(solution)/shard_map/ppermute | solution.py:443
  9.5 8.0 %all-to-all-start = ((bf16[16,2,16,128]{3,2,1,0:T(8,128)(2,1)}), bf16[16,2,16,128]{3,2,1,0:T(8,128)(2,1)S(1)}, u32[]{:S(2)}, u32[]{:S(2)}) async-start(bf16[16,2,16,128]{3,2,1,0:T(8,128)(2,1)} %get-tuple-element.21), calls=%async_computation | async-start | bytes 262144 | tf_op jit(solution)/shard_map/all_to_all | solution.py:457
  17.5 4.6 %collective-permute-start.2 = (bf16[32,1024]{1,0:T(8,128)(2,1)S(1)}, bf16[32,1024]{1,0:T(8,128)(2,1)S(1)}, u32[]{:S(2)}, u32[]{:S(2)}) collective-permute-start(bf16[32,1024]{1,0:T(8,128)(2,1)S(1)} %get-tuple-element.22), channel_id=1, source_target_pairs={{0,1},{1,2},{2,3},{3,4},{4,5},{5,6},{6,7},{7,8},{8,9},{9,10},{10,1... | collective-permute-start | bytes 196616 | tf_op jit(solution)/shard_map/ppermute | solution.py:443
  22.1 1.9 %collective-permute-start.3 = (bf16[32,1024]{1,0:T(8,128)(2,1)S(1)}, bf16[32,1024]{1,0:T(8,128)(2,1)S(1)}, u32[]{:S(2)}, u32[]{:S(2)}) collective-permute-start(bf16[32,1024]{1,0:T(8,128)(2,1)S(1)} %get-tuple-element.23), channel_id=1, source_target_pairs={{1,0},{2,1},{3,2},{4,3},{5,4},{6,5},{7,6},{8,7},{9,8},{10,9},{11,1... | collective-permute-start | bytes 196616 | tf_op jit(solution)/shard_map/ppermute | solution.py:443
  24.1 0.2 all-to-all-done.coarse_ref
  24.2 0.0 collective-permute-done.below_ref
  24.2 0.0 collective-permute-done.1.above_ref
  24.2 1.3 %assemble.1 = bf16[8,48,16,128]{3,2,1,0:T(8,128)(2,1)} custom-call(s32[1]{0:T(128)} %bitcast.column_ref, bf16[8,8,16,128]{3,2,1,0:T(8,128)(2,1)S(1)} %get-tuple-element.18.own_ref, bf16[8,8,16,128]{3,2,1,0:T(8,128)(2,1)S(1)} %collective-permute-done.below_ref, bf16[8,8,16,128]{3,2,1,0:T(8,128)(2,1)S(1)} %collective-permute-done.1.above_ref, ...), custom_call_target="tpu_custom_call" | custom-call | bytes 3145728 | tf_op jit(solution)/shard_map/assemble/pallas_call | solution.py:318
  25.5 0.0 collective-permute-done.2.below_ref
  25.5 2.2 %collective-permute-done.3.above_ref = bf16[32,1024]{1,0:T(8,128)(2,1)S(1)} collective-permute-done((bf16[32,1024]{1,0:T(8,128)(2,1)S(1)}, bf16[32,1024]{1,0:T(8,128)(2,1)S(1)}, u32[]{:S(2)}, u32[]{:S(2)}) %collective-permute-start.3) | collective-permute-done | bytes 65568 | tf_op jit(solution)/shard_map/ppermute | solution.py:443
  27.7 6.5 %all-to-all-start.1 = ((bf16[8,48,16,128]{3,2,1,0:T(8,128)(2,1)}), bf16[8,48,16,128]{3,2,1,0:T(8,128)(2,1)S(1)}, u32[]{:S(2)}, u32[]{:S(2)}) async-start(bf16[8,48,16,128]{3,2,1,0:T(8,128)(2,1)} %assemble.1), calls=%async_computation.1 | async-start | bytes 3145728 | tf_op jit(solution)/shard_map/all_to_all | solution.py:464
  34.2 14.5 %near.1 = (f32[16,4096]{1,0:T(8,128)}, bf16[32,64,2048]{2,1,0:T(8,128)(2,1)}, bf16[4,64,2048]{2,1,0:T(8,128)(2,1)S(1)}) custom-call(s32[13,32]{1,0:T(8,128)} %bitcast.8, bf16[32,4096]{1,0:T(8,128)(2,1)S(1)} %get-tuple-element.25.pack_ref, bf16[32,1024]{1,0:T(8,128)(2,1)S(1)} %collective-permute-done.2.below_ref, ...), custom_call_target="tpu_custom_call" | custom-call | flops 654311424 | bytes 20971520 | tf_op jit(solution)/shard_map/near/pallas_call | solution.py:270
  48.8 6.2 %all-to-all-done.1.swapped_ref = bf16[8,48,16,128]{3,2,1,0:T(8,128)(2,1)S(1)} async-done(((bf16[8,48,16,128]{3,2,1,0:T(8,128)(2,1)}), bf16[8,48,16,128]{3,2,1,0:T(8,128)(2,1)S(1)}, u32[]{:S(2)}, u32[]{:S(2)}) %all-to-all-start.1) | async-done | bytes 1572896 | tf_op jit(solution)/shard_map/all_to_all | solution.py:464
  55.0 10.4 %finish.1 = f32[16,4096]{1,0:T(8,128)} custom-call(s32[1]{0:T(128)} %bitcast.column_ref, s32[32,32]{1,0:T(8,128)} %leaf_hbm.1, s32[4,32]{1,0:T(4,128)} %group_hbm.1, bf16[8,48,16,128]{3,2,1,0:T(8,128)(2,1)S(1)} %all-to-all-done.1.swapped_ref, bf16[8,8,16,128]{3,2,1,0:T(8,128)(2,1)S(1)} %collective-permute-done.below_ref, ...), custom_call_target="tpu_custom_call" | custom-call | flops 200000000 | bytes 4194304 | tf_op jit(solution)/shard_map/finish/pallas_call | solution.py:417
Async XLA Ops:
  3.8 20.4 %collective-permute-start = (bf16[8,8,16,128]{3,2,1,0:T(8,128)(2,1)S(1)}, bf16[8,8,16,128]{3,2,1,0:T(8,128)(2,1)S(1)}, u32[]{:S(2)}, u32[]{:S(2)}) collective-permute-start(bf16[8,8,16,128]{3,2,1,0:T(8,128)(2,1)S(1)} %get-tuple-element.19), channel_id=1, source_target_pairs={{0,8},{1,9},{2,10},{3,11},{4,12},{5,13},{6,14},{7,15},{8,16},{9,17... | collective-permute-start | bytes 786440 | tf_op jit(solution)/shard_map/ppermute | solution.py:443
  8.2 16.0 %collective-permute-start.1 = (bf16[8,8,16,128]{3,2,1,0:T(8,128)(2,1)S(1)}, bf16[8,8,16,128]{3,2,1,0:T(8,128)(2,1)S(1)}, u32[]{:S(2)}, u32[]{:S(2)}) collective-permute-start(bf16[8,8,16,128]{3,2,1,0:T(8,128)(2,1)S(1)} %get-tuple-element.20), channel_id=1, source_target_pairs={{8,0},{9,1},{10,2},{11,3},{12,4},{13,5},{14,6},{15,7},{16,8},{17,9... | collective-permute-start | bytes 786440 | tf_op jit(solution)/shard_map/ppermute | solution.py:443
  9.5 14.7 %all-to-all-start = ((bf16[16,2,16,128]{3,2,1,0:T(8,128)(2,1)}), bf16[16,2,16,128]{3,2,1,0:T(8,128)(2,1)S(1)}, u32[]{:S(2)}, u32[]{:S(2)}) async-start(bf16[16,2,16,128]{3,2,1,0:T(8,128)(2,1)} %get-tuple-element.21), calls=%async_computation | async-start | bytes 262144 | tf_op jit(solution)/shard_map/all_to_all | solution.py:457
  17.5 8.0 %collective-permute-start.2 = (bf16[32,1024]{1,0:T(8,128)(2,1)S(1)}, bf16[32,1024]{1,0:T(8,128)(2,1)S(1)}, u32[]{:S(2)}, u32[]{:S(2)}) collective-permute-start(bf16[32,1024]{1,0:T(8,128)(2,1)S(1)} %get-tuple-element.22), channel_id=1, source_target_pairs={{0,1},{1,2},{2,3},{3,4},{4,5},{5,6},{6,7},{7,8},{8,9},{9,10},{10,1... | collective-permute-start | bytes 196616 | tf_op jit(solution)/shard_map/ppermute | solution.py:443
  22.1 5.6 %collective-permute-start.3 = (bf16[32,1024]{1,0:T(8,128)(2,1)S(1)}, bf16[32,1024]{1,0:T(8,128)(2,1)S(1)}, u32[]{:S(2)}, u32[]{:S(2)}) collective-permute-start(bf16[32,1024]{1,0:T(8,128)(2,1)S(1)} %get-tuple-element.23), channel_id=1, source_target_pairs={{1,0},{2,1},{3,2},{4,3},{5,4},{6,5},{7,6},{8,7},{9,8},{10,9},{11,1... | collective-permute-start | bytes 196616 | tf_op jit(solution)/shard_map/ppermute | solution.py:443
  27.7 27.2 %all-to-all-start.1 = ((bf16[8,48,16,128]{3,2,1,0:T(8,128)(2,1)}), bf16[8,48,16,128]{3,2,1,0:T(8,128)(2,1)S(1)}, u32[]{:S(2)}, u32[]{:S(2)}) async-start(bf16[8,48,16,128]{3,2,1,0:T(8,128)(2,1)} %assemble.1), calls=%async_computation.1 | async-start | bytes 3145728 | tf_op jit(solution)/shard_map/all_to_all | solution.py:464

commit v5 on v4

--- a/solution.py
+++ b/solution.py
@@ -145,20 +145,26 @@
 
 
 def near_kernel(
-    offsets_hbm, pack_ref, below_ref, above_ref, coupling_hbm, coarse_hbm,
+    first, edge, offsets_hbm, pack_ref, below_ref, above_ref, coupling_hbm, coarse_hbm,
     near_hbm, packed_hbm, packed_coarse_ref,
     offsets_ref, near_ref, left_ref, right_ref, wide_ref, buffer_ref, packed_ref, coarse_ref,
     sems, out_sems, more_sems,
 ):
     rim = REACH * 128
     inner = pack_ref.shape[1]
-    leaves, tiles = coupling_hbm.shape[:2]
+    all_leaves, tiles = coupling_hbm.shape[:2]
     per_step = buffer_ref.shape[1]
+    leaves = near_ref.shape[1] // 128
     steps = leaves // per_step
+
+    def base(step):
+        if not edge:
+            return first + step * per_step
+        return step * per_step + jnp.where(step < steps // 2, 0, all_leaves - leaves)
 
     def fetch(step, slot):
         return [
-            pltpu.make_async_copy(coupling_hbm.at[step * per_step + i], buffer_ref.at[slot, i], sems.at[slot, i])
+            pltpu.make_async_copy(coupling_hbm.at[base(step) + i], buffer_ref.at[slot, i], sems.at[slot, i])
             for i in range(per_step)
         ]
 
@@ -169,11 +175,12 @@
         ]
 
     table = pltpu.make_async_copy(offsets_hbm, offsets_ref, more_sems.at[0])
-    upper = pltpu.make_async_copy(coarse_hbm, coarse_ref, more_sems.at[1])
     table.start()
     for copy in fetch(0, 0):
         copy.start()
-    upper.start()
+    if edge:
+        upper = pltpu.make_async_copy(coarse_hbm, coarse_ref, more_sems.at[1])
+        upper.start()
 
     def merged(source, tile):
         return jnp.concatenate([source[tile], source[tile + 1]], axis=1)
@@ -196,7 +203,7 @@
             )
             left_ref[:, pl.ds(start, width)] = left.astype(bf16)
 
-    for part in range(rim // 512):
+    for part in range(rim // 512 if edge else 0):
         build(below_ref, part * 512, part * 512, 512, False)
         build(above_ref, rim + inner + part * 512, part * 512, 512, False)
     for part in range(inner // 512):
@@ -232,54 +239,70 @@
 
         work = [(inside, s) for inside in range(per_step) for s in range(0, slots, 2)]
         totals = [jnp.zeros((16, 128), f32)] * per_step
-        ahead = [squares(step * per_step + inside, s) for inside, s in work[:DEPTH]]
+        ahead = [squares(base(step) + inside, s) for inside, s in work[:DEPTH]]
         for at, (inside, s) in enumerate(work):
-            leaf = step * per_step + inside
+            place = step * per_step + inside
             if at + DEPTH < len(work):
                 later, other = work[at + DEPTH]
-                ahead.append(squares(step * per_step + later, other))
+                ahead.append(squares(base(step) + later, other))
             wide, square = ahead.pop(0)
             totals[inside] += nt(wide, lax.rsqrt(square).astype(bf16))
             for tile in range(s * 2, min(s * 2 + 4, tiles) if s + 2 < slots else tiles, 2):
                 packed_ref[slot, inside, :, tile * 64 : (tile + 2) * 64] = merged(buffer_ref.at[slot, inside], tile)
             if s + 2 >= slots:
-                near_ref[:, pl.ds(pl.multiple_of(leaf * 128, 128), 128)] = totals[inside]
-                flush(step, slot)[inside].start()
+                near_ref[:, pl.ds(pl.multiple_of(place * 128, 128), 128)] = totals[inside]
+                pltpu.make_async_copy(packed_ref.at[slot, inside], packed_hbm.at[place], out_sems.at[slot, inside]).start()
         return carry
 
     lax.fori_loop(0, steps, one_step, 0)
     last = pltpu.make_async_copy(near_ref, near_hbm, more_sems.at[2])
     last.start()
-    upper.wait()
-    for group in range(coarse_ref.shape[0]):
-        for tile in range(0, tiles, 2):
-            packed_coarse_ref[group, :, tile * 64 : (tile + 2) * 64] = merged(coarse_ref.at[group], tile)
+    if edge:
+        upper.wait()
+        for group in range(coarse_ref.shape[0]):
+            for tile in range(0, tiles, 2):
+                packed_coarse_ref[group, :, tile * 64 : (tile + 2) * 64] = merged(coarse_ref.at[group], tile)
     for step in range(steps - 2, steps):
         for copy in flush(step, step % 2):
             copy.wait()
     last.wait()
 
 
-def near_field(offsets, pack, below, above, coupling, coarse_coupling):
+def inner_kernel(offsets, pack, coupling, near, packed, *scratch):
+    near_kernel(REACH, False, offsets, pack, None, None, coupling, None, near, packed, None, *scratch)
+
+
+def edge_kernel(*refs):
+    near_kernel(0, True, *refs)
+
+
+def near_field(offsets, pack, rims, coupling, coarse_coupling):
     count = pack.shape[1]
     wide = count + 2 * REACH * 128
-    leaves, tiles = coupling.shape[:2]
+    tiles = coupling.shape[1]
+    leaves = coupling.shape[0] - 2 * REACH if rims is None else 2 * REACH
     groups = coarse_coupling.shape[0]
     per_step = 4
-    points = count * offsets.shape[0] * 128
+    points = leaves * 128 * offsets.shape[0] * 128
+    edge = rims is not None
+    out_shape = [pltpu.HBM((16, leaves * 128), f32), pltpu.HBM((leaves, 64, tiles * 64), bf16)]
+    operands = [pinned(offsets), pack] + list(rims or ()) + [pinned(coupling)]
+    in_specs = [HBM] + [VMEM] * (len(operands) - 2) + [HBM]
+    out_specs = [HBM, HBM]
+    if edge:
+        out_shape.append(pltpu.VMEM((groups, 64, tiles * 64), bf16))
+        out_specs.append(VMEM)
+        operands.append(pinned(coarse_coupling))
+        in_specs.append(HBM)
     return pl.pallas_call(
-        near_kernel,
-        name="near",
-        out_shape=(
-            pltpu.HBM((16, count), f32),
-            pltpu.HBM((leaves, 64, tiles * 64), bf16),
-            pltpu.VMEM((groups, 64, tiles * 64), bf16),
-        ),
-        in_specs=[HBM, VMEM, VMEM, VMEM, HBM, HBM],
-        out_specs=[HBM, HBM, VMEM],
+        edge_kernel if edge else inner_kernel,
+        name="near_edge" if edge else "near_inner",
+        out_shape=tuple(out_shape),
+        in_specs=in_specs,
+        out_specs=out_specs,
         scratch_shapes=[
             pltpu.SMEM(offsets.shape, jnp.int32),
-            pltpu.VMEM((16, count), f32),
+            pltpu.VMEM((16, leaves * 128), f32),
             pltpu.VMEM((32, count), bf16),
             pltpu.VMEM((32, wide), bf16),
             pltpu.VMEM((16, wide), bf16),
@@ -291,8 +314,8 @@
             pltpu.SemaphoreType.DMA((3,)),
         ],
         compiler_params=pltpu.CompilerParams(vmem_limit_bytes=16 << 20),
-        cost_estimate=pl.CostEstimate(flops=points * 96, bytes_accessed=20 << 20, transcendentals=points),
-    )(pinned(offsets), pack, below, above, pinned(coupling), pinned(coarse_coupling))
+        cost_estimate=pl.CostEstimate(flops=points * 96, bytes_accessed=14 << 20, transcendentals=points),
+    )(*operands)
 
 
 def assemble_kernel(column_ref, own_ref, below_ref, above_ref, coarse_ref, out_ref):
@@ -340,24 +363,30 @@
 
 def finish_kernel(
     column_ref, leaf_hbm, group_hbm, swapped_ref, below_ref, above_ref, coupling_ref,
-    packed_hbm, transfer_hbm, basis_hbm, near_hbm,
+    inner_hbm, edge_hbm, transfer_hbm, basis_hbm, near_inner_hbm, near_edge_hbm,
     out_ref, leaf_refs, group_refs, packed_ref, near_ref, transfer_ref, basis_ref, table_ref, picked_ref, sems,
 ):
     groups = coupling_ref.shape[0]
     slots = coupling_ref.shape[2] // 64
+    rim = REACH * 128
     copies = [
         pltpu.make_async_copy(source, target, sems.at[i])
         for i, (source, target) in enumerate((
             (group_hbm, group_refs), (leaf_hbm, leaf_refs), (transfer_hbm, transfer_ref), (basis_hbm, basis_ref),
-            (near_hbm, near_ref),
+            (near_inner_hbm, near_ref.at[:, rim:-rim]), (near_edge_hbm.at[:, :rim], near_ref.at[:, :rim]),
+            (near_edge_hbm.at[:, rim:], near_ref.at[:, -rim:]),
         ))
     ]
-    chunks = [
-        pltpu.make_async_copy(packed_hbm.at[pl.ds(i * 4, 4)], packed_ref.at[pl.ds(i * 4, 4)], sems.at[5 + i])
-        for i in range(2 * groups)
-    ]
-    copies[2:2] = chunks
-    for copy in copies:
+    chunks = []
+    for i in range(2 * groups):
+        if i < 2:
+            source = edge_hbm.at[pl.ds(i * 4, 4)]
+        elif i < 2 * groups - 2:
+            source = inner_hbm.at[pl.ds(i * 4 - REACH, 4)]
+        else:
+            source = edge_hbm.at[pl.ds(i * 4 - 8 * groups + 2 * REACH, 4)]
+        chunks.append(pltpu.make_async_copy(source, packed_ref.at[pl.ds(i * 4, 4)], sems.at[7 + i]))
+    for copy in copies[:2] + chunks[:4] + copies[2:]:
         copy.start()
     mask = low_half((16, 128))
     column = column_ref[0]
@@ -397,11 +426,13 @@
         nt(paired(slots, lambda s: both[group][s]), coupling_ref[group]).astype(bf16) for group in range(groups)
     ]
     copies[1].wait()
-    for copy in copies[2 + len(chunks):]:
+    for copy in copies[2:]:
         copy.wait()
     for group in range(groups):
         chunks[2 * group].wait()
         chunks[2 * group + 1].wait()
+        for copy in chunks[2 * group + 4 : 2 * group + 6]:
+            copy.start()
         leaves = range(group * 8, group * 8 + 8)
         fields = [nt(paired(slots, lambda s: table_ref[leaf_refs[leaf, s]]), packed_ref[leaf]) for leaf in leaves]
         passed = [nt(local1[group], transfer_ref[leaf]) for leaf in leaves]
@@ -411,31 +442,32 @@
             out_ref[:, span] = near_ref[:, span] + jnp.dot(field, basis_ref[leaf], preferred_element_type=f32)
 
 
-def finish(column, leaf_refs, group_refs, swapped, below, above, packed, coupling, transfer, basis, near):
+def finish(column, leaf_refs, group_refs, swapped, below, above, inner, edge, coupling, transfer, basis, near_inner, near_edge):
     groups = coupling.shape[0]
-    slots = leaf_refs.shape[1]
+    leaves, slots = leaf_refs.shape
+    shape = (16, near_inner.shape[1] + near_edge.shape[1])
     return pl.pallas_call(
         finish_kernel,
         name="finish",
-        out_shape=jax.ShapeDtypeStruct(near.shape, f32),
-        in_specs=[SMEM] + [HBM] * 2 + [VMEM] * 4 + [HBM] * 4,
+        out_shape=jax.ShapeDtypeStruct(shape, f32),
+        in_specs=[SMEM] + [HBM] * 2 + [VMEM] * 4 + [HBM] * 6,
         out_specs=VMEM,
         scratch_shapes=[
             pltpu.SMEM(leaf_refs.shape, jnp.int32),
             pltpu.SMEM(group_refs.shape, jnp.int32),
-            pltpu.VMEM(packed.shape, bf16),
-            pltpu.VMEM(near.shape, f32),
+            pltpu.VMEM((leaves,) + inner.shape[1:], bf16),
+            pltpu.VMEM(shape, f32),
             pltpu.VMEM(transfer.shape, bf16),
             pltpu.VMEM(basis.shape, bf16),
             pltpu.VMEM(((2 * WINDOW + 1) * 16, 16, 128), bf16),
             pltpu.VMEM((groups * slots, 16, 128), bf16),
-            pltpu.SemaphoreType.DMA((5 + 2 * groups,)),
+            pltpu.SemaphoreType.DMA((7 + 2 * groups,)),
         ],
         compiler_params=pltpu.CompilerParams(vmem_limit_bytes=20 << 20),
         cost_estimate=pl.CostEstimate(flops=200_000_000, bytes_accessed=4 << 20, transcendentals=0),
     )(
         column, pinned(leaf_refs), pinned(group_refs), swapped, below, above,
-        kept(coupling), pinned(packed), pinned(transfer), pinned(basis), pinned(near),
+        kept(coupling), *(pinned(x) for x in (inner, edge, transfer, basis, near_inner, near_edge)),
     )
 
 
@@ -458,16 +490,16 @@
     lists_below = shifted(up, ROW, devices)
     lists_above = shifted(down, -ROW, devices)
     from_below = shifted(rim_last, 1, devices)
-    from_above = shifted(rim_first, -1, devices)
     payload = assemble(column, own, lists_below, lists_above, coarse_rows)
-    payload, from_below, from_above = lax.optimization_barrier((payload, from_below, from_above))
+    payload, from_below, rim_first, pack = lax.optimization_barrier((payload, from_below, rim_first, pack))
     swapped = lax.all_to_all(payload, AXES, 0, 0, axis_index_groups=rows, tiled=True)
-    near, packed, packed_coarse = near_field(
-        near_offsets.T, pack, from_below, from_above, leaf_coupling, coarse_coupling
-    )
+    rims = (from_below, shifted(rim_first, -1, devices))
+    offsets = near_offsets.T
+    near_inner, inner = near_field(offsets, pack, None, leaf_coupling, coarse_coupling)
+    near_edge, edge, packed_coarse = near_field(offsets, pack, rims, leaf_coupling, coarse_coupling)
     return finish(
-        column, relay_refs, coarse_refs, swapped, lists_below, lists_above, packed, packed_coarse, transfer,
-        leaf_basis, near,
+        column, relay_refs, coarse_refs, swapped, lists_below, lists_above, inner, edge, packed_coarse, transfer,
+        leaf_basis, near_inner, near_edge,
     )
 
 

time: 66.1 us -> 71.4 us (1.080)
  waiting for transfers between devices: 8.51 us -> 12.2 us
  Pallas kernels: 30.1 us -> 31.1 us
    ppermute x4, waiting for transfers between devices: 2.18 us -> 10.1 us  [shifted(): lax.ppermute(shard, AXES, [(i, i + by) for i in range(devices) if 0 <= i...]
    all_to_all x1, waiting for transfers between devices: 6.18 us -> 0.01 us  [local(): lax.all_to_all(payload, AXES, 0, 0, axis_index_groups=rows, tiled=True)]
    pallas_call x1 -> x2, Pallas kernels: 14.5 us -> 16.8 us  [near_field(): pl.pallas_call(edge_kernel if edge else inner_kernel, name='near_edge' if...]
    all_to_all x1, waiting for transfers between devices: 0.15 us -> 2.08 us  [local(): lax.all_to_all(coarse, AXES, 0, 0, axis_index_groups=columns, tiled=True)]
    pallas_call x1, Pallas kernels: 10.4 us -> 9.23 us  [finish(): pl.pallas_call(finish_kernel, name='finish', out_shape=jax.ShapeDtypeStru...]
  transfers between devices with their start and end apart: 6 -> 6, of which waited for: 3 -> 2; matrix products, arithmetic and copies ran while one was open for 0% -> 0% of each run, Pallas kernels for 24% -> 26%
where the time goes in v5:
time: 71.4 us; the launch traced here: 70.8 us
  Pallas kernels  31.1 us (44%)
  starting transfers between devices  27.4 us (38%)
  waiting for transfers between devices  12.2 us (17%)
    pallas_call x2, Pallas kernels, near_field(): pl.pallas_call(edge_kernel if edge else inner_kernel, name='near_edge' if...  16.8 us
    ppermute x4, starting transfers between devices, shifted(): lax.ppermute(shard, AXES, [(i, i + by) for i in range(devices) if 0 <= i...  12.2 us
    ppermute x4, waiting for transfers between devices, shifted(): lax.ppermute(shard, AXES, [(i, i + by) for i in range(devices) if 0 <= i...  10.1 us
    pallas_call x1, Pallas kernels, finish(): pl.pallas_call(finish_kernel, name='finish', out_shape=jax.ShapeDtypeStru...  9.23 us
    all_to_all x1, starting transfers between devices, local(): lax.all_to_all(coarse, AXES, 0, 0, axis_index_groups=columns, tiled=True)  8.04 us
    all_to_all x1, starting transfers between devices, local(): lax.all_to_all(payload, AXES, 0, 0, axis_index_groups=rows, tiled=True)  7.14 us
    pallas_call x1, Pallas kernels, upward(): pl.pallas_call(upward_kernel, name='upward', out_shape=(jax.ShapeDtypeStr...  3.77 us
    all_to_all x1, waiting for transfers between devices, local(): lax.all_to_all(coarse, AXES, 0, 0, axis_index_groups=columns, tiled=True)  2.08 us
  transfers between devices with their start and end apart: 6, of which 2 were waited for; matrix products, arithmetic and copies ran while one was open for 0% of the time, Pallas kernels for 26%

profile of v5, /device:TPU:1, one launch (start us, length us, event | category | flops | bytes accessed | tf_op | source)
XLA Modules:
  0.0 70.8 jit_solution(6138499039526791872)
XLA Ops:
  0.0 3.8 %upward.1 = (bf16[32,4096]{1,0:T(8,128)(2,1)S(1)}, bf16[32,1024]{1,0:T(8,128)(2,1)S(1)}, bf16[32,1024]{1,0:T(8,128)(2,1)S(1)}, bf16[8,8,16,128]{3,2,1,0:T(8,128)...) custom-call(s32[1]{0:T(128)} %bitcast.column_ref, ...), custom_call_target="tpu_custom_call" | custom-call | flops 20000000 | bytes 4194304 | tf_op jit(solution)/shard_map/upward/pallas_call | solution.py:120
  3.8 4.4 %collective-permute-start = (bf16[8,8,16,128]{3,2,1,0:T(8,128)(2,1)S(1)}, bf16[8,8,16,128]{3,2,1,0:T(8,128)(2,1)S(1)}, u32[]{:S(2)}, u32[]{:S(2)}) collective-permute-start(bf16[8,8,16,128]{3,2,1,0:T(8,128)(2,1)S(1)} %get-tuple-element.22), channel_id=1, source_target_pairs={{0,8},{1,9},{2,10},{3,11},{4,12},{5,13},{6,14},{7,15},{8,16},{9,17... | collective-permute-start | bytes 786440 | tf_op jit(solution)/shard_map/ppermute | solution.py:475
  8.2 1.3 %collective-permute-start.1 = (bf16[8,8,16,128]{3,2,1,0:T(8,128)(2,1)S(1)}, bf16[8,8,16,128]{3,2,1,0:T(8,128)(2,1)S(1)}, u32[]{:S(2)}, u32[]{:S(2)}) collective-permute-start(bf16[8,8,16,128]{3,2,1,0:T(8,128)(2,1)S(1)} %get-tuple-element.23), channel_id=1, source_target_pairs={{8,0},{9,1},{10,2},{11,3},{12,4},{13,5},{14,6},{15,7},{16,8},{17,9... | collective-permute-start | bytes 786440 | tf_op jit(solution)/shard_map/ppermute | solution.py:475
  9.5 8.0 %all-to-all-start = ((bf16[16,2,16,128]{3,2,1,0:T(8,128)(2,1)}), bf16[16,2,16,128]{3,2,1,0:T(8,128)(2,1)S(1)}, u32[]{:S(2)}, u32[]{:S(2)}) async-start(bf16[16,2,16,128]{3,2,1,0:T(8,128)(2,1)} %get-tuple-element.24), calls=%async_computation | async-start | bytes 262144 | tf_op jit(solution)/shard_map/all_to_all | solution.py:489
  17.5 4.6 %collective-permute-start.2 = (bf16[32,1024]{1,0:T(8,128)(2,1)S(1)}, bf16[32,1024]{1,0:T(8,128)(2,1)S(1)}, u32[]{:S(2)}, u32[]{:S(2)}) collective-permute-start(bf16[32,1024]{1,0:T(8,128)(2,1)S(1)} %get-tuple-element.25), channel_id=1, source_target_pairs={{0,1},{1,2},{2,3},{3,4},{4,5},{5,6},{6,7},{7,8},{8,9},{9,10},{10,1... | collective-permute-start | bytes 196616 | tf_op jit(solution)/shard_map/ppermute | solution.py:475
  22.1 2.1 %all-to-all-done.coarse_ref = bf16[16,2,16,128]{3,2,1,0:T(8,128)(2,1)S(1)} async-done(((bf16[16,2,16,128]{3,2,1,0:T(8,128)(2,1)}), bf16[16,2,16,128]{3,2,1,0:T(8,128)(2,1)S(1)}, u32[]{:S(2)}, u32[]{:S(2)}) %all-to-all-start) | async-done | bytes 131104 | tf_op jit(solution)/shard_map/all_to_all | solution.py:489
  24.2 0.0 collective-permute-done.below_ref
  24.2 0.0 collective-permute-done.1.above_ref
  24.2 1.3 %assemble.1 = bf16[8,48,16,128]{3,2,1,0:T(8,128)(2,1)} custom-call(s32[1]{0:T(128)} %bitcast.column_ref, bf16[8,8,16,128]{3,2,1,0:T(8,128)(2,1)S(1)} %get-tuple-element.21.own_ref, bf16[8,8,16,128]{3,2,1,0:T(8,128)(2,1)S(1)} %collective-permute-done.below_ref, bf16[8,8,16,128]{3,2,1,0:T(8,128)(2,1)S(1)} %collective-permute-done.1.above_ref, ...), custom_call_target="tpu_custom_call" | custom-call | bytes 3145728 | tf_op jit(solution)/shard_map/assemble/pallas_call | solution.py:341
  25.5 0.0 collective-permute-done.2.refs_2_
  25.5 7.1 %all-to-all-start.1 = ((bf16[8,48,16,128]{3,2,1,0:T(8,128)(2,1)}), bf16[8,48,16,128]{3,2,1,0:T(8,128)(2,1)S(1)}, u32[]{:S(2)}, u32[]{:S(2)}) async-start(bf16[8,48,16,128]{3,2,1,0:T(8,128)(2,1)} %assemble.1), calls=%async_computation.1 | async-start | bytes 3145728 | tf_op jit(solution)/shard_map/all_to_all | solution.py:495
  32.7 1.9 %collective-permute-start.3 = (bf16[32,1024]{1,0:T(8,128)(2,1)S(1)}, bf16[32,1024]{1,0:T(8,128)(2,1)S(1)}, u32[]{:S(2)}, u32[]{:S(2)}) collective-permute-start(bf16[32,1024]{1,0:T(8,128)(2,1)S(1)} %get-tuple-element.31), channel_id=1, source_target_pairs={{1,0},{2,1},{3,2},{4,3},{5,4},{6,5},{7,6},{8,7},{9,8},{10,9},{11,1... | collective-permute-start | bytes 196616 | tf_op jit(solution)/shard_map/ppermute | solution.py:475
  34.6 8.3 %near_inner.1 = (f32[16,2048]{1,0:T(8,128)}, bf16[16,64,2048]{2,1,0:T(8,128)(2,1)}) custom-call(s32[13,32]{1,0:T(8,128)} %bitcast.6, bf16[32,4096]{1,0:T(8,128)(2,1)S(1)} %get-tuple-element.29.refs_1_.pack, bf16[32,32,64,64]{3,2,1,0:T(8,128)(2,1)} %coupling.1), custom_call_target="tpu_custom_call" | custom-call | flops 327155712 | bytes 14680064 | tf_op jit(solution)/shard_map/near_inner/pallas_call | solution.py:297
  42.9 10.1 %collective-permute-done.3.refs_3_ = bf16[32,1024]{1,0:T(8,128)(2,1)S(1)} collective-permute-done((bf16[32,1024]{1,0:T(8,128)(2,1)S(1)}, bf16[32,1024]{1,0:T(8,128)(2,1)S(1)}, u32[]{:S(2)}, u32[]{:S(2)}) %collective-permute-start.3) | collective-permute-done | bytes 65568 | tf_op jit(solution)/shard_map/ppermute | solution.py:475
  53.1 8.5 %near_edge.1 = (f32[16,2048]{1,0:T(8,128)}, bf16[16,64,2048]{2,1,0:T(8,128)(2,1)}, bf16[4,64,2048]{2,1,0:T(8,128)(2,1)S(1)}) custom-call(s32[13,32]{1,0:T(8,128)} %bitcast.7, bf16[32,4096]{1,0:T(8,128)(2,1)S(1)} %get-tuple-element.29.refs_1_.pack, bf16[32,1024]{1,0:T(8,128)(2,1)S(1)} %collective-permute-done.2.refs_2_, ...), custom_call_target="tpu_custom_call" | custom-call | flops 327155712 | bytes 14680064 | tf_op jit(solution)/shard_map/near_edge/pallas_call | solution.py:297
  61.5 0.0 all-to-all-done.1.swapped_ref
  61.6 9.2 %finish.1 = f32[16,4096]{1,0:T(8,128)} custom-call(s32[1]{0:T(128)} %bitcast.column_ref, s32[32,32]{1,0:T(8,128)} %leaf_hbm.1, s32[4,32]{1,0:T(4,128)} %group_hbm.1, bf16[8,48,16,128]{3,2,1,0:T(8,128)(2,1)S(1)} %all-to-all-done.1.swapped_ref, bf16[8,8,16,128]{3,2,1,0:T(8,128)(2,1)S(1)} %collective-permute-done.below_ref, ...), custom_call_target="tpu_custom_call" | custom-call | flops 200000000 | bytes 4194304 | tf_op jit(solution)/shard_map/finish/pallas_call | solution.py:449
Async XLA Ops:
  3.8 20.4 %collective-permute-start = (bf16[8,8,16,128]{3,2,1,0:T(8,128)(2,1)S(1)}, bf16[8,8,16,128]{3,2,1,0:T(8,128)(2,1)S(1)}, u32[]{:S(2)}, u32[]{:S(2)}) collective-permute-start(bf16[8,8,16,128]{3,2,1,0:T(8,128)(2,1)S(1)} %get-tuple-element.22), channel_id=1, source_target_pairs={{0,8},{1,9},{2,10},{3,11},{4,12},{5,13},{6,14},{7,15},{8,16},{9,17... | collective-permute-start | bytes 786440 | tf_op jit(solution)/shard_map/ppermute | solution.py:475
  8.2 16.0 %collective-permute-start.1 = (bf16[8,8,16,128]{3,2,1,0:T(8,128)(2,1)S(1)}, bf16[8,8,16,128]{3,2,1,0:T(8,128)(2,1)S(1)}, u32[]{:S(2)}, u32[]{:S(2)}) collective-permute-start(bf16[8,8,16,128]{3,2,1,0:T(8,128)(2,1)S(1)} %get-tuple-element.23), channel_id=1, source_target_pairs={{8,0},{9,1},{10,2},{11,3},{12,4},{13,5},{14,6},{15,7},{16,8},{17,9... | collective-permute-start | bytes 786440 | tf_op jit(solution)/shard_map/ppermute | solution.py:475
  9.5 14.7 %all-to-all-start = ((bf16[16,2,16,128]{3,2,1,0:T(8,128)(2,1)}), bf16[16,2,16,128]{3,2,1,0:T(8,128)(2,1)S(1)}, u32[]{:S(2)}, u32[]{:S(2)}) async-start(bf16[16,2,16,128]{3,2,1,0:T(8,128)(2,1)} %get-tuple-element.24), calls=%async_computation | async-start | bytes 262144 | tf_op jit(solution)/shard_map/all_to_all | solution.py:489
  17.5 8.0 %collective-permute-start.2 = (bf16[32,1024]{1,0:T(8,128)(2,1)S(1)}, bf16[32,1024]{1,0:T(8,128)(2,1)S(1)}, u32[]{:S(2)}, u32[]{:S(2)}) collective-permute-start(bf16[32,1024]{1,0:T(8,128)(2,1)S(1)} %get-tuple-element.25), channel_id=1, source_target_pairs={{0,1},{1,2},{2,3},{3,4},{4,5},{5,6},{6,7},{7,8},{8,9},{9,10},{10,1... | collective-permute-start | bytes 196616 | tf_op jit(solution)/shard_map/ppermute | solution.py:475
  25.5 36.0 %all-to-all-start.1 = ((bf16[8,48,16,128]{3,2,1,0:T(8,128)(2,1)}), bf16[8,48,16,128]{3,2,1,0:T(8,128)(2,1)S(1)}, u32[]{:S(2)}, u32[]{:S(2)}) async-start(bf16[8,48,16,128]{3,2,1,0:T(8,128)(2,1)} %assemble.1), calls=%async_computation.1 | async-start | bytes 3145728 | tf_op jit(solution)/shard_map/all_to_all | solution.py:495
  32.7 20.4 %collective-permute-start.3 = (bf16[32,1024]{1,0:T(8,128)(2,1)S(1)}, bf16[32,1024]{1,0:T(8,128)(2,1)S(1)}, u32[]{:S(2)}, u32[]{:S(2)}) collective-permute-start(bf16[32,1024]{1,0:T(8,128)(2,1)S(1)} %get-tuple-element.31), channel_id=1, source_target_pairs={{1,0},{2,1},{3,2},{4,3},{5,4},{6,5},{7,6},{8,7},{9,8},{10,9},{11,1... | collective-permute-start | bytes 196616 | tf_op jit(solution)/shard_map/ppermute | solution.py:475

commit v6 on v5

--- a/solution.py
+++ b/solution.py
@@ -145,9 +145,9 @@
 
 
 def near_kernel(
-    first, edge, offsets_hbm, pack_ref, below_ref, above_ref, coupling_hbm, coarse_hbm,
+    first, edge, offsets_hbm, pack_ref, below_hbm, above_hbm, coupling_hbm, coarse_hbm,
     near_hbm, packed_hbm, packed_coarse_ref,
-    offsets_ref, near_ref, left_ref, right_ref, wide_ref, buffer_ref, packed_ref, coarse_ref,
+    offsets_ref, near_ref, left_ref, right_ref, wide_ref, buffer_ref, packed_ref, coarse_ref, rims_ref,
     sems, out_sems, more_sems,
 ):
     rim = REACH * 128
@@ -176,6 +176,13 @@
 
     table = pltpu.make_async_copy(offsets_hbm, offsets_ref, more_sems.at[0])
     table.start()
+    if edge:
+        rims = [
+            pltpu.make_async_copy(below_hbm, rims_ref.at[0], more_sems.at[3]),
+            pltpu.make_async_copy(above_hbm, rims_ref.at[1], more_sems.at[4]),
+        ]
+        for copy in rims:
+            copy.start()
     for copy in fetch(0, 0):
         copy.start()
     if edge:
@@ -203,11 +210,14 @@
             )
             left_ref[:, pl.ds(start, width)] = left.astype(bf16)
 
-    for part in range(rim // 512 if edge else 0):
-        build(below_ref, part * 512, part * 512, 512, False)
-        build(above_ref, rim + inner + part * 512, part * 512, 512, False)
     for part in range(inner // 512):
         build(pack_ref, rim + part * 512, part * 512, 512, True)
+    if edge:
+        for copy in rims:
+            copy.wait()
+        for part in range(rim // 512):
+            build(rims_ref.at[0], part * 512, part * 512, 512, False)
+            build(rims_ref.at[1], rim + inner + part * 512, part * 512, 512, False)
 
     table.wait()
     slots = offsets_ref.shape[0]
@@ -286,8 +296,8 @@
     points = leaves * 128 * offsets.shape[0] * 128
     edge = rims is not None
     out_shape = [pltpu.HBM((16, leaves * 128), f32), pltpu.HBM((leaves, 64, tiles * 64), bf16)]
-    operands = [pinned(offsets), pack] + list(rims or ()) + [pinned(coupling)]
-    in_specs = [HBM] + [VMEM] * (len(operands) - 2) + [HBM]
+    operands = [pinned(offsets), pack] + [pinned(x) for x in rims or ()] + [pinned(coupling)]
+    in_specs = [HBM, VMEM] + [HBM] * (len(operands) - 2)
     out_specs = [HBM, HBM]
     if edge:
         out_shape.append(pltpu.VMEM((groups, 64, tiles * 64), bf16))
@@ -309,9 +319,10 @@
             pltpu.VMEM((2, per_step) + coupling.shape[1:], bf16),
             pltpu.VMEM((2, per_step, 64, tiles * 64), bf16),
             pltpu.VMEM(coarse_coupling.shape, bf16),
+            pltpu.VMEM((2, 32, REACH * 128), bf16),
             pltpu.SemaphoreType.DMA((2, per_step)),
             pltpu.SemaphoreType.DMA((2, per_step)),
-            pltpu.SemaphoreType.DMA((3,)),
+            pltpu.SemaphoreType.DMA((5,)),
         ],
         compiler_params=pltpu.CompilerParams(vmem_limit_bytes=16 << 20),
         cost_estimate=pl.CostEstimate(flops=points * 96, bytes_accessed=14 << 20, transcendentals=points),
@@ -320,7 +331,6 @@
 
 def assemble_kernel(column_ref, own_ref, below_ref, above_ref, coarse_ref, out_ref):
     column = column_ref[0]
-    rows, pairs = coarse_ref.shape[:2]
     for target in range(out_ref.shape[0]):
         out_ref[target, 0:8] = own_ref[target]
         crossed = jnp.where(target < column, 0, 1)
@@ -333,20 +343,38 @@
         def _():
             out_ref[target, 8:16] = above_ref[target]
 
-        out_ref[target, 16:] = coarse_ref[...].reshape(rows * pairs, 16, 128)
+        out_ref[target, 16:] = coarse_ref[0]
 
 
 def assemble(column, own, below, above, coarse):
-    rows, pairs = coarse.shape[:2]
     return pl.pallas_call(
         assemble_kernel,
         name="assemble",
-        out_shape=jax.ShapeDtypeStruct((ROW, 16 + rows * pairs, 16, 128), bf16),
+        out_shape=jax.ShapeDtypeStruct((ROW, 16 + coarse.shape[1], 16, 128), bf16),
         in_specs=[SMEM] + [VMEM] * 4,
         out_specs=VMEM,
-        compiler_params=pltpu.CompilerParams(vmem_limit_bytes=8 << 20),
-        cost_estimate=pl.CostEstimate(flops=0, bytes_accessed=3 << 20, transcendentals=0),
+        compiler_params=pltpu.CompilerParams(vmem_limit_bytes=4 << 20),
+        cost_estimate=pl.CostEstimate(flops=0, bytes_accessed=1 << 20, transcendentals=0),
     )(column, own, below, above, coarse)
+
+
+def repeat_kernel(swapped_ref, out_ref):
+    pairs = out_ref.shape[2]
+    for owner in range(swapped_ref.shape[0]):
+        tiles = swapped_ref[owner, 16:]
+        out_ref[:, owner] = jnp.broadcast_to(tiles[None], (out_ref.shape[0], pairs, 16, 128))
+
+
+def repeat(swapped, rows):
+    return pl.pallas_call(
+        repeat_kernel,
+        name="repeat",
+        out_shape=jax.ShapeDtypeStruct((rows, ROW, swapped.shape[1] - 16, 16, 128), bf16),
+        in_specs=[VMEM],
+        out_specs=VMEM,
+        compiler_params=pltpu.CompilerParams(vmem_limit_bytes=4 << 20),
+        cost_estimate=pl.CostEstimate(flops=0, bytes_accessed=1 << 20, transcendentals=0),
+    )(swapped)
 
 
 def spread_matrix():
@@ -361,34 +389,26 @@
     return jnp.concatenate([jnp.where(mask, pick(s), pick(s + 1)) for s in range(0, slots, 2)], axis=1)
 
 
-def finish_kernel(
-    column_ref, leaf_hbm, group_hbm, swapped_ref, below_ref, above_ref, coupling_ref,
-    inner_hbm, edge_hbm, transfer_hbm, basis_hbm, near_inner_hbm, near_edge_hbm,
-    out_ref, leaf_refs, group_refs, packed_ref, near_ref, transfer_ref, basis_ref, table_ref, picked_ref, sems,
+def leaf_kernel(
+    column_ref, leaf_hbm, swapped_ref, below_ref, above_ref, inner_hbm, edge_hbm,
+    out_ref, leaf_refs, packed_ref, table_ref, sems,
 ):
-    groups = coupling_ref.shape[0]
-    slots = coupling_ref.shape[2] // 64
-    rim = REACH * 128
-    copies = [
-        pltpu.make_async_copy(source, target, sems.at[i])
-        for i, (source, target) in enumerate((
-            (group_hbm, group_refs), (leaf_hbm, leaf_refs), (transfer_hbm, transfer_ref), (basis_hbm, basis_ref),
-            (near_inner_hbm, near_ref.at[:, rim:-rim]), (near_edge_hbm.at[:, :rim], near_ref.at[:, :rim]),
-            (near_edge_hbm.at[:, rim:], near_ref.at[:, -rim:]),
-        ))
-    ]
+    leaves, slots = leaf_refs.shape
+    size = 4
+    count = leaves // size
+    table = pltpu.make_async_copy(leaf_hbm, leaf_refs, sems.at[count])
+    table.start()
     chunks = []
-    for i in range(2 * groups):
-        if i < 2:
-            source = edge_hbm.at[pl.ds(i * 4, 4)]
-        elif i < 2 * groups - 2:
-            source = inner_hbm.at[pl.ds(i * 4 - REACH, 4)]
+    for i in range(count):
+        if i * size < REACH:
+            source = edge_hbm.at[pl.ds(i * size, size)]
+        elif i * size < leaves - REACH:
+            source = inner_hbm.at[pl.ds(i * size - REACH, size)]
         else:
-            source = edge_hbm.at[pl.ds(i * 4 - 8 * groups + 2 * REACH, 4)]
-        chunks.append(pltpu.make_async_copy(source, packed_ref.at[pl.ds(i * 4, 4)], sems.at[7 + i]))
-    for copy in copies[:2] + chunks[:4] + copies[2:]:
+            source = edge_hbm.at[pl.ds(i * size - leaves + 2 * REACH, size)]
+        chunks.append(pltpu.make_async_copy(source, packed_ref.at[pl.ds(i * size, size)], sems.at[i]))
+    for copy in chunks[:4]:
         copy.start()
-    mask = low_half((16, 128))
     column = column_ref[0]
     spread = spread_matrix()
 
@@ -405,12 +425,56 @@
         owner = place & (ROW - 1)
         crossed = jnp.where((place >= ROW) & (place < 2 * ROW), 0, 8)
         put(window, swapped_ref[owner, pl.ds(pl.multiple_of(crossed, 8), 8)])
-
+    table.wait()
+    for chunk in range(count):
+        chunks[chunk].wait()
+        if chunk + 4 < count:
+            chunks[chunk + 4].start()
+        for leaf in range(chunk * size, (chunk + 1) * size):
+            out_ref[leaf] = nt(paired(slots, lambda s: table_ref[leaf_refs[leaf, s]]), packed_ref[leaf])
+
+
+def leaf_local(column, leaf_refs, swapped, below, above, inner, edge):
+    leaves = leaf_refs.shape[0]
+    return pl.pallas_call(
+        leaf_kernel,
+        name="leaf_local",
+        out_shape=jax.ShapeDtypeStruct((leaves, 16, 64), f32),
+        in_specs=[SMEM, HBM] + [VMEM] * 3 + [HBM] * 2,
+        out_specs=VMEM,
+        scratch_shapes=[
+            pltpu.SMEM(leaf_refs.shape, jnp.int32),
+            pltpu.VMEM((leaves,) + inner.shape[1:], bf16),
+            pltpu.VMEM(((2 * WINDOW + 1) * 16, 16, 128), bf16),
+            pltpu.SemaphoreType.DMA((leaves // 4 + 1,)),
+        ],
+        compiler_params=pltpu.CompilerParams(vmem_limit_bytes=16 << 20),
+        cost_estimate=pl.CostEstimate(flops=140_000_000, bytes_accessed=9 << 20, transcendentals=0),
+    )(column, pinned(leaf_refs), swapped, below, above, pinned(inner), pinned(edge))
+
+
+def downward_kernel(
+    group_hbm, coarse_ref, local_ref, coupling_ref, transfer_hbm, basis_hbm, near_inner_hbm, near_edge_hbm,
+    out_ref, group_refs, transfer_ref, basis_ref, near_ref, picked_ref, sems,
+):
+    groups, slots = group_refs.shape
+    rim = REACH * 128
+    copies = [
+        pltpu.make_async_copy(source, target, sems.at[i])
+        for i, (source, target) in enumerate((
+            (group_hbm, group_refs), (transfer_hbm, transfer_ref), (basis_hbm, basis_ref),
+            (near_inner_hbm, near_ref.at[:, rim:-rim]), (near_edge_hbm.at[:, :rim], near_ref.at[:, :rim]),
+            (near_edge_hbm.at[:, rim:], near_ref.at[:, -rim:]),
+        ))
+    ]
+    for copy in copies:
+        copy.start()
+    mask = low_half((16, 128))
     copies[0].wait()
     for group in range(groups):
         for slot in range(slots):
             ref = group_refs[group, slot]
-            tile = swapped_ref[(ref >> 2) & (ROW - 1), 16 + ((ref >> 5) << 1) + ((ref >> 1) & 1)]
+            tile = coarse_ref[ref >> 5, (ref >> 2) & (ROW - 1), (ref >> 1) & 1]
             keep = mask == ((ref & 1) == 0)
             picked_ref[group * slots + slot] = jnp.where(keep, tile, jnp.zeros_like(tile))
     row = lax.broadcasted_iota(jnp.int32, (128, 128), 0)
@@ -425,49 +489,38 @@
     local1 = [
         nt(paired(slots, lambda s: both[group][s]), coupling_ref[group]).astype(bf16) for group in range(groups)
     ]
-    copies[1].wait()
-    for copy in copies[2:]:
+    for copy in copies[1:]:
         copy.wait()
-    for group in range(groups):
-        chunks[2 * group].wait()
-        chunks[2 * group + 1].wait()
-        for copy in chunks[2 * group + 4 : 2 * group + 6]:
-            copy.start()
-        leaves = range(group * 8, group * 8 + 8)
-        fields = [nt(paired(slots, lambda s: table_ref[leaf_refs[leaf, s]]), packed_ref[leaf]) for leaf in leaves]
-        passed = [nt(local1[group], transfer_ref[leaf]) for leaf in leaves]
-        rounded = [(one + two).astype(bf16) for one, two in zip(fields, passed)]
-        for leaf, field in zip(leaves, rounded):
-            span = slice(leaf * 128, (leaf + 1) * 128)
-            out_ref[:, span] = near_ref[:, span] + jnp.dot(field, basis_ref[leaf], preferred_element_type=f32)
-
-
-def finish(column, leaf_refs, group_refs, swapped, below, above, inner, edge, coupling, transfer, basis, near_inner, near_edge):
-    groups = coupling.shape[0]
-    leaves, slots = leaf_refs.shape
+    leaves = range(groups * 8)
+    passed = [nt(local1[leaf // 8], transfer_ref[leaf]) for leaf in leaves]
+    rounded = [(local_ref[leaf] + one).astype(bf16) for leaf, one in zip(leaves, passed)]
+    for leaf, field in zip(leaves, rounded):
+        span = slice(leaf * 128, (leaf + 1) * 128)
+        out_ref[:, span] = near_ref[:, span] + jnp.dot(field, basis_ref[leaf], preferred_element_type=f32)
+
+
+def downward(group_refs, coarse, local0, coupling, transfer, basis, near_inner, near_edge):
+    groups, slots = group_refs.shape
     shape = (16, near_inner.shape[1] + near_edge.shape[1])
     return pl.pallas_call(
-        finish_kernel,
-        name="finish",
+        downward_kernel,
+        name="downward",
         out_shape=jax.ShapeDtypeStruct(shape, f32),
-        in_specs=[SMEM] + [HBM] * 2 + [VMEM] * 4 + [HBM] * 6,
+        in_specs=[HBM] + [VMEM] * 3 + [HBM] * 4,
         out_specs=VMEM,
         scratch_shapes=[
-            pltpu.SMEM(leaf_refs.shape, jnp.int32),
             pltpu.SMEM(group_refs.shape, jnp.int32),
-            pltpu.VMEM((leaves,) + inner.shape[1:], bf16),
-            pltpu.VMEM(shape, f32),
             pltpu.VMEM(transfer.shape, bf16),
             pltpu.VMEM(basis.shape, bf16),
-            pltpu.VMEM(((2 * WINDOW + 1) * 16, 16, 128), bf16),
+            pltpu.VMEM(shape, f32),
             pltpu.VMEM((groups * slots, 16, 128), bf16),
-            pltpu.SemaphoreType.DMA((7 + 2 * groups,)),
+            pltpu.SemaphoreType.DMA((6,)),
         ],
-        compiler_params=pltpu.CompilerParams(vmem_limit_bytes=20 << 20),
-        cost_estimate=pl.CostEstimate(flops=200_000_000, bytes_accessed=4 << 20, transcendentals=0),
+        compiler_params=pltpu.CompilerParams(vmem_limit_bytes=8 << 20),
+        cost_estimate=pl.CostEstimate(flops=60_000_000, bytes_accessed=4 << 20, transcendentals=0),
     )(
-        column, pinned(leaf_refs), pinned(group_refs), swapped, below, above,
-        kept(coupling), *(pinned(x) for x in (inner, edge, transfer, basis, near_inner, near_edge)),
+        pinned(group_refs), coarse, local0, kept(coupling),
+        *(pinned(x) for x in (transfer, basis, near_inner, near_edge)),
     )
 
 
@@ -484,22 +537,27 @@
     rows = [[row * ROW + i for i in range(ROW)] for row in range(devices // ROW)]
     columns = [[col + ROW * i for i in range(devices // ROW)] for col in range(ROW)]
     pack, rim_last, rim_first, own, up, down, coarse = upward(
-        column, send_lists[0].T, densities, points, weights[None, :], leaf_basis, transfer, devices // ROW
+        column, send_lists[0].T, densities, points, weights[None, :], leaf_basis, transfer, 1
     )
-    coarse_rows = lax.all_to_all(coarse, AXES, 0, 0, axis_index_groups=columns, tiled=True)
     lists_below = shifted(up, ROW, devices)
     lists_above = shifted(down, -ROW, devices)
     from_below = shifted(rim_last, 1, devices)
-    payload = assemble(column, own, lists_below, lists_above, coarse_rows)
-    payload, from_below, rim_first, pack = lax.optimization_barrier((payload, from_below, rim_first, pack))
+    from_above = shifted(rim_first, -1, devices)
+    payload = assemble(column, own, lists_below, lists_above, coarse)
+    payload, from_below, from_above = lax.optimization_barrier((payload, from_below, from_above))
     swapped = lax.all_to_all(payload, AXES, 0, 0, axis_index_groups=rows, tiled=True)
-    rims = (from_below, shifted(rim_first, -1, devices))
     offsets = near_offsets.T
     near_inner, inner = near_field(offsets, pack, None, leaf_coupling, coarse_coupling)
-    near_edge, edge, packed_coarse = near_field(offsets, pack, rims, leaf_coupling, coarse_coupling)
-    return finish(
-        column, relay_refs, coarse_refs, swapped, lists_below, lists_above, inner, edge, packed_coarse, transfer,
-        leaf_basis, near_inner, near_edge,
+    swapped, pack, near_inner, inner = lax.optimization_barrier((swapped, pack, near_inner, inner))
+    everyone = lax.all_to_all(
+        repeat(swapped, devices // ROW), AXES, 0, 0, axis_index_groups=columns, tiled=True
+    )
+    near_edge, edge, packed_coarse = near_field(
+        offsets, pack, (from_below, from_above), leaf_coupling, coarse_coupling
+    )
+    local0 = leaf_local(column, relay_refs, swapped, lists_below, lists_above, inner, edge)
+    return downward(
+        coarse_refs, everyone, local0, packed_coarse, transfer, leaf_basis, near_inner, near_edge
     )
 
 

time: 71.4 us -> 68 us (0.952)
  the two profiles are of different devices: /device:TPU:1 before, /device:TPU:0 now
where the time goes in v6:
time: 68 us; the launch traced here: 67.3 us
  Pallas kernels  30 us (44%)
  starting transfers between devices  24.6 us (36%)
  waiting for transfers between devices  12.6 us (19%)
    pallas_call x2, Pallas kernels, near_field(): pl.pallas_call(edge_kernel if edge else inner_kernel, name='near_edge' if...  16.9 us
    all_to_all x1, starting transfers between devices, local(): lax.all_to_all(repeat(swapped, devices // ROW), AXES, 0, 0, axis_index_gr...  10.2 us
    ppermute x4, starting transfers between devices, shifted(): lax.ppermute(shard, AXES, [(i, i + by) for i in range(devices) if 0 <= i...  7.97 us
    all_to_all x1, starting transfers between devices, local(): lax.all_to_all(payload, AXES, 0, 0, axis_index_groups=rows, tiled=True)  6.48 us
    ppermute x4, waiting for transfers between devices, shifted(): lax.ppermute(shard, AXES, [(i, i + by) for i in range(devices) if 0 <= i...  5.77 us
    pallas_call x1, Pallas kernels, leaf_local(): pl.pallas_call(leaf_kernel, name='leaf_local', out_shape=jax.ShapeDtypeSt...  4.72 us
    all_to_all x1, waiting for transfers between devices, local(): lax.all_to_all(repeat(swapped, devices // ROW), AXES, 0, 0, axis_index_gr...  4.1 us
    pallas_call x1, Pallas kernels, downward(): pl.pallas_call(downward_kernel, name='downward', out_shape=jax.ShapeDtype...  3.17 us
  transfers between devices with their start and end apart: 6, of which 4 were waited for; matrix products, arithmetic and copies ran while one was open for 0% of the time, Pallas kernels for 33%

profile of v6, /device:TPU:0, one launch (start us, length us, event | category | flops | bytes accessed | tf_op | source)
XLA Modules:
  0.0 67.3 jit_solution(14435668770685301901)
XLA Ops:
  0.0 3.1 %upward.1 = (bf16[32,4096]{1,0:T(8,128)(2,1)S(1)}, bf16[32,1024]{1,0:T(8,128)(2,1)S(1)}, bf16[32,1024]{1,0:T(8,128)(2,1)S(1)}, bf16[8,8,16,128]{3,2,1,0:T(8,128)...) custom-call(s32[1]{0:T(128)} %bitcast.column_ref, ...), custom_call_target="tpu_custom_call" | custom-call | flops 20000000 | bytes 4194304 | tf_op jit(solution)/shard_map/upward/pallas_call | solution.py:120
  3.1 3.9 %collective-permute-start = (bf16[8,8,16,128]{3,2,1,0:T(8,128)(2,1)S(1)}, bf16[8,8,16,128]{3,2,1,0:T(8,128)(2,1)S(1)}, u32[]{:S(2)}, u32[]{:S(2)}) collective-permute-start(bf16[8,8,16,128]{3,2,1,0:T(8,128)(2,1)S(1)} %get-tuple-element.25), channel_id=1, source_target_pairs={{0,8},{1,9},{2,10},{3,11},{4,12},{5,13},{6,14},{7,15},{8,16},{9,17... | collective-permute-start | bytes 786440 | tf_op jit(solution)/shard_map/ppermute | solution.py:528
  7.0 1.3 %collective-permute-start.1 = (bf16[8,8,16,128]{3,2,1,0:T(8,128)(2,1)S(1)}, bf16[8,8,16,128]{3,2,1,0:T(8,128)(2,1)S(1)}, u32[]{:S(2)}, u32[]{:S(2)}) collective-permute-start(bf16[8,8,16,128]{3,2,1,0:T(8,128)(2,1)S(1)} %get-tuple-element.26), channel_id=1, source_target_pairs={{8,0},{9,1},{10,2},{11,3},{12,4},{13,5},{14,6},{15,7},{16,8},{17,9... | collective-permute-start | bytes 786440 | tf_op jit(solution)/shard_map/ppermute | solution.py:528
  8.3 1.5 %collective-permute-start.2 = (bf16[32,1024]{1,0:T(8,128)(2,1)S(1)}, bf16[32,1024]{1,0:T(8,128)(2,1)S(1)}, u32[]{:S(2)}, u32[]{:S(2)}) collective-permute-start(bf16[32,1024]{1,0:T(8,128)(2,1)S(1)} %get-tuple-element.28), channel_id=1, source_target_pairs={{0,1},{1,2},{2,3},{3,4},{4,5},{5,6},{6,7},{7,8},{8,9},{9,10},{10,1... | collective-permute-start | bytes 196616 | tf_op jit(solution)/shard_map/ppermute | solution.py:528
  9.8 1.3 %collective-permute-start.3 = (bf16[32,1024]{1,0:T(8,128)(2,1)S(1)}, bf16[32,1024]{1,0:T(8,128)(2,1)S(1)}, u32[]{:S(2)}, u32[]{:S(2)}) collective-permute-start(bf16[32,1024]{1,0:T(8,128)(2,1)S(1)} %get-tuple-element.29), channel_id=1, source_target_pairs={{1,0},{2,1},{3,2},{4,3},{5,4},{6,5},{7,6},{8,7},{9,8},{10,9},{11,1... | collective-permute-start | bytes 196616 | tf_op jit(solution)/shard_map/ppermute | solution.py:528
  11.1 1.5 %collective-permute-done.below_ref = bf16[8,8,16,128]{3,2,1,0:T(8,128)(2,1)S(1)} collective-permute-done((bf16[8,8,16,128]{3,2,1,0:T(8,128)(2,1)S(1)}, bf16[8,8,16,128]{3,2,1,0:T(8,128)(2,1)S(1)}, u32[]{:S(2)}, u32[]{:S(2)}) %collective-permute-start) | collective-permute-done | bytes 262176 | tf_op jit(solution)/shard_map/ppermute | solution.py:528
  12.6 4.3 %collective-permute-done.1.above_ref = bf16[8,8,16,128]{3,2,1,0:T(8,128)(2,1)S(1)} collective-permute-done((bf16[8,8,16,128]{3,2,1,0:T(8,128)(2,1)S(1)}, bf16[8,8,16,128]{3,2,1,0:T(8,128)(2,1)S(1)}, u32[]{:S(2)}, u32[]{:S(2)}) %collective-permute-start.1) | collective-permute-done | bytes 262176 | tf_op jit(solution)/shard_map/ppermute | solution.py:528
  16.9 0.9 %assemble.1 = bf16[8,18,16,128]{3,2,1,0:T(8,128)(2,1)} custom-call(s32[1]{0:T(128)} %bitcast.column_ref, bf16[8,8,16,128]{3,2,1,0:T(8,128)(2,1)S(1)} %get-tuple-element.24.own_ref, bf16[8,8,16,128]{3,2,1,0:T(8,128)(2,1)S(1)} %collective-permute-done.below_ref, bf16[8,8,16,128]{3,2,1,0:T(8,128)(2,1)S(1)} %collective-permute-done.1.above_ref, ...), custom_call_target="tpu_custom_call" | custom-call | bytes 1048576 | tf_op jit(solution)/shard_map/assemble/pallas_call | solution.py:350
  17.8 0.0 collective-permute-done.2.refs_2_
  17.8 0.0 copy-start
  17.8 0.0 collective-permute-done.3.refs_3_
  17.8 0.0 copy-start.1
  17.8 6.5 %all-to-all-start = ((bf16[8,18,16,128]{3,2,1,0:T(8,128)(2,1)}), bf16[8,18,16,128]{3,2,1,0:T(8,128)(2,1)S(1)}, u32[]{:S(2)}, u32[]{:S(2)}) async-start(bf16[8,18,16,128]{3,2,1,0:T(8,128)(2,1)} %assemble.1), calls=%async_computation | async-start | bytes 1179648 | tf_op jit(solution)/shard_map/all_to_all | solution.py:548
  24.3 8.3 %near_inner.1 = (f32[16,2048]{1,0:T(8,128)}, bf16[16,64,2048]{2,1,0:T(8,128)(2,1)}) custom-call(s32[13,32]{1,0:T(8,128)} %bitcast.6, bf16[32,4096]{1,0:T(8,128)(2,1)S(1)} %get-tuple-element.36.pack.refs_1_, bf16[32,32,64,64]{3,2,1,0:T(8,128)(2,1)} %refs_4_.1), custom_call_target="tpu_custom_call" | custom-call | flops 327155712 | bytes 14680064 | tf_op jit(solution)/shard_map/near_inner/pallas_call | solution.py:307
  32.6 0.0 copy-done
  32.6 0.0 copy-done.1
  32.6 2.7 %all-to-all-done.swapped_ref = bf16[8,18,16,128]{3,2,1,0:T(8,128)(2,1)S(1)} async-done(((bf16[8,18,16,128]{3,2,1,0:T(8,128)(2,1)}), bf16[8,18,16,128]{3,2,1,0:T(8,128)(2,1)S(1)}, u32[]{:S(2)}, u32[]{:S(2)}) %all-to-all-start) | async-done | bytes 589856 | tf_op jit(solution)/shard_map/all_to_all | solution.py:548
  35.3 1.3 %repeat.1 = bf16[16,8,2,16,128]{4,3,2,1,0:T(8,128)(2,1)} custom-call(bf16[8,18,16,128]{3,2,1,0:T(8,128)(2,1)S(1)} %all-to-all-done.swapped_ref), custom_call_target="tpu_custom_call" | custom-call | bytes 1048576 | tf_op jit(solution)/shard_map/repeat/pallas_call | solution.py:369
  36.6 10.2 %all-to-all-start.1 = ((bf16[16,8,2,16,128]{4,3,2,1,0:T(8,128)(2,1)}), bf16[16,8,2,16,128]{4,3,2,1,0:T(8,128)(2,1)S(1)}, u32[]{:S(2)}, u32[]{:S(2)}) async-start(bf16[16,8,2,16,128]{4,3,2,1,0:T(8,128)(2,1)} %repeat.1), calls=%async_computation.1 | async-start | bytes 2097152 | tf_op jit(solution)/shard_map/all_to_all | solution.py:552
  46.8 8.6 %near_edge.1 = (f32[16,2048]{1,0:T(8,128)}, bf16[16,64,2048]{2,1,0:T(8,128)(2,1)}, bf16[4,64,2048]{2,1,0:T(8,128)(2,1)S(1)}) custom-call(s32[13,32]{1,0:T(8,128)} %bitcast.7, bf16[32,4096]{1,0:T(8,128)(2,1)S(1)} %get-tuple-element.36.pack.refs_1_, bf16[32,1024]{1,0:T(8,128)(2,1)} %copy-done, bf16[32,1024]{1,0:T(8,128)(2,1)} %copy-done.1, ...), custom_call_target="tpu_custom_call" | custom-call | flops 327155712 | bytes 14680064 | tf_op jit(solution)/shard_map/near_edge/pallas_call | solution.py:307
  55.3 4.7 %leaf_local.1.local_ref = f32[32,16,64]{2,1,0:T(8,128)S(1)} custom-call(s32[1]{0:T(128)} %bitcast.column_ref, s32[32,32]{1,0:T(8,128)} %leaf_hbm.1, bf16[8,18,16,128]{3,2,1,0:T(8,128)(2,1)S(1)} %all-to-all-done.swapped_ref, bf16[8,8,16,128]{3,2,1,0:T(8,128)(2,1)S(1)} %collective-permute-done.below_ref, ...), custom_call_target="tpu_custom_call" | custom-call | flops 140000000 | bytes 9437184 | tf_op jit(solution)/shard_map/leaf_local/pallas_call | solution.py:439
  60.1 4.1 %all-to-all-done.1.coarse_ref = bf16[16,8,2,16,128]{4,3,2,1,0:T(8,128)(2,1)S(1)} async-done(((bf16[16,8,2,16,128]{4,3,2,1,0:T(8,128)(2,1)}), bf16[16,8,2,16,128]{4,3,2,1,0:T(8,128)(2,1)S(1)}, u32[]{:S(2)}, u32[]{:S(2)}) %all-to-all-start.1) | async-done | bytes 1048608 | tf_op jit(solution)/shard_map/all_to_all | solution.py:552
  64.2 3.2 %downward.1 = f32[16,4096]{1,0:T(8,128)} custom-call(s32[4,32]{1,0:T(4,128)} %group_hbm.1, bf16[16,8,2,16,128]{4,3,2,1,0:T(8,128)(2,1)S(1)} %all-to-all-done.1.coarse_ref, f32[32,16,64]{2,1,0:T(8,128)S(1)} %leaf_local.1.local_ref, bf16[4,64,2048]{2,1,0:T(8,128)(2,1)S(1)} %get-tuple-element.40.coupling_ref, bf16[32,64,64]{2,1,0:T(8,128)(2,1)} %transfer_hbm.3, ...), custom_call_target="tpu_custom_call" | custom-call | flops 60000000 | bytes 4194304 | tf_op jit(solution)/shard_map/downward/pallas_call | solution.py:505
Async XLA Ops:
  3.1 9.5 %collective-permute-start = (bf16[8,8,16,128]{3,2,1,0:T(8,128)(2,1)S(1)}, bf16[8,8,16,128]{3,2,1,0:T(8,128)(2,1)S(1)}, u32[]{:S(2)}, u32[]{:S(2)}) collective-permute-start(bf16[8,8,16,128]{3,2,1,0:T(8,128)(2,1)S(1)} %get-tuple-element.25), channel_id=1, source_target_pairs={{0,8},{1,9},{2,10},{3,11},{4,12},{5,13},{6,14},{7,15},{8,16},{9,17... | collective-permute-start | bytes 786440 | tf_op jit(solution)/shard_map/ppermute | solution.py:528
  7.0 9.8 %collective-permute-start.1 = (bf16[8,8,16,128]{3,2,1,0:T(8,128)(2,1)S(1)}, bf16[8,8,16,128]{3,2,1,0:T(8,128)(2,1)S(1)}, u32[]{:S(2)}, u32[]{:S(2)}) collective-permute-start(bf16[8,8,16,128]{3,2,1,0:T(8,128)(2,1)S(1)} %get-tuple-element.26), channel_id=1, source_target_pairs={{8,0},{9,1},{10,2},{11,3},{12,4},{13,5},{14,6},{15,7},{16,8},{17,9... | collective-permute-start | bytes 786440 | tf_op jit(solution)/shard_map/ppermute | solution.py:528
  8.3 9.4 %collective-permute-start.2 = (bf16[32,1024]{1,0:T(8,128)(2,1)S(1)}, bf16[32,1024]{1,0:T(8,128)(2,1)S(1)}, u32[]{:S(2)}, u32[]{:S(2)}) collective-permute-start(bf16[32,1024]{1,0:T(8,128)(2,1)S(1)} %get-tuple-element.28), channel_id=1, source_target_pairs={{0,1},{1,2},{2,3},{3,4},{4,5},{5,6},{6,7},{7,8},{8,9},{9,10},{10,1... | collective-permute-start | bytes 196616 | tf_op jit(solution)/shard_map/ppermute | solution.py:528
  9.8 8.0 %collective-permute-start.3 = (bf16[32,1024]{1,0:T(8,128)(2,1)S(1)}, bf16[32,1024]{1,0:T(8,128)(2,1)S(1)}, u32[]{:S(2)}, u32[]{:S(2)}) collective-permute-start(bf16[32,1024]{1,0:T(8,128)(2,1)S(1)} %get-tuple-element.29), channel_id=1, source_target_pairs={{1,0},{2,1},{3,2},{4,3},{5,4},{6,5},{7,6},{8,7},{9,8},{10,9},{11,1... | collective-permute-start | bytes 196616 | tf_op jit(solution)/shard_map/ppermute | solution.py:528
  17.8 14.8 %copy-start = (bf16[32,1024]{1,0:T(8,128)(2,1)}, bf16[32,1024]{1,0:T(8,128)(2,1)S(1)}, u32[]{:S(2)}) copy-start(bf16[32,1024]{1,0:T(8,128)(2,1)S(1)} %collective-permute-done.2.refs_2_) | copy-start | bytes 196612
  17.8 14.8 %copy-start.1 = (bf16[32,1024]{1,0:T(8,128)(2,1)}, bf16[32,1024]{1,0:T(8,128)(2,1)S(1)}, u32[]{:S(2)}) copy-start(bf16[32,1024]{1,0:T(8,128)(2,1)S(1)} %collective-permute-done.3.refs_3_) | copy-start | bytes 196612
  17.8 17.5 %all-to-all-start = ((bf16[8,18,16,128]{3,2,1,0:T(8,128)(2,1)}), bf16[8,18,16,128]{3,2,1,0:T(8,128)(2,1)S(1)}, u32[]{:S(2)}, u32[]{:S(2)}) async-start(bf16[8,18,16,128]{3,2,1,0:T(8,128)(2,1)} %assemble.1), calls=%async_computation | async-start | bytes 1179648 | tf_op jit(solution)/shard_map/all_to_all | solution.py:548
  36.6 27.6 %all-to-all-start.1 = ((bf16[16,8,2,16,128]{4,3,2,1,0:T(8,128)(2,1)}), bf16[16,8,2,16,128]{4,3,2,1,0:T(8,128)(2,1)S(1)}, u32[]{:S(2)}, u32[]{:S(2)}) async-start(bf16[16,8,2,16,128]{4,3,2,1,0:T(8,128)(2,1)} %repeat.1), calls=%async_computation.1 | async-start | bytes 2097152 | tf_op jit(solution)/shard_map/all_to_all | solution.py:552

commit v7 on v4

--- a/solution.py
+++ b/solution.py
@@ -298,6 +298,7 @@
 def assemble_kernel(column_ref, own_ref, below_ref, above_ref, coarse_ref, out_ref):
     column = column_ref[0]
     rows, pairs = coarse_ref.shape[:2]
+    halves = coarse_ref[...].reshape(rows // 2, 2, pairs, 16, 128)
     for target in range(out_ref.shape[0]):
         out_ref[target, 0:8] = own_ref[target]
         crossed = jnp.where(target < column, 0, 1)
@@ -310,7 +311,7 @@
         def _():
             out_ref[target, 8:16] = above_ref[target]
 
-        out_ref[target, 16:] = coarse_ref[...].reshape(rows * pairs, 16, 128)
+        out_ref[target, 16:] = halves[:, target % 2].reshape(rows // 2 * pairs, 16, 128)
 
 
 def assemble(column, own, below, above, coarse):
@@ -318,7 +319,7 @@
     return pl.pallas_call(
         assemble_kernel,
         name="assemble",
-        out_shape=jax.ShapeDtypeStruct((ROW, 16 + rows * pairs, 16, 128), bf16),
+        out_shape=jax.ShapeDtypeStruct((ROW, 16 + rows // 2 * pairs, 16, 128), bf16),
         in_specs=[SMEM] + [VMEM] * 4,
         out_specs=VMEM,
         compiler_params=pltpu.CompilerParams(vmem_limit_bytes=8 << 20),
@@ -338,28 +339,21 @@
     return jnp.concatenate([jnp.where(mask, pick(s), pick(s + 1)) for s in range(0, slots, 2)], axis=1)
 
 
-def finish_kernel(
-    column_ref, leaf_hbm, group_hbm, swapped_ref, below_ref, above_ref, coupling_ref,
-    packed_hbm, transfer_hbm, basis_hbm, near_hbm,
-    out_ref, leaf_refs, group_refs, packed_ref, near_ref, transfer_ref, basis_ref, table_ref, picked_ref, sems,
+def leaf_kernel(
+    column_ref, leaf_hbm, swapped_ref, below_ref, above_ref, packed_hbm,
+    out_ref, leaf_refs, packed_ref, table_ref, sems,
 ):
-    groups = coupling_ref.shape[0]
-    slots = coupling_ref.shape[2] // 64
-    copies = [
-        pltpu.make_async_copy(source, target, sems.at[i])
-        for i, (source, target) in enumerate((
-            (group_hbm, group_refs), (leaf_hbm, leaf_refs), (transfer_hbm, transfer_ref), (basis_hbm, basis_ref),
-            (near_hbm, near_ref),
-        ))
-    ]
-    chunks = [
-        pltpu.make_async_copy(packed_hbm.at[pl.ds(i * 4, 4)], packed_ref.at[pl.ds(i * 4, 4)], sems.at[5 + i])
-        for i in range(2 * groups)
-    ]
-    copies[2:2] = chunks
-    for copy in copies:
+    leaves, slots = leaf_refs.shape
+    size = 4
+    count = leaves // size
+    table = pltpu.make_async_copy(leaf_hbm, leaf_refs, sems.at[count])
+    table.start()
+    chunks = []
+    for i in range(count):
+        span = pl.ds(i * size, size)
+        chunks.append(pltpu.make_async_copy(packed_hbm.at[span], packed_ref.at[span], sems.at[i]))
+    for copy in chunks[:4]:
         copy.start()
-    mask = low_half((16, 128))
     column = column_ref[0]
     spread = spread_matrix()
 
@@ -376,12 +370,58 @@
         owner = place & (ROW - 1)
         crossed = jnp.where((place >= ROW) & (place < 2 * ROW), 0, 8)
         put(window, swapped_ref[owner, pl.ds(pl.multiple_of(crossed, 8), 8)])
-
+    table.wait()
+    for chunk in range(count):
+        chunks[chunk].wait()
+        if chunk + 4 < count:
+            chunks[chunk + 4].start()
+        for leaf in range(chunk * size, (chunk + 1) * size):
+            out_ref[leaf] = nt(paired(slots, lambda s: table_ref[leaf_refs[leaf, s]]), packed_ref[leaf])
+
+
+def leaf_local(column, leaf_refs, swapped, below, above, packed):
+    leaves = leaf_refs.shape[0]
+    return pl.pallas_call(
+        leaf_kernel,
+        name="leaf_local",
+        out_shape=jax.ShapeDtypeStruct((leaves, 16, 64), f32),
+        in_specs=[SMEM, HBM] + [VMEM] * 3 + [HBM],
+        out_specs=VMEM,
+        scratch_shapes=[
+            pltpu.SMEM(leaf_refs.shape, jnp.int32),
+            pltpu.VMEM(packed.shape, bf16),
+            pltpu.VMEM(((2 * WINDOW + 1) * 16, 16, 128), bf16),
+            pltpu.SemaphoreType.DMA((leaves // 4 + 1,)),
+        ],
+        compiler_params=pltpu.CompilerParams(vmem_limit_bytes=16 << 20),
+        cost_estimate=pl.CostEstimate(flops=140_000_000, bytes_accessed=9 << 20, transcendentals=0),
+    )(column, pinned(leaf_refs), swapped, below, above, pinned(packed))
+
+
+def downward_kernel(
+    column_ref, group_hbm, swapped_ref, other_ref, local_ref, coupling_ref, transfer_hbm, basis_hbm, near_hbm,
+    out_ref, group_refs, transfer_ref, basis_ref, near_ref, picked_ref, sems,
+):
+    groups, slots = group_refs.shape
+    copies = [
+        pltpu.make_async_copy(source, target, sems.at[i])
+        for i, (source, target) in enumerate((
+            (group_hbm, group_refs), (transfer_hbm, transfer_ref), (basis_hbm, basis_ref),
+            (near_hbm, near_ref),
+        ))
+    ]
+    for copy in copies:
+        copy.start()
+    mask = low_half((16, 128))
+    core = column_ref[0] & 1
     copies[0].wait()
     for group in range(groups):
         for slot in range(slots):
             ref = group_refs[group, slot]
-            tile = swapped_ref[(ref >> 2) & (ROW - 1), 16 + ((ref >> 5) << 1) + ((ref >> 1) & 1)]
+            owner = (ref >> 2) & (ROW - 1)
+            place = ((ref >> 6) << 1) + ((ref >> 1) & 1)
+            here = ((ref >> 5) & 1) == core
+            tile = jnp.where(here, swapped_ref[owner, 16 + place], other_ref[owner, place])
             keep = mask == ((ref & 1) == 0)
             picked_ref[group * slots + slot] = jnp.where(keep, tile, jnp.zeros_like(tile))
     row = lax.broadcasted_iota(jnp.int32, (128, 128), 0)
@@ -396,46 +436,38 @@
     local1 = [
         nt(paired(slots, lambda s: both[group][s]), coupling_ref[group]).astype(bf16) for group in range(groups)
     ]
-    copies[1].wait()
-    for copy in copies[2 + len(chunks):]:
+    for copy in copies[1:]:
         copy.wait()
-    for group in range(groups):
-        chunks[2 * group].wait()
-        chunks[2 * group + 1].wait()
-        leaves = range(group * 8, group * 8 + 8)
-        fields = [nt(paired(slots, lambda s: table_ref[leaf_refs[leaf, s]]), packed_ref[leaf]) for leaf in leaves]
-        passed = [nt(local1[group], transfer_ref[leaf]) for leaf in leaves]
-        rounded = [(one + two).astype(bf16) for one, two in zip(fields, passed)]
-        for leaf, field in zip(leaves, rounded):
-            span = slice(leaf * 128, (leaf + 1) * 128)
-            out_ref[:, span] = near_ref[:, span] + jnp.dot(field, basis_ref[leaf], preferred_element_type=f32)
-
-
-def finish(column, leaf_refs, group_refs, swapped, below, above, packed, coupling, transfer, basis, near):
-    groups = coupling.shape[0]
-    slots = leaf_refs.shape[1]
+    leaves = range(groups * 8)
+    passed = [nt(local1[leaf // 8], transfer_ref[leaf]) for leaf in leaves]
+    rounded = [(local_ref[leaf] + one).astype(bf16) for leaf, one in zip(leaves, passed)]
+    for leaf, field in zip(leaves, rounded):
+        span = slice(leaf * 128, (leaf + 1) * 128)
+        out_ref[:, span] = near_ref[:, span] + jnp.dot(field, basis_ref[leaf], preferred_element_type=f32)
+
+
+def downward(column, group_refs, swapped, other, local0, coupling, transfer, basis, near):
+    groups, slots = group_refs.shape
+    shape = near.shape
     return pl.pallas_call(
-        finish_kernel,
-        name="finish",
-        out_shape=jax.ShapeDtypeStruct(near.shape, f32),
-        in_specs=[SMEM] + [HBM] * 2 + [VMEM] * 4 + [HBM] * 4,
+        downward_kernel,
+        name="downward",
+        out_shape=jax.ShapeDtypeStruct(shape, f32),
+        in_specs=[SMEM, HBM] + [VMEM] * 4 + [HBM] * 3,
         out_specs=VMEM,
         scratch_shapes=[
-            pltpu.SMEM(leaf_refs.shape, jnp.int32),
             pltpu.SMEM(group_refs.shape, jnp.int32),
-            pltpu.VMEM(packed.shape, bf16),
-            pltpu.VMEM(near.shape, f32),
             pltpu.VMEM(transfer.shape, bf16),
             pltpu.VMEM(basis.shape, bf16),
-            pltpu.VMEM(((2 * WINDOW + 1) * 16, 16, 128), bf16),
+            pltpu.VMEM(shape, f32),
             pltpu.VMEM((groups * slots, 16, 128), bf16),
-            pltpu.SemaphoreType.DMA((5 + 2 * groups,)),
+            pltpu.SemaphoreType.DMA((4,)),
         ],
-        compiler_params=pltpu.CompilerParams(vmem_limit_bytes=20 << 20),
-        cost_estimate=pl.CostEstimate(flops=200_000_000, bytes_accessed=4 << 20, transcendentals=0),
+        compiler_params=pltpu.CompilerParams(vmem_limit_bytes=8 << 20),
+        cost_estimate=pl.CostEstimate(flops=60_000_000, bytes_accessed=4 << 20, transcendentals=0),
     )(
-        column, pinned(leaf_refs), pinned(group_refs), swapped, below, above,
-        kept(coupling), pinned(packed), pinned(transfer), pinned(basis), pinned(near),
+        column, pinned(group_refs), swapped, other, local0, kept(coupling),
+        *(pinned(x) for x in (transfer, basis, near)),
     )
 
 
@@ -465,9 +497,11 @@
     near, packed, packed_coarse = near_field(
         near_offsets.T, pack, from_below, from_above, leaf_coupling, coarse_coupling
     )
-    return finish(
-        column, relay_refs, coarse_refs, swapped, lists_below, lists_above, packed, packed_coarse, transfer,
-        leaf_basis, near,
+    swapped, near, packed = lax.optimization_barrier((swapped, near, packed))
+    other = lax.ppermute(swapped[:, 16:], AXES, [(i, i ^ 1) for i in range(devices)])
+    local0 = leaf_local(column, relay_refs, swapped, lists_below, lists_above, packed)
+    return downward(
+        column, coarse_refs, swapped, other, local0, packed_coarse, transfer, leaf_basis, near
     )
 
 

time: 66.1 us -> 59.1 us (0.89)
  waiting for transfers between devices: 8.51 us -> 2.99 us
  Pallas kernels: 30.1 us -> 27.7 us
  starting transfers between devices: 26.8 us -> 27.7 us
    all_to_all x1, waiting for transfers between devices: 6.18 us -> 0.53 us  [local(): lax.all_to_all(payload, AXES, 0, 0, axis_index_groups=rows, tiled=True)]
    pallas_call x1 -> x2, Pallas kernels: 10.4 us -> 8.16 us  [the longest x1 4.73 us: leaf_local(): pl.pallas_call(leaf_kernel, name='leaf_local', out_shape=jax.ShapeDtypeSt...]
    ppermute x0 -> x1, starting transfers between devices: none -> 0.95 us  [local(): lax.ppermute(swapped[:, 16:], AXES, [(i, i ^ 1) for i in range(devices)])]
  transfers between devices with their start and end apart: 6 -> 7, of which waited for: 3 -> 3; matrix products, arithmetic and copies ran while one was open for 0% -> 0% of each run, Pallas kernels for 24% -> 35%
where the time goes in v7:
time: 59.1 us; the launch traced here: 58.5 us
  Pallas kernels  27.7 us (47%)
  starting transfers between devices  27.7 us (47%)
  waiting for transfers between devices  2.99 us (5%)
    pallas_call x1, Pallas kernels, near_field(): pl.pallas_call(near_kernel, name='near', out_shape=(pltpu.HBM((16, count)...  14.6 us
    ppermute x4, starting transfers between devices, shifted(): lax.ppermute(shard, AXES, [(i, i + by) for i in range(devices) if 0 <= i...  12.2 us
    all_to_all x1, starting transfers between devices, local(): lax.all_to_all(coarse, AXES, 0, 0, axis_index_groups=columns, tiled=True)  8.04 us
    all_to_all x1, starting transfers between devices, local(): lax.all_to_all(payload, AXES, 0, 0, axis_index_groups=rows, tiled=True)  6.51 us
    pallas_call x1, Pallas kernels, leaf_local(): pl.pallas_call(leaf_kernel, name='leaf_local', out_shape=jax.ShapeDtypeSt...  4.73 us
    pallas_call x1, Pallas kernels, upward(): pl.pallas_call(upward_kernel, name='upward', out_shape=(jax.ShapeDtypeStr...  3.77 us
    pallas_call x1, Pallas kernels, downward(): pl.pallas_call(downward_kernel, name='downward', out_shape=jax.ShapeDtype...  3.43 us
    ppermute x4, waiting for transfers between devices, shifted(): lax.ppermute(shard, AXES, [(i, i + by) for i in range(devices) if 0 <= i...  2.3 us
  transfers between devices with their start and end apart: 7, of which 3 were waited for; matrix products, arithmetic and copies ran while one was open for 0% of the time, Pallas kernels for 35%

profile of v7, /device:TPU:1, one launch (start us, length us, event | category | flops | bytes accessed | tf_op | source)
XLA Modules:
  0.0 58.5 jit_solution(14456244261561306673)
XLA Ops:
  0.0 3.8 %upward.1 = (bf16[32,4096]{1,0:T(8,128)(2,1)S(1)}, bf16[32,1024]{1,0:T(8,128)(2,1)S(1)}, bf16[32,1024]{1,0:T(8,128)(2,1)S(1)}, bf16[8,8,16,128]{3,2,1,0:T(8,128)...) custom-call(s32[1]{0:T(128)} %bitcast.column_ref, ...), custom_call_target="tpu_custom_call" | custom-call | flops 20000000 | bytes 4194304 | tf_op jit(solution)/shard_map/upward/pallas_call | solution.py:120
  3.8 4.4 %collective-permute-start = (bf16[8,8,16,128]{3,2,1,0:T(8,128)(2,1)S(1)}, bf16[8,8,16,128]{3,2,1,0:T(8,128)(2,1)S(1)}, u32[]{:S(2)}, u32[]{:S(2)}) collective-permute-start(bf16[8,8,16,128]{3,2,1,0:T(8,128)(2,1)S(1)} %get-tuple-element.22), channel_id=1, source_target_pairs={{0,8},{1,9},{2,10},{3,11},{4,12},{5,13},{6,14},{7,15},{8,16},{9,17... | collective-permute-start | bytes 786440 | tf_op jit(solution)/shard_map/ppermute | solution.py:475
  8.2 1.3 %collective-permute-start.1 = (bf16[8,8,16,128]{3,2,1,0:T(8,128)(2,1)S(1)}, bf16[8,8,16,128]{3,2,1,0:T(8,128)(2,1)S(1)}, u32[]{:S(2)}, u32[]{:S(2)}) collective-permute-start(bf16[8,8,16,128]{3,2,1,0:T(8,128)(2,1)S(1)} %get-tuple-element.23), channel_id=1, source_target_pairs={{8,0},{9,1},{10,2},{11,3},{12,4},{13,5},{14,6},{15,7},{16,8},{17,9... | collective-permute-start | bytes 786440 | tf_op jit(solution)/shard_map/ppermute | solution.py:475
  9.5 8.0 %all-to-all-start = ((bf16[16,2,16,128]{3,2,1,0:T(8,128)(2,1)}), bf16[16,2,16,128]{3,2,1,0:T(8,128)(2,1)S(1)}, u32[]{:S(2)}, u32[]{:S(2)}) async-start(bf16[16,2,16,128]{3,2,1,0:T(8,128)(2,1)} %get-tuple-element.24), calls=%async_computation | async-start | bytes 262144 | tf_op jit(solution)/shard_map/all_to_all | solution.py:489
  17.5 4.6 %collective-permute-start.2 = (bf16[32,1024]{1,0:T(8,128)(2,1)S(1)}, bf16[32,1024]{1,0:T(8,128)(2,1)S(1)}, u32[]{:S(2)}, u32[]{:S(2)}) collective-permute-start(bf16[32,1024]{1,0:T(8,128)(2,1)S(1)} %get-tuple-element.25), channel_id=1, source_target_pairs={{0,1},{1,2},{2,3},{3,4},{4,5},{5,6},{6,7},{7,8},{8,9},{9,10},{10,1... | collective-permute-start | bytes 196616 | tf_op jit(solution)/shard_map/ppermute | solution.py:475
  22.1 1.9 %collective-permute-start.3 = (bf16[32,1024]{1,0:T(8,128)(2,1)S(1)}, bf16[32,1024]{1,0:T(8,128)(2,1)S(1)}, u32[]{:S(2)}, u32[]{:S(2)}) collective-permute-start(bf16[32,1024]{1,0:T(8,128)(2,1)S(1)} %get-tuple-element.26), channel_id=1, source_target_pairs={{1,0},{2,1},{3,2},{4,3},{5,4},{6,5},{7,6},{8,7},{9,8},{10,9},{11,1... | collective-permute-start | bytes 196616 | tf_op jit(solution)/shard_map/ppermute | solution.py:475
  24.1 0.2 all-to-all-done.coarse_ref
  24.2 0.0 collective-permute-done.below_ref
  24.2 0.0 collective-permute-done.1.above_ref
  24.2 1.2 %assemble.1 = bf16[8,32,16,128]{3,2,1,0:T(8,128)(2,1)} custom-call(s32[1]{0:T(128)} %bitcast.column_ref, bf16[8,8,16,128]{3,2,1,0:T(8,128)(2,1)S(1)} %get-tuple-element.21.own_ref, bf16[8,8,16,128]{3,2,1,0:T(8,128)(2,1)S(1)} %collective-permute-done.below_ref, bf16[8,8,16,128]{3,2,1,0:T(8,128)(2,1)S(1)} %collective-permute-done.1.above_ref, ...), custom_call_target="tpu_custom_call" | custom-call | bytes 3145728 | tf_op jit(solution)/shard_map/assemble/pallas_call | solution.py:319
  25.4 0.0 collective-permute-done.2.below_ref
  25.4 2.3 %collective-permute-done.3.above_ref = bf16[32,1024]{1,0:T(8,128)(2,1)S(1)} collective-permute-done((bf16[32,1024]{1,0:T(8,128)(2,1)S(1)}, bf16[32,1024]{1,0:T(8,128)(2,1)S(1)}, u32[]{:S(2)}, u32[]{:S(2)}) %collective-permute-start.3) | collective-permute-done | bytes 65568 | tf_op jit(solution)/shard_map/ppermute | solution.py:475
  27.7 6.5 %all-to-all-start.1 = ((bf16[8,32,16,128]{3,2,1,0:T(8,128)(2,1)}), bf16[8,32,16,128]{3,2,1,0:T(8,128)(2,1)S(1)}, u32[]{:S(2)}, u32[]{:S(2)}) async-start(bf16[8,32,16,128]{3,2,1,0:T(8,128)(2,1)} %assemble.1), calls=%async_computation.1 | async-start | bytes 2097152 | tf_op jit(solution)/shard_map/all_to_all | solution.py:496
  34.2 14.6 %near.1 = (f32[16,4096]{1,0:T(8,128)}, bf16[32,64,2048]{2,1,0:T(8,128)(2,1)}, bf16[4,64,2048]{2,1,0:T(8,128)(2,1)S(1)}) custom-call(s32[13,32]{1,0:T(8,128)} %bitcast.8, bf16[32,4096]{1,0:T(8,128)(2,1)S(1)} %get-tuple-element.28.pack_ref, bf16[32,1024]{1,0:T(8,128)(2,1)S(1)} %collective-permute-done.2.below_ref, ...), custom_call_target="tpu_custom_call" | custom-call | flops 654311424 | bytes 20971520 | tf_op jit(solution)/shard_map/near/pallas_call | solution.py:270
  48.8 0.5 all-to-all-done.1.swapped_ref
  49.4 1.0 %collective-permute-start.4 = (bf16[8,16,16,128]{3,2,1,0:T(8,128)(2,1)S(1)}, bf16[8,16,16,128]{3,2,1,0:T(8,128)(2,1)S(1)}, u32[]{:S(2)}, u32[]{:S(2)}) collective-permute-start(bf16[8,16,16,128]{3,2,1,0:T(8,128)(2,1)S(1)} %slice.3), channel_id=1, source_target_pairs={{0,1},{1,0},{2,3},{3,2},{4,5},{5,4},{6,7},{7,6},{8,9},{9,8},{10,11... | collective-permute-start | bytes 1572872 | tf_op jit(solution)/shard_map/ppermute | solution.py:501
  50.3 4.7 %leaf_local.1.local_ref = f32[32,16,64]{2,1,0:T(8,128)S(1)} custom-call(s32[1]{0:T(128)} %bitcast.column_ref, s32[32,32]{1,0:T(8,128)} %leaf_hbm.1, bf16[8,32,16,128]{3,2,1,0:T(8,128)(2,1)S(1)} %all-to-all-done.1.swapped_ref, bf16[8,8,16,128]{3,2,1,0:T(8,128)(2,1)S(1)} %collective-permute-done.below_ref, ...), custom_call_target="tpu_custom_call" | custom-call | flops 140000000 | bytes 9437184 | tf_op jit(solution)/shard_map/leaf_local/pallas_call | solution.py:384
  55.1 0.0 collective-permute-done.4.other_ref
  55.1 3.4 %downward.1 = f32[16,4096]{1,0:T(8,128)} custom-call(s32[1]{0:T(128)} %bitcast.column_ref, s32[4,32]{1,0:T(4,128)} %group_hbm.1, bf16[8,32,16,128]{3,2,1,0:T(8,128)(2,1)S(1)} %all-to-all-done.1.swapped_ref, bf16[8,16,16,128]{3,2,1,0:T(8,128)(2,1)S(1)} %collective-permute-done.4.other_ref, f32[32,16,64]{2,1,0:T(8,128)S(1)} %leaf_local.1.local_ref, ...), custom_call_target="tpu_custom_call" | custom-call | flops 60000000 | bytes 4194304 | tf_op jit(solution)/shard_map/downward/pallas_call | solution.py:452
  (1 shorter events, 0.0 us)
Async XLA Ops:
  3.8 20.4 %collective-permute-start = (bf16[8,8,16,128]{3,2,1,0:T(8,128)(2,1)S(1)}, bf16[8,8,16,128]{3,2,1,0:T(8,128)(2,1)S(1)}, u32[]{:S(2)}, u32[]{:S(2)}) collective-permute-start(bf16[8,8,16,128]{3,2,1,0:T(8,128)(2,1)S(1)} %get-tuple-element.22), channel_id=1, source_target_pairs={{0,8},{1,9},{2,10},{3,11},{4,12},{5,13},{6,14},{7,15},{8,16},{9,17... | collective-permute-start | bytes 786440 | tf_op jit(solution)/shard_map/ppermute | solution.py:475
  8.2 16.0 %collective-permute-start.1 = (bf16[8,8,16,128]{3,2,1,0:T(8,128)(2,1)S(1)}, bf16[8,8,16,128]{3,2,1,0:T(8,128)(2,1)S(1)}, u32[]{:S(2)}, u32[]{:S(2)}) collective-permute-start(bf16[8,8,16,128]{3,2,1,0:T(8,128)(2,1)S(1)} %get-tuple-element.23), channel_id=1, source_target_pairs={{8,0},{9,1},{10,2},{11,3},{12,4},{13,5},{14,6},{15,7},{16,8},{17,9... | collective-permute-start | bytes 786440 | tf_op jit(solution)/shard_map/ppermute | solution.py:475
  9.5 14.7 %all-to-all-start = ((bf16[16,2,16,128]{3,2,1,0:T(8,128)(2,1)}), bf16[16,2,16,128]{3,2,1,0:T(8,128)(2,1)S(1)}, u32[]{:S(2)}, u32[]{:S(2)}) async-start(bf16[16,2,16,128]{3,2,1,0:T(8,128)(2,1)} %get-tuple-element.24), calls=%async_computation | async-start | bytes 262144 | tf_op jit(solution)/shard_map/all_to_all | solution.py:489
  17.5 7.9 %collective-permute-start.2 = (bf16[32,1024]{1,0:T(8,128)(2,1)S(1)}, bf16[32,1024]{1,0:T(8,128)(2,1)S(1)}, u32[]{:S(2)}, u32[]{:S(2)}) collective-permute-start(bf16[32,1024]{1,0:T(8,128)(2,1)S(1)} %get-tuple-element.25), channel_id=1, source_target_pairs={{0,1},{1,2},{2,3},{3,4},{4,5},{5,6},{6,7},{7,8},{8,9},{9,10},{10,1... | collective-permute-start | bytes 196616 | tf_op jit(solution)/shard_map/ppermute | solution.py:475
  22.1 5.6 %collective-permute-start.3 = (bf16[32,1024]{1,0:T(8,128)(2,1)S(1)}, bf16[32,1024]{1,0:T(8,128)(2,1)S(1)}, u32[]{:S(2)}, u32[]{:S(2)}) collective-permute-start(bf16[32,1024]{1,0:T(8,128)(2,1)S(1)} %get-tuple-element.26), channel_id=1, source_target_pairs={{1,0},{2,1},{3,2},{4,3},{5,4},{6,5},{7,6},{8,7},{9,8},{10,9},{11,1... | collective-permute-start | bytes 196616 | tf_op jit(solution)/shard_map/ppermute | solution.py:475
  27.7 21.6 %all-to-all-start.1 = ((bf16[8,32,16,128]{3,2,1,0:T(8,128)(2,1)}), bf16[8,32,16,128]{3,2,1,0:T(8,128)(2,1)S(1)}, u32[]{:S(2)}, u32[]{:S(2)}) async-start(bf16[8,32,16,128]{3,2,1,0:T(8,128)(2,1)} %assemble.1), calls=%async_computation.1 | async-start | bytes 2097152 | tf_op jit(solution)/shard_map/all_to_all | solution.py:496
  49.4 5.7 %collective-permute-start.4 = (bf16[8,16,16,128]{3,2,1,0:T(8,128)(2,1)S(1)}, bf16[8,16,16,128]{3,2,1,0:T(8,128)(2,1)S(1)}, u32[]{:S(2)}, u32[]{:S(2)}) collective-permute-start(bf16[8,16,16,128]{3,2,1,0:T(8,128)(2,1)S(1)} %slice.3), channel_id=1, source_target_pairs={{0,1},{1,0},{2,3},{3,2},{4,5},{5,4},{6,7},{7,6},{8,9},{9,8},{10,11... | collective-permute-start | bytes 1572872 | tf_op jit(solution)/shard_map/ppermute | solution.py:501

commit v8 on v7

--- a/solution.py
+++ b/solution.py
@@ -244,7 +244,9 @@
                 packed_ref[slot, inside, :, tile * 64 : (tile + 2) * 64] = merged(buffer_ref.at[slot, inside], tile)
             if s + 2 >= slots:
                 near_ref[:, pl.ds(pl.multiple_of(leaf * 128, 128), 128)] = totals[inside]
-                flush(step, slot)[inside].start()
+                pltpu.make_async_copy(
+                    packed_ref.at[slot, inside], packed_hbm.at[leaf], out_sems.at[slot, inside]
+                ).start()
         return carry
 
     lax.fori_loop(0, steps, one_step, 0)
@@ -265,7 +267,7 @@
     wide = count + 2 * REACH * 128
     leaves, tiles = coupling.shape[:2]
     groups = coarse_coupling.shape[0]
-    per_step = 4
+    per_step = 8
     points = count * offsets.shape[0] * 128
     return pl.pallas_call(
         near_kernel,
@@ -290,7 +292,7 @@
             pltpu.SemaphoreType.DMA((2, per_step)),
             pltpu.SemaphoreType.DMA((3,)),
         ],
-        compiler_params=pltpu.CompilerParams(vmem_limit_bytes=16 << 20),
+        compiler_params=pltpu.CompilerParams(vmem_limit_bytes=28 << 20),
         cost_estimate=pl.CostEstimate(flops=points * 96, bytes_accessed=20 << 20, transcendentals=points),
     )(pinned(offsets), pack, below, above, pinned(coupling), pinned(coarse_coupling))
 

time: 59.1 us -> 58.9 us (level)
  Pallas kernels: 27.7 us -> 25.8 us
  waiting for transfers between devices: 2.99 us -> 4.85 us
    pallas_call x1, Pallas kernels: 14.6 us -> 12.7 us  [near_field(): pl.pallas_call(near_kernel, name='near', out_shape=(pltpu.HBM((16, count)...]
    all_to_all x1, waiting for transfers between devices: 0.53 us -> 2.39 us  [local(): lax.all_to_all(payload, AXES, 0, 0, axis_index_groups=rows, tiled=True)]
  transfers between devices with their start and end apart: 7 -> 7, of which waited for: 3 -> 3; matrix products, arithmetic and copies ran while one was open for 0% -> 0% of each run, Pallas kernels for 35% -> 32%
where the time goes in v8:
time: 58.9 us; the launch traced here: 58.5 us
  starting transfers between devices  27.7 us (47%)
  Pallas kernels  25.8 us (44%)
  waiting for transfers between devices  4.85 us (8%)
    pallas_call x1, Pallas kernels, near_field(): pl.pallas_call(near_kernel, name='near', out_shape=(pltpu.HBM((16, count)...  12.7 us
    ppermute x4, starting transfers between devices, shifted(): lax.ppermute(shard, AXES, [(i, i + by) for i in range(devices) if 0 <= i...  12.2 us
    all_to_all x1, starting transfers between devices, local(): lax.all_to_all(coarse, AXES, 0, 0, axis_index_groups=columns, tiled=True)  8.04 us
    all_to_all x1, starting transfers between devices, local(): lax.all_to_all(payload, AXES, 0, 0, axis_index_groups=rows, tiled=True)  6.51 us
    pallas_call x1, Pallas kernels, leaf_local(): pl.pallas_call(leaf_kernel, name='leaf_local', out_shape=jax.ShapeDtypeSt...  4.73 us
    pallas_call x1, Pallas kernels, upward(): pl.pallas_call(upward_kernel, name='upward', out_shape=(jax.ShapeDtypeStr...  3.77 us
    pallas_call x1, Pallas kernels, downward(): pl.pallas_call(downward_kernel, name='downward', out_shape=jax.ShapeDtype...  3.43 us
    all_to_all x1, waiting for transfers between devices, local(): lax.all_to_all(payload, AXES, 0, 0, axis_index_groups=rows, tiled=True)  2.39 us
  transfers between devices with their start and end apart: 7, of which 3 were waited for; matrix products, arithmetic and copies ran while one was open for 0% of the time, Pallas kernels for 32%

profile of v8, /device:TPU:1, one launch (start us, length us, event | category | flops | bytes accessed | tf_op | source)
XLA Modules:
  0.0 58.5 jit_solution(11807659212703211880)
XLA Ops:
  0.0 3.8 %upward.1 = (bf16[32,4096]{1,0:T(8,128)(2,1)S(1)}, bf16[32,1024]{1,0:T(8,128)(2,1)S(1)}, bf16[32,1024]{1,0:T(8,128)(2,1)S(1)}, bf16[8,8,16,128]{3,2,1,0:T(8,128)...) custom-call(s32[1]{0:T(128)} %bitcast.column_ref, ...), custom_call_target="tpu_custom_call" | custom-call | flops 20000000 | bytes 4194304 | tf_op jit(solution)/shard_map/upward/pallas_call | solution.py:120
  3.8 4.4 %collective-permute-start = (bf16[8,8,16,128]{3,2,1,0:T(8,128)(2,1)S(1)}, bf16[8,8,16,128]{3,2,1,0:T(8,128)(2,1)S(1)}, u32[]{:S(2)}, u32[]{:S(2)}) collective-permute-start(bf16[8,8,16,128]{3,2,1,0:T(8,128)(2,1)S(1)} %get-tuple-element.22), channel_id=1, source_target_pairs={{0,8},{1,9},{2,10},{3,11},{4,12},{5,13},{6,14},{7,15},{8,16},{9,17... | collective-permute-start | bytes 786440 | tf_op jit(solution)/shard_map/ppermute | solution.py:477
  8.2 1.3 %collective-permute-start.1 = (bf16[8,8,16,128]{3,2,1,0:T(8,128)(2,1)S(1)}, bf16[8,8,16,128]{3,2,1,0:T(8,128)(2,1)S(1)}, u32[]{:S(2)}, u32[]{:S(2)}) collective-permute-start(bf16[8,8,16,128]{3,2,1,0:T(8,128)(2,1)S(1)} %get-tuple-element.23), channel_id=1, source_target_pairs={{8,0},{9,1},{10,2},{11,3},{12,4},{13,5},{14,6},{15,7},{16,8},{17,9... | collective-permute-start | bytes 786440 | tf_op jit(solution)/shard_map/ppermute | solution.py:477
  9.5 8.0 %all-to-all-start = ((bf16[16,2,16,128]{3,2,1,0:T(8,128)(2,1)}), bf16[16,2,16,128]{3,2,1,0:T(8,128)(2,1)S(1)}, u32[]{:S(2)}, u32[]{:S(2)}) async-start(bf16[16,2,16,128]{3,2,1,0:T(8,128)(2,1)} %get-tuple-element.24), calls=%async_computation | async-start | bytes 262144 | tf_op jit(solution)/shard_map/all_to_all | solution.py:491
  17.5 4.6 %collective-permute-start.2 = (bf16[32,1024]{1,0:T(8,128)(2,1)S(1)}, bf16[32,1024]{1,0:T(8,128)(2,1)S(1)}, u32[]{:S(2)}, u32[]{:S(2)}) collective-permute-start(bf16[32,1024]{1,0:T(8,128)(2,1)S(1)} %get-tuple-element.25), channel_id=1, source_target_pairs={{0,1},{1,2},{2,3},{3,4},{4,5},{5,6},{6,7},{7,8},{8,9},{9,10},{10,1... | collective-permute-start | bytes 196616 | tf_op jit(solution)/shard_map/ppermute | solution.py:477
  22.1 1.9 %collective-permute-start.3 = (bf16[32,1024]{1,0:T(8,128)(2,1)S(1)}, bf16[32,1024]{1,0:T(8,128)(2,1)S(1)}, u32[]{:S(2)}, u32[]{:S(2)}) collective-permute-start(bf16[32,1024]{1,0:T(8,128)(2,1)S(1)} %get-tuple-element.26), channel_id=1, source_target_pairs={{1,0},{2,1},{3,2},{4,3},{5,4},{6,5},{7,6},{8,7},{9,8},{10,9},{11,1... | collective-permute-start | bytes 196616 | tf_op jit(solution)/shard_map/ppermute | solution.py:477
  24.1 0.2 all-to-all-done.coarse_ref
  24.2 0.0 collective-permute-done.below_ref
  24.2 0.0 collective-permute-done.1.above_ref
  24.2 1.2 %assemble.1 = bf16[8,32,16,128]{3,2,1,0:T(8,128)(2,1)} custom-call(s32[1]{0:T(128)} %bitcast.column_ref, bf16[8,8,16,128]{3,2,1,0:T(8,128)(2,1)S(1)} %get-tuple-element.21.own_ref, bf16[8,8,16,128]{3,2,1,0:T(8,128)(2,1)S(1)} %collective-permute-done.below_ref, bf16[8,8,16,128]{3,2,1,0:T(8,128)(2,1)S(1)} %collective-permute-done.1.above_ref, ...), custom_call_target="tpu_custom_call" | custom-call | bytes 3145728 | tf_op jit(solution)/shard_map/assemble/pallas_call | solution.py:321
  25.4 0.0 collective-permute-done.2.below_ref
  25.4 2.3 %collective-permute-done.3.above_ref = bf16[32,1024]{1,0:T(8,128)(2,1)S(1)} collective-permute-done((bf16[32,1024]{1,0:T(8,128)(2,1)S(1)}, bf16[32,1024]{1,0:T(8,128)(2,1)S(1)}, u32[]{:S(2)}, u32[]{:S(2)}) %collective-permute-start.3) | collective-permute-done | bytes 65568 | tf_op jit(solution)/shard_map/ppermute | solution.py:477
  27.7 6.5 %all-to-all-start.1 = ((bf16[8,32,16,128]{3,2,1,0:T(8,128)(2,1)}), bf16[8,32,16,128]{3,2,1,0:T(8,128)(2,1)S(1)}, u32[]{:S(2)}, u32[]{:S(2)}) async-start(bf16[8,32,16,128]{3,2,1,0:T(8,128)(2,1)} %assemble.1), calls=%async_computation.1 | async-start | bytes 2097152 | tf_op jit(solution)/shard_map/all_to_all | solution.py:498
  34.2 12.7 %near.1 = (f32[16,4096]{1,0:T(8,128)}, bf16[32,64,2048]{2,1,0:T(8,128)(2,1)}, bf16[4,64,2048]{2,1,0:T(8,128)(2,1)S(1)}) custom-call(s32[13,32]{1,0:T(8,128)} %bitcast.8, bf16[32,4096]{1,0:T(8,128)(2,1)S(1)} %get-tuple-element.28.pack_ref, bf16[32,1024]{1,0:T(8,128)(2,1)S(1)} %collective-permute-done.2.below_ref, ...), custom_call_target="tpu_custom_call" | custom-call | flops 654311424 | bytes 20971520 | tf_op jit(solution)/shard_map/near/pallas_call | solution.py:272
  46.9 2.4 %all-to-all-done.1.swapped_ref = bf16[8,32,16,128]{3,2,1,0:T(8,128)(2,1)S(1)} async-done(((bf16[8,32,16,128]{3,2,1,0:T(8,128)(2,1)}), bf16[8,32,16,128]{3,2,1,0:T(8,128)(2,1)S(1)}, u32[]{:S(2)}, u32[]{:S(2)}) %all-to-all-start.1) | async-done | bytes 1048608 | tf_op jit(solution)/shard_map/all_to_all | solution.py:498
  49.4 1.0 %collective-permute-start.4 = (bf16[8,16,16,128]{3,2,1,0:T(8,128)(2,1)S(1)}, bf16[8,16,16,128]{3,2,1,0:T(8,128)(2,1)S(1)}, u32[]{:S(2)}, u32[]{:S(2)}) collective-permute-start(bf16[8,16,16,128]{3,2,1,0:T(8,128)(2,1)S(1)} %slice.3), channel_id=1, source_target_pairs={{0,1},{1,0},{2,3},{3,2},{4,5},{5,4},{6,7},{7,6},{8,9},{9,8},{10,11... | collective-permute-start | bytes 1572872 | tf_op jit(solution)/shard_map/ppermute | solution.py:503
  50.3 4.7 %leaf_local.1.local_ref = f32[32,16,64]{2,1,0:T(8,128)S(1)} custom-call(s32[1]{0:T(128)} %bitcast.column_ref, s32[32,32]{1,0:T(8,128)} %leaf_hbm.1, bf16[8,32,16,128]{3,2,1,0:T(8,128)(2,1)S(1)} %all-to-all-done.1.swapped_ref, bf16[8,8,16,128]{3,2,1,0:T(8,128)(2,1)S(1)} %collective-permute-done.below_ref, ...), custom_call_target="tpu_custom_call" | custom-call | flops 140000000 | bytes 9437184 | tf_op jit(solution)/shard_map/leaf_local/pallas_call | solution.py:386
  55.1 0.0 collective-permute-done.4.other_ref
  55.1 3.4 %downward.1 = f32[16,4096]{1,0:T(8,128)} custom-call(s32[1]{0:T(128)} %bitcast.column_ref, s32[4,32]{1,0:T(4,128)} %group_hbm.1, bf16[8,32,16,128]{3,2,1,0:T(8,128)(2,1)S(1)} %all-to-all-done.1.swapped_ref, bf16[8,16,16,128]{3,2,1,0:T(8,128)(2,1)S(1)} %collective-permute-done.4.other_ref, f32[32,16,64]{2,1,0:T(8,128)S(1)} %leaf_local.1.local_ref, ...), custom_call_target="tpu_custom_call" | custom-call | flops 60000000 | bytes 4194304 | tf_op jit(solution)/shard_map/downward/pallas_call | solution.py:454
  (1 shorter events, 0.0 us)
Async XLA Ops:
  3.8 20.4 %collective-permute-start = (bf16[8,8,16,128]{3,2,1,0:T(8,128)(2,1)S(1)}, bf16[8,8,16,128]{3,2,1,0:T(8,128)(2,1)S(1)}, u32[]{:S(2)}, u32[]{:S(2)}) collective-permute-start(bf16[8,8,16,128]{3,2,1,0:T(8,128)(2,1)S(1)} %get-tuple-element.22), channel_id=1, source_target_pairs={{0,8},{1,9},{2,10},{3,11},{4,12},{5,13},{6,14},{7,15},{8,16},{9,17... | collective-permute-start | bytes 786440 | tf_op jit(solution)/shard_map/ppermute | solution.py:477
  8.2 16.0 %collective-permute-start.1 = (bf16[8,8,16,128]{3,2,1,0:T(8,128)(2,1)S(1)}, bf16[8,8,16,128]{3,2,1,0:T(8,128)(2,1)S(1)}, u32[]{:S(2)}, u32[]{:S(2)}) collective-permute-start(bf16[8,8,16,128]{3,2,1,0:T(8,128)(2,1)S(1)} %get-tuple-element.23), channel_id=1, source_target_pairs={{8,0},{9,1},{10,2},{11,3},{12,4},{13,5},{14,6},{15,7},{16,8},{17,9... | collective-permute-start | bytes 786440 | tf_op jit(solution)/shard_map/ppermute | solution.py:477
  9.5 14.7 %all-to-all-start = ((bf16[16,2,16,128]{3,2,1,0:T(8,128)(2,1)}), bf16[16,2,16,128]{3,2,1,0:T(8,128)(2,1)S(1)}, u32[]{:S(2)}, u32[]{:S(2)}) async-start(bf16[16,2,16,128]{3,2,1,0:T(8,128)(2,1)} %get-tuple-element.24), calls=%async_computation | async-start | bytes 262144 | tf_op jit(solution)/shard_map/all_to_all | solution.py:491
  17.5 7.9 %collective-permute-start.2 = (bf16[32,1024]{1,0:T(8,128)(2,1)S(1)}, bf16[32,1024]{1,0:T(8,128)(2,1)S(1)}, u32[]{:S(2)}, u32[]{:S(2)}) collective-permute-start(bf16[32,1024]{1,0:T(8,128)(2,1)S(1)} %get-tuple-element.25), channel_id=1, source_target_pairs={{0,1},{1,2},{2,3},{3,4},{4,5},{5,6},{6,7},{7,8},{8,9},{9,10},{10,1... | collective-permute-start | bytes 196616 | tf_op jit(solution)/shard_map/ppermute | solution.py:477
  22.1 5.6 %collective-permute-start.3 = (bf16[32,1024]{1,0:T(8,128)(2,1)S(1)}, bf16[32,1024]{1,0:T(8,128)(2,1)S(1)}, u32[]{:S(2)}, u32[]{:S(2)}) collective-permute-start(bf16[32,1024]{1,0:T(8,128)(2,1)S(1)} %get-tuple-element.26), channel_id=1, source_target_pairs={{1,0},{2,1},{3,2},{4,3},{5,4},{6,5},{7,6},{8,7},{9,8},{10,9},{11,1... | collective-permute-start | bytes 196616 | tf_op jit(solution)/shard_map/ppermute | solution.py:477
  27.7 21.6 %all-to-all-start.1 = ((bf16[8,32,16,128]{3,2,1,0:T(8,128)(2,1)}), bf16[8,32,16,128]{3,2,1,0:T(8,128)(2,1)S(1)}, u32[]{:S(2)}, u32[]{:S(2)}) async-start(bf16[8,32,16,128]{3,2,1,0:T(8,128)(2,1)} %assemble.1), calls=%async_computation.1 | async-start | bytes 2097152 | tf_op jit(solution)/shard_map/all_to_all | solution.py:498
  49.4 5.7 %collective-permute-start.4 = (bf16[8,16,16,128]{3,2,1,0:T(8,128)(2,1)S(1)}, bf16[8,16,16,128]{3,2,1,0:T(8,128)(2,1)S(1)}, u32[]{:S(2)}, u32[]{:S(2)}) collective-permute-start(bf16[8,16,16,128]{3,2,1,0:T(8,128)(2,1)S(1)} %slice.3), channel_id=1, source_target_pairs={{0,1},{1,0},{2,3},{3,2},{4,5},{5,4},{6,7},{7,6},{8,9},{9,8},{10,11... | collective-permute-start | bytes 1572872 | tf_op jit(solution)/shard_map/ppermute | solution.py:503
